TPU v7x, 32 devices: a whole 2x2x4 slice. The times are simulated.
32 devices in a mesh: groups: 2 (over y), ctx: 4 (over z), fsdp: 4 (over x, core).
Axes of the slice: x: 2, y: 2, z: 4, core: 2. Of those that a mesh axis runs over, the one named last changes fastest.
Arguments:
- patches: bfloat16 [8192, 1024], P(('groups', 'ctx', 'fsdp')), parts along dimension 0, may hold values from -6 to 6
- labels: int32 [8192], P(('groups', 'ctx', 'fsdp')), parts along dimension 0, may hold values from 0 to 127
- op_ids: int32 [4, 3], P('groups'), parts along dimension 0, may hold values from 0 to 8
- mix_codes: int32 [4, 4], P('groups'), parts along dimension 0, may hold values from 1 to 8
- aug_gains: float32 [9, 1024], replicated, may hold values from 0.1 to 1.9
- in_weight: bfloat16 [1024, 1536], P('fsdp'), may hold values from -0.1875 to 0.1875
- dt_weight: bfloat16 [1024, 32], P('fsdp'), may hold values from -0.09375 to 0.09375
- dt_bias: float32 [2, 16], replicated, may hold values from -3.9 to -2.2
- decay_log: float32 [2, 16], replicated, may hold values from -12 to 0
- skip_gain: float32 [16], replicated, may hold values from 0.1 to 1.9
- norm_gain: float32 [1024], replicated, may hold values from 0.5 to 1.5
- out_weight: bfloat16 [1024, 1024], P('fsdp'), may hold values from -0.1875 to 0.1875
- head_weight: bfloat16 [1024, 128], replicated, may hold values from -8 to 8
Outputs:
- grad_out: float32 [2048, 1024], P(('groups', 'ctx', 'fsdp')), parts along dimension 0
- grad_head: float32 [2048, 128], P(('groups', 'ctx', 'fsdp')), parts along dimension 0
- patch_loss: float32 [8192], P(('groups', 'ctx', 'fsdp')), parts along dimension 0
There are 2 independent parts, one for each index of `groups`. A program takes and returns all parts, laid end to end along the dimension named above; an argument that names none is the same for every part. Nothing has to cross between parts.
All inputs are finite; a program needn't handle non-finite values.
Results may differ from a plain program's by a relative error of at most 0.01505.
The roundings to bfloat16 on the way count: a program that leaves them out, or rounds other values in their place, can miss the bound.
Values may be sent and summed in bfloat16 or wider, within the bound.
A program may use at most 128 MiB of HBM per device.

v0:
```python
import jax
import jax.numpy as jnp
from jax import lax
from jax.sharding import PartitionSpec as P

D = 1024
HEADS = 16
HEAD_DIM = 64
STATE = 128
CLASSES = 128
VIEWS = 3
NOPS = 9
WIDTH_AUG = 3
BLOCK = 128


loss_scale = 256.0
mix_lambda = 12.0
highest = lax.Precision.HIGHEST


def carried_in_2(value, axis, combine, identity, reverse):
    count, mine = (lax.axis_size(axis), lax.axis_index(axis))
    everything = jax.tree.map(lambda part: lax.all_gather(part, axis), value)
    start = jax.tree.map(
        lambda part, zero: jnp.broadcast_to(jnp.asarray(zero, part.dtype), part.shape),
        value,
        identity,
    )

    def turn(k, before):
        at = count - 1 - k if reverse else k
        reached = at > mine if reverse else at < mine
        new = combine(before, jax.tree.map(lambda part: part[at], everything))
        return jax.tree.map(lambda a, b: jnp.where(reached, a, b), new, before)

    return lax.fori_loop(0, count, turn, start)


def view_scales(op_ids, mix_codes, aug_gains):
    code_values = mix_codes.astype(jnp.float32)
    weights = code_values[:, :WIDTH_AUG] / jnp.sum(
        code_values[:, :WIDTH_AUG], axis=1, keepdims=True
    )
    keep_share = code_values[:, WIDTH_AUG] / 9.0
    onehot = (op_ids[:, :, None] == jnp.arange(NOPS, dtype=jnp.int32)[None, None, :]).astype(
        jnp.float32
    )
    op_weights = jnp.sum(onehot * weights[:, :, None], axis=1)
    mixed_gain = jnp.dot(op_weights, aug_gains, precision=highest)
    scaled = keep_share[:, None] + (1.0 - keep_share[:, None]) * mixed_gain
    return jnp.concatenate([jnp.ones((1, D), jnp.float32), scaled], axis=0)


def block_pass(values, write_vectors, read_vectors, step_sizes, decay_rates):
    length, head_count, head_width = values.shape
    pieces = length // BLOCK
    shaped = (
        values.reshape(pieces, BLOCK, head_count, head_width),
        write_vectors.reshape(pieces, BLOCK, STATE),
        read_vectors.reshape(pieces, BLOCK, STATE),
        step_sizes.reshape(pieces, BLOCK, head_count),
    )
    lower_mask = jnp.arange(BLOCK)[:, None] >= jnp.arange(BLOCK)[None, :]

    def advance(carried_in, inputs):
        state_now, offset = carried_in
        piece_values, piece_write, piece_read, piece_steps = inputs
        value_float = piece_values.astype(jnp.float32)
        write_float = piece_write.astype(jnp.float32)
        read_float = piece_read.astype(jnp.float32)
        step_logs = piece_steps * decay_rates[None, :]
        running = jnp.cumsum(step_logs, axis=0)
        log_gaps = running[:, None, :] - running[None, :, :]
        mask_decay = jnp.exp(jnp.where(lower_mask[:, :, None], log_gaps, -1e30))
        scores = jnp.dot(read_float, write_float.T, precision=highest)
        mixing = scores[:, :, None] * mask_decay * piece_steps[None, :, :]
        inside = jnp.einsum("tsh,shp->thp", mixing, value_float, precision=highest)
        carried = jnp.exp(running)[:, :, None] * jnp.einsum(
            "tn,hpn->thp", read_float, state_now, precision=highest
        )
        last_log = running[-1]
        weighted = (jnp.exp(last_log[None, :] - running) * piece_steps)[:, :, None] * value_float
        new_state = jnp.exp(last_log)[:, None, None] * state_now + jnp.einsum(
            "shp,sn->hpn", weighted, write_float, precision=highest
        )
        return ((new_state, offset + last_log), (inside + carried, offset[None, :] + running))

    initial = (
        jnp.zeros((head_count, head_width, STATE), jnp.float32),
        jnp.zeros((head_count,), jnp.float32),
    )
    (final_state, total_log), (outputs, positions_log) = lax.scan(advance, initial, shaped)
    return (
        outputs.reshape(length, head_count, head_width),
        positions_log.reshape(length, head_count),
        final_state,
        total_log,
    )


def loss_terms(logits, labels):
    log_probs = jax.nn.log_softmax(logits, axis=-1)
    probabilities = jnp.exp(log_probs)
    log_mean = jax.scipy.special.logsumexp(log_probs, axis=0) - jnp.log(jnp.float32(VIEWS))
    spread = jnp.sum(probabilities * (log_probs - log_mean[None]), axis=(0, 2)) / VIEWS
    onehot = (labels[:, None] == jnp.arange(CLASSES, dtype=jnp.int32)[None, :]).astype(jnp.float32)
    cross_entropy = -jnp.sum(onehot * log_probs[0], axis=-1)
    return cross_entropy + mix_lambda * spread


def combine_states(earlier, later):
    earlier_log, earlier_state = earlier
    later_log, later_state = later
    return (
        earlier_log + later_log,
        jnp.exp(later_log)[:, :, None, None] * earlier_state + later_state,
    )


def apply_incoming(outputs, positions_log, read_vectors, incoming):
    reached = jnp.einsum(
        "vtn,vhpn->vthp", read_vectors.astype(jnp.float32), incoming, precision=highest
    )
    return outputs + jnp.exp(positions_log)[:, :, :, None] * reached


def on_device(
    patches,
    labels,
    op_ids,
    mix_codes,
    aug_gains,
    in_weight,
    dt_weight,
    dt_bias,
    decay_log,
    skip_gain,
    norm_gain,
    out_weight,
    head_weight,
):
    row_count = patches.shape[0]
    ctx_count = lax.axis_size("ctx")
    fsdp_count = lax.axis_size("fsdp")
    fsdp_place = lax.axis_index("fsdp")
    total_patches = row_count * ctx_count * fsdp_count
    inner_width = out_weight.shape[0] * fsdp_count
    local_heads = HEADS // fsdp_count
    range_rows = row_count * fsdp_count
    scales = view_scales(op_ids, mix_codes, aug_gains)
    views = (scales[:, None, :] * patches.astype(jnp.float32)[None]).astype(jnp.bfloat16)
    flat_rows = views.reshape(VIEWS * row_count, D)
    columns = flat_rows
    proj_sum = jnp.dot(
        columns,
        lax.all_gather(in_weight, "fsdp", axis=0, tiled=True),
        preferred_element_type=jnp.float32,
    )
    raw_sum = jnp.dot(
        columns,
        lax.all_gather(dt_weight, "fsdp", axis=0, tiled=True),
        preferred_element_type=jnp.float32,
    )
    projected = proj_sum.astype(jnp.bfloat16).reshape(VIEWS, row_count, in_weight.shape[1])
    step_sizes = jax.nn.softplus(raw_sum.reshape(VIEWS, row_count, 2, HEADS) + dt_bias[None, None])
    value_rows = projected[:, :, :inner_width].reshape(
        VIEWS, row_count, fsdp_count, local_heads * HEAD_DIM
    )
    head_rows = lax.all_to_all(value_rows, "fsdp", split_axis=2, concat_axis=1, tiled=True)
    values = head_rows.reshape(VIEWS, range_rows, local_heads, HEAD_DIM)
    step_rows = step_sizes.reshape(VIEWS, row_count, 2, fsdp_count, local_heads)
    head_step_rows = lax.all_to_all(step_rows, "fsdp", split_axis=3, concat_axis=1, tiled=True)
    local_steps = head_step_rows.reshape(VIEWS, range_rows, 2, local_heads)
    shared = lax.all_gather(projected[:, :, inner_width:], "fsdp", axis=1, tiled=True)
    coefficients = shared.reshape(VIEWS, range_rows, 4, STATE)
    head_start = fsdp_place * local_heads
    decay_rates = lax.dynamic_slice_in_dim(-jnp.exp(decay_log), head_start, local_heads, 1)
    local_skip = lax.dynamic_slice_in_dim(skip_gain, head_start, local_heads, 0)
    local_gain = lax.dynamic_slice_in_dim(
        norm_gain, head_start * HEAD_DIM, local_heads * HEAD_DIM, 0
    )
    mapped = jax.vmap(block_pass, in_axes=(0, 0, 0, 0, None))
    forward_read = coefficients[:, :, 1]
    forward_out, forward_logs, forward_state, forward_total = mapped(
        values, coefficients[:, :, 0], forward_read, local_steps[:, :, 0], decay_rates[0]
    )
    reverse_values = jnp.flip(values, 1)
    reverse_read = jnp.flip(coefficients[:, :, 3], 1)
    reverse_out, reverse_logs, reverse_state, reverse_total = mapped(
        reverse_values,
        jnp.flip(coefficients[:, :, 2], 1),
        reverse_read,
        jnp.flip(local_steps[:, :, 1], 1),
        decay_rates[1],
    )
    identity = (jnp.zeros_like(forward_total), jnp.zeros_like(forward_state))
    forward_in = carried_in_2(
        (forward_total, forward_state), "ctx", combine_states, identity, False
    )
    reverse_in = carried_in_2((reverse_total, reverse_state), "ctx", combine_states, identity, True)
    forward_full = apply_incoming(forward_out, forward_logs, forward_read, forward_in[1])
    reverse_full = apply_incoming(reverse_out, reverse_logs, reverse_read, reverse_in[1])
    mixed = (
        forward_full
        + jnp.flip(reverse_full, 1)
        + local_skip[None, None, :, None] * values.astype(jnp.float32)
    )
    mixed = mixed.reshape(VIEWS, range_rows, local_heads * HEAD_DIM)
    square_total = lax.psum(jnp.sum(mixed * mixed, axis=-1), "fsdp")
    scaling = lax.rsqrt(square_total / inner_width + 1e-05)
    normed_heads = (mixed * scaling[:, :, None] * local_gain[None, None, :]).astype(jnp.bfloat16)
    normed_rows = lax.all_to_all(normed_heads, "fsdp", split_axis=1, concat_axis=2, tiled=True)
    normed = normed_rows.reshape(VIEWS * row_count, inner_width)
    columns = normed
    out_sum = jnp.dot(
        columns,
        lax.all_gather(out_weight, "fsdp", axis=0, tiled=True),
        preferred_element_type=jnp.float32,
    )
    hidden = (flat_rows.astype(jnp.float32) + out_sum).astype(jnp.bfloat16)
    logits = jnp.dot(hidden, head_weight, preferred_element_type=jnp.float32).reshape(
        VIEWS, row_count, CLASSES
    )

    def per_patch(logit_values):
        return loss_terms(logit_values, labels)

    patch_loss, pullback = jax.vjp(per_patch, logits)
    (grad_logits,) = pullback(jnp.full((row_count,), loss_scale / total_patches, jnp.float32))
    grad_logits_bf = grad_logits.reshape(VIEWS * row_count, CLASSES).astype(jnp.bfloat16)
    grad_hidden = lax.dot_general(
        grad_logits_bf, head_weight, (((1,), (1,)), ((), ())), preferred_element_type=jnp.float32
    ).astype(jnp.bfloat16)
    head_term = lax.dot_general(
        hidden, grad_logits_bf, (((0,), (0,)), ((), ())), preferred_element_type=jnp.float32
    )
    columns = normed
    grad_out = lax.psum_scatter(
        lax.dot_general(
            columns, grad_hidden, (((0,), (0,)), ((), ())), preferred_element_type=jnp.float32
        ),
        ("ctx", "fsdp"),
        scatter_dimension=0,
        tiled=True,
    )
    grad_head = lax.psum_scatter(head_term, ("ctx", "fsdp"), scatter_dimension=0, tiled=True)
    return (grad_out, grad_head, patch_loss)


def solution(mesh):
    return jax.shard_map(
        on_device,
        mesh=mesh,
        in_specs=(
            P(("groups", "ctx", "fsdp"), None),
            P(("groups", "ctx", "fsdp")),
            P("groups", None),
            P("groups", None),
            P(),
            P("fsdp", None),
            P("fsdp", None),
            P(),
            P(),
            P(),
            P(),
            P("fsdp", None),
            P(),
        ),
        out_specs=(
            P(("groups", "ctx", "fsdp"), None),
            P(("groups", "ctx", "fsdp"), None),
            P(("groups", "ctx", "fsdp")),
        ),
        check_vma=False,
    )
```

profile of v0, /device:TPU:0, one launch (start us, length us, event | category | flops | bytes accessed | tf_op | source)
XLA Modules:
  0.0 552.4 jit_solution(7558193707011760850)
XLA Ops:
  11.7 29.2 %all-gather.12.cloned.1.call-done = bf16[1024,1536]{1,0:T(8,128)(2,1)} async-done(((bf16[256,1536]{1,0:T(8,128)(2,1)}), bf16[1024,1536]{1,0:T(8,128)(2,1)}) %all-gather.12.cloned.1.call-update) | async-done | bytes 3145744 | tf_op jit(solution)/shard_map/all_gather | solution.py:157
  40.8 4.7 convolution_convert_fusion
  48.3 5.2 all_gather.36
  54.9 3.3 all-to-all-start
  61.7 2.1 all-to-all-done
  63.8 3.6 all-to-all-start.1
  68.5 24.8 %all-to-all-done.1 = bf16[3,256,4,256]{1,3,0,2:T(8,128)(2,1)S(1)} async-done(((bf16[3,256,4,256]{1,3,0,2:T(8,128)(2,1)}), bf16[3,256,4,256]{1,3,0,2:T(8,128)(2,1)S(1)}, u32[]{:S(2)}, u32[]{:S(2)}) %all-to-all-start.1) | async-done | bytes 1572896 | tf_op jit(solution)/shard_map/all_to_all | solution.py:170
  93.3 2.4 copy.250
  95.7 2.8 reshape.248
  98.5 3.6 reshape_reshape.3
  102.2 3.7 rev.20
  105.9 3.1 copy.256
  110.7 3.6 fusion.116
  114.3 10.3 %rev.22 = bf16[3,1024,128]{1,2,0:T(8,128)(2,1)S(1)} reverse(bf16[3,1024,128]{1,2,0:T(8,128)(2,1)} %get-tuple-element.680), dimensions={1} | reverse | bytes 1572864 | tf_op jit(solution)/shard_map/jit(_flip)/rev | solution.py:189
  125.8 2.4 copy.262
  128.2 10.3 %rev.21 = bf16[3,1024,128]{1,2,0:T(8,128)(2,1)S(1)} reverse(bf16[3,1024,128]{1,2,0:T(8,128)(2,1)} %get-tuple-element.681), dimensions={1} | reverse | bytes 1572864 | tf_op jit(solution)/shard_map/jit(_flip)/rev | solution.py:192
  139.6 2.4 copy.261
  142.0 2.1 broadcast.141.clone
  145.5 72.5 %while.66 = (s32[]{:T(128)}, f32[3,4,64,128]{3,2,1,0:T(8,128)S(1)}, f32[3,4]{1,0:T(4,128)S(1)}, f32[8,3,128,4,64]{2,4,3,1,0:T(8,128)}, f32[8,3,128,4]{3,2,1,0:T(...) while((s32[]{:T(128)}, f32[3,4,64,128]{3,2,1,0:T(8,128)S(1)}, ...), condition=%wide.region_9.10_spmd.clone, body=%wide.region_7.9_spmd.clone.sunk | while | flops 467358240 | bytes 3932897 | solution.py:93
  146.0 2.0 convolution_multiply_fusion.6
  149.4 2.9 fusion.193
  155.1 2.0 convolution_multiply_fusion.6
  158.5 2.9 fusion.193
  164.1 2.0 convolution_multiply_fusion.6
  167.5 2.9 fusion.193
  176.6 2.9 fusion.193
  182.2 2.0 convolution_multiply_fusion.6
  185.6 2.9 fusion.193
  194.7 2.9 fusion.193
  200.4 2.0 convolution_multiply_fusion.6
  203.8 2.9 fusion.193
  209.4 2.0 convolution_multiply_fusion.6
  212.8 2.9 fusion.193
  218.9 2.3 copy.290
  221.2 2.4 copy.252
  224.8 2.1 copy.310
  227.0 2.1 broadcast.141.clone.1
  230.4 65.1 %while.64 = (s32[]{:T(128)}, f32[3,4,64,128]{3,2,1,0:T(8,128)S(1)}, f32[3,4]{1,0:T(4,128)S(1)}, f32[8,3,128,4,64]{2,4,3,1,0:T(8,128)}, f32[8,3,128,4]{3,2,1,0:T(...) while((s32[]{:T(128)}, f32[3,4,64,128]{3,2,1,0:T(8,128)S(1)}, ...), condition=%wide.region_4.5_spmd.clone, body=%wide.region_2.4_spmd.clone.sunk | while | flops 467358240 | bytes 3932897 | solution.py:93
  233.6 2.7 fusion.179
  241.7 2.7 fusion.179
  249.9 2.7 fusion.179
  258.0 2.7 fusion.179
  266.1 2.7 fusion.179
  274.2 2.7 fusion.179
  282.4 2.7 fusion.179
  290.5 2.7 fusion.179
  297.7 12.0 %all-gather.5 = f32[4,3,4]{2,1,0:T(4,128)S(1)} all-gather(f32[1,3,4]{2,1,0:T(4,128)S(1)} %bitcast.380), channel_id=4, replica_groups=mesh['groups'=2,'ctx'=4,'fsdp'=4] {'ctx'}, dimensions={0}, use_global_device_ids=true | all-gather | bytes 240 | tf_op jit(solution)/shard_map/all_gather | solution.py:24
  309.7 2.8 exponential_bitcast_fusion.2
  314.4 12.2 %all-gather.4 = f32[4,3,4]{2,1,0:T(4,128)S(1)} all-gather(f32[1,3,4]{2,1,0:T(4,128)S(1)} %bitcast.379), channel_id=2, replica_groups=mesh['groups'=2,'ctx'=4,'fsdp'=4] {'ctx'}, dimensions={0}, use_global_device_ids=true | all-gather | bytes 240 | tf_op jit(solution)/shard_map/all_gather | solution.py:24
  326.6 2.8 exponential_bitcast_fusion.3
  331.4 4.7 while.67
  336.1 5.0 bitcast_add_fusion.4
  341.2 6.7 %rev.23 = f32[3,1024,4,64]{1,3,2,0:T(8,128)} reverse(f32[3,1024,4,64]{1,3,2,0:T(8,128)} %bitcast_add_fusion.4), dimensions={1} | reverse | bytes 6291456 | tf_op jit(solution)/shard_map/jit(_flip)/rev | solution.py:206
  347.8 4.6 while.65
  352.4 6.9 %multiply_reduce_fusion = (f32[3,1024]{1,0:T(4,128)S(1)}, f32[3,1024,4,64]{1,3,2,0:T(8,128)}) fusion(bf16[3,1024,4,64]{1,3,2,0:T(8,128)(2,1)S(1)} %reshape.248, f32[4]{0:T(128)S(1)} %dynamic_slice.71, f32[3,1024,4,64]{1,3,2,0:T(8,128)} %rev.23, f32[3,4,64,128]{3,2,1,0:T(8,128)S(1)} %get-tuple-element.353, bf16[3,1024,4,128]{1,3,2,0:T(8,128)(2,1)} %bitcast.353, ...), kind=kOutput, calls=%fused_computation.119 | convolution fusion | flops 1214247936 | bytes 12251152 | tf_op jit(solution)/shard_map/vtn,vhpn->vthp/dot_general | solution.py:122
  359.3 2.4 copy.267
  361.7 10.4 %psum.7 = f32[3,1024]{1,0:T(4,128)S(1)} all-reduce(f32[3,1024]{1,0:T(4,128)S(1)} %get-tuple-element.690), channel_id=1, replica_groups=mesh['groups'=2,'ctx'=4,'fsdp'=4] {'fsdp'}, use_global_device_ids=true, to_apply=%region_13.14 | all-reduce | flops 3072 | bytes 24576 | tf_op jit(solution)/shard_map/psum | solution.py:210
  372.6 2.7 copy.268
  375.3 3.7 all-to-all-start.2
  379.4 25.3 %all-to-all-done.2 = bf16[3,1024,256]{2,0,1:T(4,128)(2,1)S(1)} async-done(((bf16[3,1024,256]{2,0,1:T(4,128)(2,1)}), bf16[3,1024,256]{2,0,1:T(4,128)(2,1)S(1)}, u32[]{:S(2)}, u32[]{:S(2)}) %all-to-all-start.2) | async-done | bytes 1572896 | tf_op jit(solution)/shard_map/all_to_all | solution.py:213
  407.7 4.3 add_convert_fusion
  416.0 5.6 %fusion.94 = f32[1024,1024]{1,0:T(8,128)} fusion(bf16[768,1024]{1,0:T(8,128)(2,1)} %bitcast.371, bf16[768,128]{1,0:T(8,128)(2,1)S(1)} %bitcast.373, bf16[1024,128]{1,0:T(8,128)(2,1)S(1)} %copy-done), kind=kOutput, calls=%fused_computation.127 | convolution fusion | flops 1812725760 | bytes 6225920 | tf_op jit(solution)/shard_map/dot_general | solution.py:240
  422.8 46.5 %reduce-scatter.5.cloned.1.call-done = f32[64,128]{1,0:T(8,128)} async-done(((f32[1024,128]{1,0:T(8,128)}), f32[64,128]{1,0:T(8,128)}) %reduce-scatter.5.cloned.1.call-update) | async-done | bytes 32784 | tf_op jit(solution)/shard_map/reduce_scatter | solution.py:247
  469.3 76.3 %reduce-scatter.3.cloned.1.call-done = f32[64,1024]{1,0:T(8,128)} async-done(((f32[1024,1024]{1,0:T(8,128)}), f32[64,1024]{1,0:T(8,128)}) %reduce-scatter.3.cloned.1.call-update) | async-done | bytes 262160 | tf_op jit(solution)/shard_map/reduce_scatter | solution.py:239
  (401 shorter events, 125.7 us)
Async XLA Ops:
  7.2 404.8 %copy-start = (bf16[1024,128]{1,0:T(8,128)(2,1)S(1)}, bf16[1024,128]{1,0:T(8,128)(2,1)}, u32[]{:S(2)}) copy-start(bf16[1024,128]{1,0:T(8,128)(2,1)} %param.33) | copy-start | bytes 786436
  7.2 4.0 copy-start.12
  7.2 33.7 %all-gather.12.cloned.1.call-start = ((), (), s32[]{:S(2)}) async-start(), calls=%async_computation.5 | async-start | bytes 3932160 | tf_op jit(solution)/shard_map/all_gather | solution.py:157
  7.9 102.7 %all-gather.14.cloned.1.call-start = ((), (), s32[]{:S(2)}) async-start(), calls=%async_computation.6 | async-start | bytes 3932160 | tf_op jit(solution)/shard_map/all_gather | solution.py:175
  11.7 33.9 %copy-start.8 = (bf16[3,256,1024]{2,1,0:T(8,128)(2,1)}, bf16[3,256,1024]{2,1,0:T(8,128)(2,1)S(1)}, u32[]{:S(2)}) copy-start(bf16[3,256,1024]{2,1,0:T(8,128)(2,1)S(1)} %multiply_convert_fusion.1) | copy-start | bytes 4718596
  45.5 1.4 copy-start.7
  47.0 1.3 copy-start.9
  47.0 6.5 %copy-start.13 = (f32[2,16]{1,0:T(2,128)S(1)}, f32[2,16]{1,0:T(2,128)}, u32[]{:S(2)}) copy-start(f32[2,16]{1,0:T(2,128)} %param.28) | copy-start | bytes 388
  54.9 8.9 %all-to-all-start = ((f32[3,256,2,4,4]{1,4,2,0,3:T(4,128)}), f32[3,256,2,4,4]{1,4,2,0,3:T(4,128)S(1)}, u32[]{:S(2)}, u32[]{:S(2)}) async-start(f32[3,256,2,4,4]{1,4,2,0,3:T(4,128)} %copy.246), calls=%async_computation | async-start | bytes 196608 | tf_op jit(solution)/shard_map/all_to_all | solution.py:173
  61.7 5.8 %copy-start.11 = (f32[2,16]{1,0:T(2,128)S(1)}, f32[2,16]{1,0:T(2,128)}, u32[]{:S(2)}) copy-start(f32[2,16]{1,0:T(2,128)} %param.29) | copy-start | bytes 388
  63.8 29.5 %all-to-all-start.1 = ((bf16[3,256,4,256]{1,3,0,2:T(8,128)(2,1)}), bf16[3,256,4,256]{1,3,0,2:T(8,128)(2,1)S(1)}, u32[]{:S(2)}, u32[]{:S(2)}) async-start(bf16[3,256,4,256]{1,3,0,2:T(8,128)(2,1)} %copy.249), calls=%async_computation.1 | async-start | bytes 3145728 | tf_op jit(solution)/shard_map/all_to_all | solution.py:170
  67.4 264.0 %all-gather.20.cloned.1.call-start = ((), (), s32[]{:S(2)}) async-start(), calls=%async_computation.11 | async-start | bytes 1966080 | tf_op jit(solution)/shard_map/all_gather | solution.py:24
  105.9 3.1 copy-start.5
  124.6 3.6 copy-start.3
  217.9 0.7 copy-start.2
  218.7 129.1 %all-gather.18.cloned.1.call-start = ((), (), s32[]{:S(2)}) async-start(), calls=%async_computation.10 | async-start | bytes 1966080 | tf_op jit(solution)/shard_map/all_gather | solution.py:24
  218.9 4.7 copy-start.6
  230.4 66.5 %copy-start.14 = (f32[16]{0:T(128)S(1)}, f32[16]{0:T(128)}, u32[]{:S(2)}) copy-start(f32[16]{0:T(128)} %param.30) | copy-start | bytes 196
  295.5 0.8 copy-start.1
  296.3 111.4 %all-gather.16.cloned.1.call-start = ((), (), s32[]{:S(2)}) async-start(), calls=%async_computation.7 | async-start | bytes 2621440 | tf_op jit(solution)/shard_map/all_gather | solution.py:218
  331.4 4.8 copy-start.4
  375.3 4.0 copy-start.10
  375.3 29.4 %all-to-all-start.2 = ((bf16[3,1024,256]{2,0,1:T(4,128)(2,1)}), bf16[3,1024,256]{2,0,1:T(4,128)(2,1)S(1)}, u32[]{:S(2)}, u32[]{:S(2)}) async-start(bf16[3,1024,256]{2,0,1:T(4,128)(2,1)} %copy.268), calls=%async_computation.2 | async-start | bytes 4194304 | tf_op jit(solution)/shard_map/all_to_all | solution.py:213
  379.0 90.3 %reduce-scatter.5.cloned.1.call-start = ((), (), s32[]{:S(2)}) async-start(), calls=%async_computation.9 | async-start | bytes 557056 | tf_op jit(solution)/shard_map/reduce_scatter | solution.py:247
  415.9 129.6 %reduce-scatter.3.cloned.1.call-start = ((), (), s32[]{:S(2)}) async-start(), calls=%async_computation.8 | async-start | bytes 4456448 | tf_op jit(solution)/shard_map/reduce_scatter | solution.py:239
Sparse Core Ops, SparseCore 0:
  9.6 31.2 all-gather.11
  48.4 35.9 all-gather.13
  218.8 37.0 all-gather.19
  296.4 37.3 all-gather.17
  335.2 21.4 all-gather.15
  416.1 53.1 reduce-scatter.4
  474.2 71.3 reduce-scatter.2
where the time goes:
time: 558 us; the launch traced here: 552 us
  waiting for transfers between devices  205 us (37%)
  matrix products  141 us (25%)
  local copies, waits for them, and re-layouts  107 us (19%)
  blocking collectives  39.8 us (7%)
  other arithmetic  32.1 us (6%)
  between operations  14.7 us (3%)
  starting transfers between devices  11.3 us (2%)
    reduce_scatter x1, waiting for transfers between devices, on_device(): lax.psum_scatter(lax.dot_general(columns, grad_hidden, (((0,), (0,)), (()...  76.3 us
    reduce_scatter x1, waiting for transfers between devices, on_device(): lax.psum_scatter(head_term, ('ctx', 'fsdp'), scatter_dimension=0, tiled=T...  46.5 us
    dot_general x16, matrix products, advance(): inside = jnp.einsum('tsh,shp->thp', mixing, value_float, precision=highest)  44.6 us
    all_gather x1, waiting for transfers between devices, on_device(): lax.all_gather(in_weight, 'fsdp', axis=0, tiled=True)  29.2 us
    dot_general x16, matrix products, advance(): jnp.einsum('tn,hpn->thp', read_float, state_now, precision=highest)  26 us
    all_to_all x1, waiting for transfers between devices, on_device(): lax.all_to_all(normed_heads, 'fsdp', split_axis=1, concat_axis=2, tiled=T...  25.3 us
    all_to_all x1, waiting for transfers between devices, on_device(): lax.all_to_all(value_rows, 'fsdp', split_axis=2, concat_axis=1, tiled=True)  24.8 us
    all_gather x2, blocking collectives, carried_in_2(): everything = jax.tree.map(lambda part: lax.all_gather(part, axis), value)  24.2 us
  transfers between devices with their start and end apart: 10, of which 6 were waited for; matrix products, arithmetic and copies ran while one was open for 28% of the time, Pallas kernels for 0%

commit v1 on v0

v1 whole, which is shorter than its diff:
```python
import functools
import jax
import jax.numpy as jnp
from jax import lax
from jax.experimental import pallas as pl
from jax.experimental.pallas import tpu as pltpu
from jax.sharding import PartitionSpec as P

D = 1024
HEADS = 16
HEAD_DIM = 64
STATE = 128
CLASSES = 128
VIEWS = 3
NOPS = 9
WIDTH_AUG = 3
BLOCK = 128
LANES = 128
LOG_ROWS = 8


loss_scale = 256.0
mix_lambda = 12.0
highest = lax.Precision.HIGHEST
f32 = jnp.float32
bf16 = jnp.bfloat16


def view_scales(op_ids, mix_codes, aug_gains):
    code_values = mix_codes.astype(jnp.float32)
    weights = code_values[:, :WIDTH_AUG] / jnp.sum(
        code_values[:, :WIDTH_AUG], axis=1, keepdims=True
    )
    keep_share = code_values[:, WIDTH_AUG] / 9.0
    onehot = (op_ids[:, :, None] == jnp.arange(NOPS, dtype=jnp.int32)[None, None, :]).astype(
        jnp.float32
    )
    op_weights = jnp.sum(onehot * weights[:, :, None], axis=1)
    mixed_gain = jnp.dot(op_weights, aug_gains, precision=highest)
    scaled = keep_share[:, None] + (1.0 - keep_share[:, None]) * mixed_gain
    return jnp.concatenate([jnp.ones((1, D), jnp.float32), scaled], axis=0)


def halves(value):
    high = value.astype(bf16)
    return high, (value - high.astype(f32)).astype(bf16)


def thirds(value):
    high = value.astype(bf16)
    rest = value - high.astype(f32)
    mid = rest.astype(bf16)
    return high, mid, (rest - mid.astype(f32)).astype(bf16)


def dot(a, b, dims=((1,), (0,))):
    return lax.dot_general(a, b, (dims, ((), ())), preferred_element_type=f32)


def spread(columns, first, heads):
    rows = columns.shape[0]
    lane = lax.broadcasted_iota(jnp.int32, (rows, LANES), 1)
    pieces = []
    for h in range(first, first + heads, 2):
        left = jnp.broadcast_to(columns[:, h : h + 1], (rows, LANES))
        right = jnp.broadcast_to(columns[:, h + 1 : h + 2], (rows, LANES))
        pieces.append(jnp.where(lane < HEAD_DIM, left, right))
    return jnp.concatenate(pieces, axis=1) if len(pieces) > 1 else pieces[0]


def states_kernel(heads, raw_ref, x_ref, coef_ref, bias_ref, rate_ref,
                  final_ref, prefix_ref, steps_ref, run_ref, pos_ref):
    rows, width = x_ref.shape[1:]
    pieces = rows // BLOCK
    row = lax.broadcasted_iota(jnp.int32, (BLOCK, BLOCK), 0)
    col = lax.broadcasted_iota(jnp.int32, (BLOCK, BLOCK), 1)
    lower = (row >= col).astype(f32).astype(bf16)
    upper = (row <= col).astype(f32).astype(bf16)
    is_forward = col < heads

    def first_pass(i, carried):
        state, total = carried
        at = pl.ds(pl.multiple_of(i * BLOCK, BLOCK), BLOCK)
        raw = raw_ref[0, at, :] + bias_ref[...]
        steps = jnp.maximum(raw, 0.0) + jnp.log1p(jnp.exp(-jnp.abs(raw)))
        parts = thirds(steps * rate_ref[...])
        down = sum(dot(lower, part) for part in parts)
        up = sum(dot(upper, part) for part in parts)
        run = jnp.where(is_forward, down, up)
        steps_ref[0, at, :] = steps
        run_ref[0, at, :] = run
        pos_ref[0, at, :] = run + total
        last = jnp.where(is_forward[:1], run[BLOCK - 1 :], run[:1])
        x = x_ref[0, at, :].astype(f32)
        weight = spread(jnp.exp(last - run) * steps, 0, heads)
        high, low = halves(weight * x)
        write = coef_ref[0, at, :STATE]
        fresh = dot(write, high, ((0,), (0,))) + dot(write, low, ((0,), (0,)))
        s_high, s_low = halves(state)
        prefix_ref[0, 0, i, :STATE, :] = s_high
        prefix_ref[0, 0, i, STATE:, :] = s_low
        return spread(jnp.exp(last), 0, heads) * state + fresh, total + last

    zero = jnp.zeros((STATE, width), f32)
    no_log = jnp.zeros((1, LANES), f32)
    state, total = lax.fori_loop(0, pieces, first_pass, (zero, no_log))
    final_ref[0, 0, :STATE, :] = state
    final_ref[0, 0, STATE:, :] = jnp.broadcast_to(spread(total, 0, heads), (LOG_ROWS, width))

    def second_pass(k, carried):
        state, total = carried
        i = pieces - 1 - k
        at = pl.ds(pl.multiple_of(i * BLOCK, BLOCK), BLOCK)
        run = run_ref[0, at, :]
        last = run[:1]
        pos_ref[0, at, :] = jnp.where(is_forward, pos_ref[0, at, :], run + total)
        x = x_ref[0, at, :].astype(f32)
        weight = spread(jnp.exp(last - run) * steps_ref[0, at, :], heads, heads)
        high, low = halves(weight * x)
        write = coef_ref[0, at, 2 * STATE : 3 * STATE]
        fresh = dot(write, high, ((0,), (0,))) + dot(write, low, ((0,), (0,)))
        s_high, s_low = halves(state)
        prefix_ref[0, 1, i, :STATE, :] = s_high
        prefix_ref[0, 1, i, STATE:, :] = s_low
        return spread(jnp.exp(last), heads, heads) * state + fresh, total + last

    state, total = lax.fori_loop(0, pieces, second_pass, (zero, no_log))
    final_ref[0, 1, :STATE, :] = state
    final_ref[0, 1, STATE:, :] = jnp.broadcast_to(spread(total, heads, heads), (LOG_ROWS, width))


def inside_kernel(heads, x_ref, coef_ref, prefix_ref, steps_ref, run_ref, skip_ref, out_ref):
    row = lax.broadcasted_iota(jnp.int32, (BLOCK, BLOCK), 0)
    col = lax.broadcasted_iota(jnp.int32, (BLOCK, BLOCK), 1)
    below, above = row > col, row < col
    x = x_ref[0]
    steps_t = steps_ref[0].T
    run = run_ref[0]
    run_t = run.T
    coef = coef_ref[0]
    write_f, read_f = coef[:, :STATE], coef[:, STATE : 2 * STATE]
    write_r, read_r = coef[:, 2 * STATE : 3 * STATE], coef[:, 3 * STATE :]
    score_f = dot(read_f, write_f, ((1,), (1,)))
    score_r = dot(read_r, write_r, ((1,), (1,)))
    lane = lax.broadcasted_iota(jnp.int32, (BLOCK, LANES), 1)
    zero = jnp.zeros((BLOCK, LANES), bf16)
    pieces = []
    for pair in range(heads // 2):
        highs, lows = [], []
        for h in (2 * pair, 2 * pair + 1):
            r = heads + h
            gap = jnp.where(
                below, run[:, h : h + 1] - run_t[h : h + 1], run[:, r : r + 1] - run_t[r : r + 1]
            )
            gap = jnp.where(row == col, 0.0, gap)
            from_f = score_f * steps_t[h : h + 1]
            from_r = score_r * steps_t[r : r + 1]
            weight = jnp.where(below, from_f, jnp.where(above, from_r, from_f + from_r))
            high, low = halves(weight * jnp.exp(gap))
            highs.append(high)
            lows.append(low)
        values = x[:, pair * LANES : (pair + 1) * LANES]
        stacked = jnp.concatenate(
            [jnp.where(lane < HEAD_DIM, values, zero), jnp.where(lane < HEAD_DIM, zero, values)],
            axis=0,
        )
        pieces.append(
            dot(jnp.concatenate(highs, axis=1), stacked)
            + dot(jnp.concatenate(lows, axis=1), stacked)
        )
    inside = jnp.concatenate(pieces, axis=1) if len(pieces) > 1 else pieces[0]
    grown = jnp.exp(run)
    carried_f = dot(jnp.concatenate([read_f, read_f], axis=1), prefix_ref[0, 0, 0])
    carried_r = dot(jnp.concatenate([read_r, read_r], axis=1), prefix_ref[0, 1, 0])
    out_ref[0] = (
        inside
        + spread(grown, 0, heads) * carried_f
        + spread(grown, heads, heads) * carried_r
        + skip_ref[...] * x.astype(f32)
    )


def incoming_kernel(heads, count, mine_ref, states_ref, coef_ref, pos_ref, local_ref,
                    mixed_ref, square_ref, held):
    width = local_ref.shape[2]
    mine = mine_ref[0]

    @pl.when(pl.program_id(1) == 0)
    def _():
        for way in range(2):
            before = jnp.zeros((STATE, width), f32)
            for k in range(count):
                at = k if way == 0 else count - 1 - k
                decay = jnp.exp(states_ref[at, 0, way, STATE : STATE + 1, :])
                new = decay * before + states_ref[at, 0, way, :STATE, :]
                reached = (at < mine) if way == 0 else (at > mine)
                before = jnp.where(reached, new, before)
            high, low = halves(before)
            held[way, :STATE, :] = high
            held[way, STATE:, :] = low

    grown = jnp.exp(pos_ref[0])
    coef = coef_ref[0]
    read_f = coef[:, STATE : 2 * STATE]
    read_r = coef[:, 3 * STATE :]
    mixed = (
        local_ref[0]
        + spread(grown, 0, heads) * dot(jnp.concatenate([read_f, read_f], axis=1), held[0])
        + spread(grown, heads, heads) * dot(jnp.concatenate([read_r, read_r], axis=1), held[1])
    )
    mixed_ref[0] = mixed
    ones = jnp.ones((8, width), bf16)
    square_ref[0] = sum(dot(ones, part, ((1,), (1,))) for part in thirds(mixed * mixed))


def tail_kernel(shards, factor, normed_ref, out_w_ref, head_ref, patches_ref, scale_ref,
                label_ref, logit_ref, loss_ref, head_grad_ref, hidden_ref=None):
    rows = patches_ref.shape[0]
    head = head_ref[...]
    patches = patches_ref[...].astype(f32)
    hiddens, logs = [], []
    for v in range(VIEWS):
        total = dot(normed_ref[0, v], out_w_ref[0])
        for s in range(1, shards):
            total += dot(normed_ref[s, v], out_w_ref[s])
        view = (scale_ref[v : v + 1, :] * patches).astype(bf16)
        hidden = (view.astype(f32) + total).astype(bf16)
        hiddens.append(hidden)
        logits = dot(hidden, head)
        shifted = logits - jnp.max(logits, axis=1, keepdims=True)
        logs.append(shifted - jnp.log(jnp.sum(jnp.exp(shifted), axis=1, keepdims=True)))
    top = jnp.maximum(jnp.maximum(logs[0], logs[1]), logs[2])
    mean = top + jnp.log(sum(jnp.exp(log - top) for log in logs)) - jnp.log(f32(VIEWS))
    lane = lax.broadcasted_iota(jnp.int32, (rows, CLASSES), 1)
    onehot = (lane == label_ref[...]).astype(f32)
    spread_sum = jnp.zeros((rows, 1), f32)
    grads = []
    for v in range(VIEWS):
        prob = jnp.exp(logs[v])
        gap = logs[v] - mean
        inner = jnp.sum(prob * gap, axis=1, keepdims=True)
        spread_sum += inner
        grad = (mix_lambda / VIEWS) * prob * (gap - inner)
        if v == 0:
            grad += prob - onehot
        grads.append((factor * grad).astype(bf16))
        logit_ref[v] = grads[v]
    cross = -jnp.sum(onehot * logs[0], axis=1, keepdims=True)
    loss_ref[...] = cross + mix_lambda * (spread_sum / VIEWS)
    update = sum(dot(hiddens[v], grads[v], ((0,), (0,))) for v in range(VIEWS))

    @pl.when(pl.program_id(0) == 0)
    def _():
        head_grad_ref[...] = update

    @pl.when(pl.program_id(0) > 0)
    def _():
        head_grad_ref[...] += update


def grad_kernel(shards, normed_ref, logit_ref, head_ref, out_ref):
    grads = logit_ref[0, 0]
    hidden = dot(grads, head_ref[...], ((1,), (1,))).astype(bf16)
    update = dot(normed_ref[0], hidden, ((0,), (0,)))
    first = (pl.program_id(0) == 0) & (pl.program_id(1) == 0)

    @pl.when(first)
    def _():
        out_ref[...] = update

    @pl.when(jnp.logical_not(first))
    def _():
        out_ref[...] += update


def call(kernel, name, flops, moved, limit=48 << 20, **options):
    return pl.pallas_call(
        kernel,
        name=name,
        compiler_params=pltpu.CompilerParams(vmem_limit_bytes=limit),
        cost_estimate=pl.CostEstimate(flops=flops, bytes_accessed=moved, transcendentals=0),
        **options,
    )


def own(columns, place, shards, heads, width):
    shaped = columns.reshape(columns.shape[0], heads, shards, width)
    return lax.dynamic_index_in_dim(shaped, place, 2, False).reshape(-1, heads * width)


def on_device(
    patches,
    labels,
    op_ids,
    mix_codes,
    aug_gains,
    in_weight,
    dt_weight,
    dt_bias,
    decay_log,
    skip_gain,
    norm_gain,
    out_weight,
    head_weight,
):
    row_count = patches.shape[0]
    ctx_count = lax.axis_size("ctx")
    shards = lax.axis_size("fsdp")
    place = lax.axis_index("fsdp")
    total_patches = row_count * ctx_count * shards
    inner = out_weight.shape[0] * shards
    heads = HEADS // shards
    width = heads * HEAD_DIM
    rows = row_count * shards
    pieces = rows // BLOCK

    patches_all = lax.all_gather(patches, "fsdp", axis=0, tiled=True)
    weights = lax.all_gather(
        jnp.concatenate([in_weight, dt_weight], axis=1), "fsdp", axis=0, tiled=True
    )
    out_all = lax.all_gather(out_weight, "fsdp", axis=0, tiled=True)
    columns_in = inner + 4 * STATE
    step_columns = weights[:, columns_in:].reshape(D, 2 * heads, shards)
    step_columns = lax.dynamic_index_in_dim(step_columns, place, 2, False)
    mine_weight = jnp.concatenate(
        [
            own(weights[:, :inner], place, shards, heads, HEAD_DIM),
            weights[:, inner:columns_in],
            step_columns,
            jnp.zeros((D, LANES - 2 * heads), bf16),
        ],
        axis=1,
    )
    scales = view_scales(op_ids, mix_codes, aug_gains)
    views = (scales[:, None, :] * patches_all.astype(f32)[None]).astype(bf16)
    projected = dot(views.reshape(VIEWS * rows, D), mine_weight)
    projected = projected.reshape(VIEWS, rows, width + 5 * STATE)
    x = projected[:, :, :width].astype(bf16)
    coef = projected[:, :, width : width + 4 * STATE].astype(bf16)
    raw = projected[:, :, width + 4 * STATE :]

    def local_lanes(values):
        picked = lax.dynamic_index_in_dim(values.reshape(2 * heads, shards), place, 1, False)
        return jnp.pad(picked, (0, LANES - 2 * heads))[None, :]

    bias = local_lanes(dt_bias)
    rate = local_lanes(-jnp.exp(decay_log))
    skip = lax.dynamic_index_in_dim(skip_gain.reshape(heads, shards), place, 1, False)
    skip = jnp.repeat(skip, HEAD_DIM)[None, :]
    gain = own(norm_gain[None, :], place, shards, heads, HEAD_DIM)

    whole = lambda *dims: pl.BlockSpec((1, *dims), lambda v: (v,) + (0,) * len(dims))
    fixed = lambda *dims: pl.BlockSpec(dims, lambda *_: (0,) * len(dims))
    final, prefix, steps, run, pos = call(
        functools.partial(states_kernel, heads), "states",
        VIEWS * rows * STATE * width * 8, VIEWS * rows * 8192,
        grid=(VIEWS,),
        in_specs=[whole(rows, LANES), whole(rows, width), whole(rows, 4 * STATE),
                  fixed(1, LANES), fixed(1, LANES)],
        out_specs=[whole(2, STATE + LOG_ROWS, width), whole(2, pieces, 2 * STATE, width),
                   whole(rows, LANES), whole(rows, LANES), whole(rows, LANES)],
        out_shape=[
            jax.ShapeDtypeStruct((VIEWS, 2, STATE + LOG_ROWS, width), f32),
            jax.ShapeDtypeStruct((VIEWS, 2, pieces, 2 * STATE, width), bf16),
            jax.ShapeDtypeStruct((VIEWS, rows, LANES), f32),
            jax.ShapeDtypeStruct((VIEWS, rows, LANES), f32),
            jax.ShapeDtypeStruct((VIEWS, rows, LANES), f32),
        ],
    )(raw, x, coef, bias, rate)
    everything = lax.all_gather(final, "ctx")

    block = lambda *dims: pl.BlockSpec((1, *dims), lambda v, i: (v, i) + (0,) * (len(dims) - 1))
    local = call(
        functools.partial(inside_kernel, heads), "inside",
        VIEWS * rows * STATE * width * 16, VIEWS * rows * 8192,
        grid=(VIEWS, pieces),
        in_specs=[block(BLOCK, width), block(BLOCK, 4 * STATE),
                  pl.BlockSpec((1, 2, 1, 2 * STATE, width), lambda v, i: (v, 0, i, 0, 0)),
                  block(BLOCK, LANES), block(BLOCK, LANES), fixed(1, width)],
        out_specs=block(BLOCK, width),
        out_shape=jax.ShapeDtypeStruct((VIEWS, rows, width), f32),
    )(x, coef, prefix, steps, run, skip)

    span = min(rows, 512)
    mixed, squares = call(
        functools.partial(incoming_kernel, heads, ctx_count), "incoming",
        VIEWS * rows * STATE * width * 8, VIEWS * rows * 8192,
        grid=(VIEWS, rows // span),
        in_specs=[
            pl.BlockSpec(memory_space=pltpu.SMEM),
            pl.BlockSpec((ctx_count, 1, 2, STATE + LOG_ROWS, width), lambda v, i: (0, v, 0, 0, 0)),
            block(span, 4 * STATE), block(span, LANES), block(span, width)],
        out_specs=[block(span, width), pl.BlockSpec((1, 8, span), lambda v, i: (v, 0, i))],
        out_shape=[
            jax.ShapeDtypeStruct((VIEWS, rows, width), f32),
            jax.ShapeDtypeStruct((VIEWS, 8, rows), f32),
        ],
        scratch_shapes=[pltpu.VMEM((2, 2 * STATE, width), bf16)],
    )(lax.axis_index("ctx").reshape(1), everything, coef, pos, local)

    square_total = lax.psum(squares[:, 0, :], "fsdp")
    scaling = lax.rsqrt(square_total / inner + 1e-05)
    normed = (mixed * scaling[:, :, None] * gain[None]).astype(bf16)
    outgoing = normed.reshape(VIEWS, shards, row_count, width).transpose(1, 0, 2, 3)
    arrived = lax.all_to_all(outgoing, "fsdp", split_axis=0, concat_axis=0)

    out_own = out_all.reshape(heads, shards, HEAD_DIM, D).transpose(1, 0, 2, 3)
    out_own = out_own.reshape(shards, width, D)
    tile = min(row_count, 128)
    grads, losses, head_term = call(
        functools.partial(tail_kernel, shards, loss_scale / total_patches), "tail",
        VIEWS * row_count * D * 3000, 6 << 20,
        grid=(row_count // tile,),
        in_specs=[
            pl.BlockSpec((shards, VIEWS, tile, width), lambda i: (0, 0, i, 0)),
            fixed(shards, width, D), fixed(D, CLASSES),
            pl.BlockSpec((tile, D), lambda i: (i, 0)),
            fixed(VIEWS, D),
            pl.BlockSpec((tile, 1), lambda i: (i, 0))],
        out_specs=[
            pl.BlockSpec((VIEWS, tile, CLASSES), lambda i: (0, i, 0)),
            pl.BlockSpec((tile, 1), lambda i: (i, 0)),
            fixed(D, CLASSES)],
        out_shape=[
            jax.ShapeDtypeStruct((VIEWS, row_count, CLASSES), bf16),
            jax.ShapeDtypeStruct((row_count, 1), f32),
            jax.ShapeDtypeStruct((D, CLASSES), f32),
        ],
    )(arrived, out_own, head_weight, patches, scales, labels[:, None])

    if ctx_count * shards == HEADS:
        grads_all = lax.all_gather(grads, "fsdp")
        grad_rows = call(
            functools.partial(grad_kernel, shards), "grads",
            VIEWS * rows * D * (width + CLASSES) * 2, 8 << 20,
            grid=(VIEWS, shards),
            in_specs=[
                pl.BlockSpec((1, row_count, width), lambda v, s: (v, s, 0)),
                pl.BlockSpec((1, 1, row_count, CLASSES), lambda v, s: (s, v, 0, 0)),
                fixed(D, CLASSES)],
            out_specs=fixed(width, D),
            out_shape=jax.ShapeDtypeStruct((width, D), f32),
        )(normed, grads_all, head_weight)
        grad_out = lax.psum_scatter(grad_rows, "ctx", scatter_dimension=0, tiled=True)
    else:
        grad_hidden = lax.dot_general(
            grads, head_weight, (((2,), (1,)), ((), ())), preferred_element_type=f32
        ).astype(bf16)
        grad_rows = lax.dot_general(
            arrived, grad_hidden, (((1, 2), (0, 1)), ((), ())), preferred_element_type=f32
        )
        grad_rows = grad_rows.reshape(shards, heads, HEAD_DIM, D).transpose(1, 0, 2, 3)
        grad_out = lax.psum_scatter(
            grad_rows.reshape(inner, D), ("ctx", "fsdp"), scatter_dimension=0, tiled=True
        )
    grad_head = lax.psum_scatter(head_term, ("ctx", "fsdp"), scatter_dimension=0, tiled=True)
    return (grad_out, grad_head, losses[:, 0])


def solution(mesh):
    return jax.shard_map(
        on_device,
        mesh=mesh,
        in_specs=(
            P(("groups", "ctx", "fsdp"), None),
            P(("groups", "ctx", "fsdp")),
            P("groups", None),
            P("groups", None),
            P(),
            P("fsdp", None),
            P("fsdp", None),
            P(),
            P(),
            P(),
            P(),
            P("fsdp", None),
            P(),
        ),
        out_specs=(
            P(("groups", "ctx", "fsdp"), None),
            P(("groups", "ctx", "fsdp"), None),
            P(("groups", "ctx", "fsdp")),
        ),
        check_vma=False,
    )
```

time: 558 us -> 334 us (0.60)
  matrix products: 141 us -> 8.78 us
  local copies, waits for them, and re-layouts: 107 us -> 31.8 us
  Pallas kernels: 0 us -> 68.9 us
  waiting for transfers between devices: 205 us -> 176 us
  other arithmetic: 32.1 us -> 9.67 us
  blocking collectives: 39.8 us -> 19.4 us
  starting transfers between devices: 11.3 us -> 3.81 us
    dot_general x72 -> x1, matrix products: 141 us -> 8.61 us  [dot(): return lax.dot_general(a, b, (dims, ((), ())), preferred_element_type=f32)]
    pallas_call x0 -> x5, Pallas kernels: none -> 68.9 us  [the longest x1 25.9 us: on_device(): call(functools.partial(states_kernel, heads), 'states', VIEWS * rows * ST...]
    all_gather x5 -> x4, waiting for transfers between devices: 29.2 us -> 93.2 us  [the longest x1 43.1 us: on_device(): everything = lax.all_gather(final, 'ctx')]
    reduce_scatter x1, waiting for transfers between devices: 76.3 us -> 29 us  [on_device(): lax.psum_scatter(grad_rows, 'ctx', scatter_dimension=0, tiled=True)]
    all_to_all x3 -> x1, waiting for transfers between devices: 52.2 us -> 16 us  [on_device(): arrived = lax.all_to_all(outgoing, 'fsdp', split_axis=0, concat_axis=0)]
    rev x5 -> x0, local copies, waits for them, and re-layouts: 31.8 us -> none  [the longest x1 10.3 us: on_device(): jnp.flip(coefficients[:, :, 2], 1)]
    all_gather x3 -> x1, blocking collectives: 29.4 us -> 8 us  [on_device(): grads_all = lax.all_gather(grads, 'fsdp')]
    another operation x24 -> x2, local copies, waits for them, and re-layouts: 16.4 us -> 0.16 us  [the longest x1 0.08 us: on_device(): skip = jnp.repeat(skip, HEAD_DIM)[None, :]]
  transfers between devices with their start and end apart: 10 -> 7, of which waited for: 6 -> 6; matrix products, arithmetic and copies ran while one was open for 28% -> 5% of each run, Pallas kernels for 0% -> 12%
where the time goes in v1:
time: 334 us; the launch traced here: 332 us
  waiting for transfers between devices  176 us (53%)
  Pallas kernels  68.9 us (21%)
  local copies, waits for them, and re-layouts  31.8 us (10%)
  blocking collectives  19.4 us (6%)
  between operations  14.4 us (4%)
  other arithmetic  9.67 us (3%)
  matrix products  8.78 us (3%)
  starting transfers between devices  3.81 us (1%)
    all_gather x1, waiting for transfers between devices, on_device(): everything = lax.all_gather(final, 'ctx')  43.1 us
    reduce_scatter x1, waiting for transfers between devices, on_device(): lax.psum_scatter(head_term, ('ctx', 'fsdp'), scatter_dimension=0, tiled=T...  36.1 us
    reduce_scatter x1, waiting for transfers between devices, on_device(): lax.psum_scatter(grad_rows, 'ctx', scatter_dimension=0, tiled=True)  29 us
    all_gather x1, waiting for transfers between devices, on_device(): lax.all_gather(jnp.concatenate([in_weight, dt_weight], axis=1), 'fsdp', a...  27.6 us
    pallas_call x1, Pallas kernels, on_device(): call(functools.partial(states_kernel, heads), 'states', VIEWS * rows * ST...  25.9 us
    all_gather x1, waiting for transfers between devices, on_device(): patches_all = lax.all_gather(patches, 'fsdp', axis=0, tiled=True)  22.5 us
    pallas_call x1, Pallas kernels, on_device(): call(functools.partial(inside_kernel, heads), 'inside', VIEWS * rows * ST...  21.2 us
    all_to_all x1, waiting for transfers between devices, on_device(): arrived = lax.all_to_all(outgoing, 'fsdp', split_axis=0, concat_axis=0)  16 us
  transfers between devices with their start and end apart: 7, of which 6 were waited for; matrix products, arithmetic and copies ran while one was open for 5% of the time, Pallas kernels for 12%

profile of v1, /device:TPU:0, one launch (start us, length us, event | category | flops | bytes accessed | tf_op | source)
XLA Modules:
  0.0 332.4 jit_solution(12120214746777386002)
XLA Ops:
  7.3 0.7 all-gather.7.cloned.1.call-update
  8.0 0.8 copy.38
  8.8 2.1 pad_maximum_fusion
  11.0 0.0 all-gather.13.cloned.1.call-start
  11.1 0.1 slice_reduce_fusion
  11.2 0.1 slice_divide_fusion
  11.3 0.1 copy.37
  11.4 0.1 copy.36
  11.5 0.1 reshape.56
  11.5 0.1 reshape.55
  11.6 0.2 fusion.11
  11.8 0.1 fusion.10
  11.9 0.2 fusion.8
  12.1 0.1 pad.13.clone
  12.2 0.2 dynamic-slice_reduce_fusion
  12.4 22.5 %all-gather.7.cloned.1.call-done = bf16[1024,1024]{1,0:T(8,128)(2,1)} async-done(((bf16[256,1024]{1,0:T(8,128)(2,1)}), bf16[1024,1024]{1,0:T(8,128)(2,1)}) %all-gather.7.cloned.1.call-update) | async-done | bytes 2097168 | tf_op jit(solution)/shard_map/all_gather | solution.py:317
  34.9 4.0 %convert_element_type.21 = f32[1024,1024]{1,0:T(8,128)} convert(bf16[1024,1024]{1,0:T(8,128)(2,1)} %all-gather.7.cloned.1.call-done) | non-fusion elementwise | flops 1048576 | bytes 6291456 | tf_op jit(solution)/shard_map/convert_element_type | solution.py:335
  38.9 27.6 %all-gather.9.cloned.1.call-done = bf16[1024,1568]{1,0:T(8,128)(2,1)} async-done(((bf16[256,1568]{1,0:T(8,128)(2,1)}), bf16[1024,1568]{1,0:T(8,128)(2,1)}) %all-gather.9.cloned.1.call-update) | async-done | bytes 3211280 | tf_op jit(solution)/shard_map/all_gather | solution.py:318
  66.6 1.6 slice-done
  68.1 2.6 copy.39
  70.8 1.2 constant_dynamic-slice_fusion.1
  71.9 0.2 copy.42
  72.1 0.1 copy.40
  72.4 0.2 copy.41
  72.5 8.6 %fusion.13 = (bf16[3,1024,896]{2,1,0:T(8,128)(2,1)S(1)}, f32[3,1024,896]{2,1,0:T(8,128)S(1)}) fusion(bf16[1024,8]{1,0:T(8,128)(2,1)S(1)} %bitcast.39, bf16[1024,512]{1,0:T(8,128)(2,1)S(1)} %slice-done.2, bf16[1024,256]{1,0:T(8,128)(2,1)S(1)} %copy.42, bf16[896]{0:T(1024)(128)(2,1)S(1)} %pad.13.clone, f32[1024,1024]{1,0:T(8,128)} %convert_element_type.21, ...), kind=kOutput, calls=%fused_computation.35 | convolution fusion | flops 5653528576 | bytes 22312704 | tf_op jit(solution)/shard_map/dot_general | solution.py:57
  81.2 2.0 slice.44.coef_ref
  83.1 1.3 slice.43.x_ref
  84.4 1.3 slice.42.raw_ref
  85.7 25.9 %states.1 = (f32[3,2,136,256]{3,2,1,0:T(8,128)S(1)}, bf16[3,2,8,256,256]{4,3,2,1,0:T(8,128)(2,1)}, f32[3,1024,128]{2,1,0:T(8,128)S(1)}, f32[3,1024,128]{2,1,0:T(8,128)S(1)}, f32[3,1024,128]{2,1,0:T(8,128)S(1)}) custom-call(f32[3,1024,128]{2,1,0:T(8,128)} %slice.42.raw_ref, bf16[3,1024,256]{2,1,0:T(8,128)(2,1)} %slice.43.x_ref, ...), custom_call_target="tpu_custom_call" | custom-call | flops 805306368 | bytes 25165824 | tf_op jit(solution)/shard_map/states/pallas_call | solution.py:354
  111.6 1.2 copy-done.5
  112.8 1.1 copy-done.7
  113.9 0.9 copy-done.9
  114.9 0.5 all-gather.11.cloned.1.call-update
  115.4 0.1 reshape.57
  115.5 0.2 dynamic-slice_reduce_fusion.3
  115.7 0.1 broadcast_in_dim.13
  115.8 0.1 broadcast_in_dim_reshape.4.skip_ref
  115.9 0.1 reshape_broadcast_in_dim.3
  116.0 0.1 mul.61
  116.1 1.4 copy-done.6
  117.5 21.2 %inside.1.local_ref = f32[3,1024,256]{2,1,0:T(8,128)} custom-call(bf16[3,1024,256]{2,1,0:T(8,128)(2,1)S(1)} %copy-done.2, bf16[3,1024,512]{2,1,0:T(8,128)(2,1)} %slice.44.coef_ref, bf16[3,2,8,256,256]{4,3,2,1,0:T(8,128)(2,1)} %get-tuple-element.15.prefix_ref, f32[3,1024,128]{2,1,0:T(8,128)S(1)} %get-tuple-element.16.steps_ref, ...), custom_call_target="tpu_custom_call" | custom-call | flops 1610612736 | bytes 25165824 | tf_op jit(solution)/shard_map/inside/pallas_call | solution.py:373
  138.7 43.1 %all-gather.13.cloned.1.call-done = f32[12,2,136,256]{3,2,1,0:T(8,128)} async-done(((f32[3,2,136,256]{3,2,1,0:T(8,128)}), f32[12,2,136,256]{3,2,1,0:T(8,128)}) %all-gather.13.cloned.1.call-update) | async-done | bytes 3342352 | tf_op jit(solution)/shard_map/all_gather | solution.py:370
  181.8 1.4 copy-done.8
  183.2 9.1 %incoming.1 = (f32[3,1024,256]{2,1,0:T(8,128)S(1)}, f32[3,8,1024]{2,1,0:T(8,128)S(1)}) custom-call(s32[1]{0:T(128)} %bitcast.mine_ref, f32[4,3,2,136,256]{4,3,2,1,0:T(8,128)} %bitcast.35, bf16[3,1024,512]{2,1,0:T(8,128)(2,1)} %slice.44.coef_ref, f32[3,1024,128]{2,1,0:T(8,128)S(1)} %copy-done.8, f32[3,1024,256]{2,1,0:T(8,128)} %inside.1.local_ref), custom_call_target="tpu_custom_call" | custom-call | flops 805306368 | bytes 25165824 | tf_op jit(solution)/shard_map/incoming/pallas_call | solution.py:385
  192.2 1.7 copy-done.3
  193.9 11.4 %psum.7 = f32[3,1024]{1,0:T(4,128)S(1)} all-reduce(f32[3,1024]{1,0:T(4,128)S(1)} %bitcast.40), channel_id=1, replica_groups=mesh['groups'=2,'ctx'=4,'fsdp'=4] {'fsdp'}, use_global_device_ids=true, to_apply=%region_2.3 | all-reduce | flops 3072 | bytes 24576 | tf_op jit(solution)/shard_map/psum | solution.py:401
  205.3 2.4 multiply_convert_fusion.2.normed_ref
  207.7 1.3 copy.49
  209.0 3.6 %all-to-all-start = ((bf16[4,3,256,256]{3,2,1,0:T(8,128)(2,1)}), bf16[4,3,256,256]{3,2,1,0:T(8,128)(2,1)S(1)}, u32[]{:S(2)}, u32[]{:S(2)}) async-start(bf16[4,3,256,256]{3,2,1,0:T(8,128)(2,1)} %bitcast.34), calls=%async_computation | async-start | bytes 3145728 | tf_op jit(solution)/shard_map/all_to_all | solution.py:405
  212.6 0.8 copy.45.label_ref
  213.4 3.2 copy.44
  216.6 16.0 %all-to-all-done.normed_ref = bf16[4,3,256,256]{3,2,1,0:T(8,128)(2,1)S(1)} async-done(((bf16[4,3,256,256]{3,2,1,0:T(8,128)(2,1)}), bf16[4,3,256,256]{3,2,1,0:T(8,128)(2,1)S(1)}, u32[]{:S(2)}, u32[]{:S(2)}) %all-to-all-start) | async-done | bytes 1572896 | tf_op jit(solution)/shard_map/all_to_all | solution.py:405
  232.6 1.6 copy-done.4
  234.2 1.0 copy-done.10
  235.2 0.9 copy-done.12
  236.1 0.9 copy-done.13
  237.1 4.5 %tail.1 = (bf16[3,256,128]{2,1,0:T(8,128)(2,1)S(1)}, f32[256,1]{1,0:T(8,128)S(1)}, f32[1024,128]{1,0:T(8,128)S(1)}) custom-call(bf16[4,3,256,256]{3,2,1,0:T(8,128)(2,1)S(1)} %all-to-all-done.normed_ref, bf16[4,256,1024]{2,1,0:T(8,128)(2,1)S(1)} %bitcast.32, bf16[1024,128]{1,0:T(8,128)(2,1)S(1)} %copy-done.13, bf16[256,1024]{1,0:T(8,128)(2,1)S(1)} %copy-done.10, ...), custom_call_target="tpu_custom_call" | custom-call | flops 2359296000 | bytes 6291456 | tf_op jit(solution)/shard_map/tail/pallas_call | solution.py:410
  241.6 0.8 copy-done.11
  242.5 8.0 %all-gather.1 = bf16[12,256,128]{2,1,0:T(8,128)(2,1)S(1)} all-gather(bf16[3,256,128]{2,1,0:T(8,128)(2,1)S(1)} %get-tuple-element.20), channel_id=3, replica_groups=mesh['groups'=2,'ctx'=4,'fsdp'=4] {'fsdp'}, dimensions={0}, use_global_device_ids=true | all-gather | bytes 983040 | tf_op jit(solution)/shard_map/all_gather | solution.py:432
  250.5 1.0 copy-done.14
  251.5 8.2 %grads.1 = f32[256,1024]{1,0:T(8,128)} custom-call(bf16[3,1024,256]{2,1,0:T(8,128)(2,1)S(1)} %multiply_convert_fusion.2.normed_ref, bf16[4,3,256,128]{3,2,1,0:T(8,128)(2,1)S(1)} %bitcast.33, bf16[1024,128]{1,0:T(8,128)(2,1)S(1)} %copy-done.14), custom_call_target="tpu_custom_call" | custom-call | flops 2415919104 | bytes 8388608 | tf_op jit(solution)/shard_map/grads/pallas_call | solution.py:433
  259.7 0.7 reduce.6
  260.4 36.1 %reduce-scatter.5.cloned.1.call-done = f32[64,128]{1,0:T(8,128)} async-done(((f32[1024,128]{1,0:T(8,128)}), f32[64,128]{1,0:T(8,128)}) %reduce-scatter.5.cloned.1.call-update) | async-done | bytes 32784 | tf_op jit(solution)/shard_map/reduce_scatter | solution.py:456
  296.5 29.0 %reduce-scatter.3.cloned.1.call-done = f32[64,1024]{1,0:T(8,128)} async-done(((f32[256,1024]{1,0:T(8,128)}), f32[64,1024]{1,0:T(8,128)}) %reduce-scatter.3.cloned.1.call-update) | async-done | bytes 262160 | tf_op jit(solution)/shard_map/reduce_scatter | solution.py:444
  (59 shorter events, 0.5 us)
Async XLA Ops:
  7.2 4.7 %copy-start = (f32[9,1024]{1,0:T(8,128)S(1)}, f32[9,1024]{1,0:T(8,128)}, u32[]{:S(2)}) copy-start(f32[9,1024]{1,0:T(8,128)} %param.17) | copy-start | bytes 110596
  7.2 3.9 %copy-start.19 = (s32[2,4]{1,0:T(2,128)S(1)}, s32[2,4]{1,0:T(2,128)}, u32[]{:S(2)}) copy-start(s32[2,4]{1,0:T(2,128)} %param.16) | copy-start | bytes 100
  7.2 4.2 %copy-start.17 = (s32[2,3]{1,0:T(2,128)S(1)}, s32[2,3]{1,0:T(2,128)}, u32[]{:S(2)}) copy-start(s32[2,3]{1,0:T(2,128)} %param.15) | copy-start | bytes 76
  7.2 4.2 %copy-start.20 = (f32[2,16]{1,0:T(2,128)S(1)}, f32[2,16]{1,0:T(2,128)}, u32[]{:S(2)}) copy-start(f32[2,16]{1,0:T(2,128)} %param.21) | copy-start | bytes 388
  7.2 4.3 %copy-start.18 = (f32[2,16]{1,0:T(2,128)S(1)}, f32[2,16]{1,0:T(2,128)}, u32[]{:S(2)}) copy-start(f32[2,16]{1,0:T(2,128)} %param.20) | copy-start | bytes 388
  7.2 27.7 %all-gather.7.cloned.1.call-start = ((), (), s32[]{:S(2)}) async-start(), calls=%async_computation.3 | async-start | bytes 2621440 | tf_op jit(solution)/shard_map/all_gather | solution.py:317
  8.0 58.6 %all-gather.9.cloned.1.call-start = ((), (), s32[]{:S(2)}) async-start(), calls=%async_computation.4 | async-start | bytes 4259840 | tf_op jit(solution)/shard_map/all_gather | solution.py:318
  11.0 170.8 %all-gather.13.cloned.1.call-start = ((), (), s32[]{:S(2)}) async-start(), calls=%async_computation.8 | async-start | bytes 4177920 | tf_op jit(solution)/shard_map/all_gather | solution.py:370
  66.5 1.6 slice-start
  68.1 4.0 %slice-start.1 = ((bf16[1024,1568]{1,0:T(8,128)(2,1)}), bf16[1024,32]{1,0:T(8,128)(2,1)S(1)}, s32[]{:S(2)}) async-start(bf16[1024,1568]{1,0:T(8,128)(2,1)} %all-gather.9.cloned.1.call-done), calls=%async_computation.10 | async-start | bytes 524288 | tf_op jit(solution)/shard_map/slice | solution.py:323
  70.8 1.8 slice-start.2
  85.7 29.8 %copy-start.21 = (f32[16]{0:T(128)S(1)}, f32[16]{0:T(128)}, u32[]{:S(2)}) copy-start(f32[16]{0:T(128)} %param.22) | copy-start | bytes 196
  85.7 30.2 %copy-start.15 = (f32[1024]{0:T(1024)S(1)}, f32[1024]{0:T(1024)}, u32[]{:S(2)}) copy-start(f32[1024]{0:T(1024)} %param.23) | copy-start | bytes 12292
  85.7 30.4 %copy-start.2 = (bf16[3,1024,256]{2,1,0:T(8,128)(2,1)S(1)}, bf16[3,1024,256]{2,1,0:T(8,128)(2,1)}, u32[]{:S(2)}) copy-start(bf16[3,1024,256]{2,1,0:T(8,128)(2,1)} %slice.43.x_ref) | copy-start | bytes 4718596
  111.6 1.2 copy-start.5
  112.8 1.1 copy-start.7
  113.9 0.9 copy-start.9
  114.8 98.5 %all-gather.11.cloned.1.call-start = ((), (), s32[]{:S(2)}) async-start(), calls=%async_computation.5 | async-start | bytes 2621440 | tf_op jit(solution)/shard_map/all_gather | solution.py:321
  116.1 1.4 copy-start.6
  181.8 1.4 copy-start.8
  192.2 1.7 copy-start.3
  207.7 4.9 %copy-start.16 = (s32[256]{0:T(256)S(1)}, s32[256]{0:T(256)}, u32[]{:S(2)}) copy-start(s32[256]{0:T(256)} %param.14) | copy-start | bytes 3076
  209.0 23.6 %all-to-all-start = ((bf16[4,3,256,256]{3,2,1,0:T(8,128)(2,1)}), bf16[4,3,256,256]{3,2,1,0:T(8,128)(2,1)S(1)}, u32[]{:S(2)}, u32[]{:S(2)}) async-start(bf16[4,3,256,256]{3,2,1,0:T(8,128)(2,1)} %bitcast.34), calls=%async_computation | async-start | bytes 3145728 | tf_op jit(solution)/shard_map/all_to_all | solution.py:405
  212.5 84.0 %reduce-scatter.5.cloned.1.call-start = ((), (), s32[]{:S(2)}) async-start(), calls=%async_computation.7 | async-start | bytes 557056 | tf_op jit(solution)/shard_map/reduce_scatter | solution.py:456
  232.6 1.6 copy-start.4
  234.2 1.0 copy-start.10
  235.2 0.9 copy-start.12
  236.1 0.9 copy-start.13
  241.6 0.8 copy-start.11
  242.5 83.1 %reduce-scatter.3.cloned.1.call-start = ((), (), s32[]{:S(2)}) async-start(), calls=%async_computation.6 | async-start | bytes 1310720 | tf_op jit(solution)/shard_map/reduce_scatter | solution.py:444
  250.5 75.0 %copy-start.1 = (f32[9,1024]{1,0:T(8,128)S(1)}, f32[9,1024]{1,0:T(8,128)}, u32[]{:S(2)}) copy-start(f32[9,1024]{1,0:T(8,128)} %param.17) | copy-start | bytes 110596
  250.5 1.0 copy-start.14
Sparse Core Ops, SparseCore 0:
  9.6 25.2 all-gather.6
  36.5 30.0 all-gather.8
  115.0 66.7 all-gather.12
  183.2 21.3 all-gather.10
  242.6 53.8 reduce-scatter.4
  299.3 26.1 reduce-scatter.2

commit v2 on v1

--- a/solution.py
+++ b/solution.py
@@ -103,7 +103,7 @@
 
     zero = jnp.zeros((STATE, width), f32)
     no_log = jnp.zeros((1, LANES), f32)
-    state, total = lax.fori_loop(0, pieces, first_pass, (zero, no_log))
+    state, total = lax.fori_loop(0, pieces, first_pass, (zero, no_log), unroll=4)
     final_ref[0, 0, :STATE, :] = state
     final_ref[0, 0, STATE:, :] = jnp.broadcast_to(spread(total, 0, heads), (LOG_ROWS, width))
 
@@ -124,12 +124,13 @@
         prefix_ref[0, 1, i, STATE:, :] = s_low
         return spread(jnp.exp(last), heads, heads) * state + fresh, total + last
 
-    state, total = lax.fori_loop(0, pieces, second_pass, (zero, no_log))
+    state, total = lax.fori_loop(0, pieces, second_pass, (zero, no_log), unroll=4)
     final_ref[0, 1, :STATE, :] = state
     final_ref[0, 1, STATE:, :] = jnp.broadcast_to(spread(total, heads, heads), (LOG_ROWS, width))
 
 
-def inside_kernel(heads, x_ref, coef_ref, prefix_ref, steps_ref, run_ref, skip_ref, out_ref):
+def inside_kernel(heads, x_ref, coef_ref, prefix_ref, steps_ref, run_ref, skip_ref, *rest):
+    out_ref = rest[-1]
     row = lax.broadcasted_iota(jnp.int32, (BLOCK, BLOCK), 0)
     col = lax.broadcasted_iota(jnp.int32, (BLOCK, BLOCK), 1)
     below, above = row > col, row < col
@@ -180,22 +181,14 @@
     )
 
 
-def incoming_kernel(heads, count, mine_ref, states_ref, coef_ref, pos_ref, local_ref,
+def incoming_kernel(heads, forward_ref, reverse_ref, coef_ref, pos_ref, local_ref,
                     mixed_ref, square_ref, held):
     width = local_ref.shape[2]
-    mine = mine_ref[0]
 
     @pl.when(pl.program_id(1) == 0)
     def _():
-        for way in range(2):
-            before = jnp.zeros((STATE, width), f32)
-            for k in range(count):
-                at = k if way == 0 else count - 1 - k
-                decay = jnp.exp(states_ref[at, 0, way, STATE : STATE + 1, :])
-                new = decay * before + states_ref[at, 0, way, :STATE, :]
-                reached = (at < mine) if way == 0 else (at > mine)
-                before = jnp.where(reached, new, before)
-            high, low = halves(before)
+        for way, before in enumerate((forward_ref, reverse_ref)):
+            high, low = halves(before[0])
             held[way, :STATE, :] = high
             held[way, STATE:, :] = low
 
@@ -283,9 +276,22 @@
     )
 
 
-def own(columns, place, shards, heads, width):
-    shaped = columns.reshape(columns.shape[0], heads, shards, width)
-    return lax.dynamic_index_in_dim(shaped, place, 2, False).reshape(-1, heads * width)
+def carried_in(state, decay, axis, reverse):
+    count = lax.axis_size(axis)
+    if reverse:
+        hops = [(j, j - 1) for j in range(1, count)]
+    else:
+        hops = [(j, j + 1) for j in range(count - 1)]
+    sent, got = state, jnp.zeros_like(state)
+    for hop in range(count - 1):
+        got = lax.ppermute(sent, axis, hops)
+        sent = decay * got + state
+    return got
+
+
+def scatter_sum(terms, axes, count):
+    blocks = terms.reshape(count, -1, terms.shape[1])
+    return jnp.sum(lax.all_to_all(blocks, axes, split_axis=0, concat_axis=0), axis=0)
 
 
 def on_device(
@@ -315,22 +321,23 @@
     pieces = rows // BLOCK
 
     patches_all = lax.all_gather(patches, "fsdp", axis=0, tiled=True)
-    weights = lax.all_gather(
-        jnp.concatenate([in_weight, dt_weight], axis=1), "fsdp", axis=0, tiled=True
-    )
+    columns_in = inner + 4 * STATE
+    depth = in_weight.shape[0]
+    sent_weight = jnp.concatenate(
+        [
+            in_weight[:, :inner]
+            .reshape(depth, heads, shards, HEAD_DIM)
+            .transpose(2, 0, 1, 3)
+            .reshape(shards, depth, width),
+            jnp.broadcast_to(in_weight[None, :, inner:], (shards, depth, 4 * STATE)),
+            dt_weight.reshape(depth, 2 * heads, shards).transpose(2, 0, 1),
+            jnp.zeros((shards, depth, LANES - 2 * heads), bf16),
+        ],
+        axis=2,
+    )
+    mine_weight = lax.all_to_all(sent_weight, "fsdp", split_axis=0, concat_axis=0)
+    mine_weight = mine_weight.reshape(D, width + 5 * STATE)
     out_all = lax.all_gather(out_weight, "fsdp", axis=0, tiled=True)
-    columns_in = inner + 4 * STATE
-    step_columns = weights[:, columns_in:].reshape(D, 2 * heads, shards)
-    step_columns = lax.dynamic_index_in_dim(step_columns, place, 2, False)
-    mine_weight = jnp.concatenate(
-        [
-            own(weights[:, :inner], place, shards, heads, HEAD_DIM),
-            weights[:, inner:columns_in],
-            step_columns,
-            jnp.zeros((D, LANES - 2 * heads), bf16),
-        ],
-        axis=1,
-    )
     scales = view_scales(op_ids, mix_codes, aug_gains)
     views = (scales[:, None, :] * patches_all.astype(f32)[None]).astype(bf16)
     projected = dot(views.reshape(VIEWS * rows, D), mine_weight)
@@ -347,7 +354,8 @@
     rate = local_lanes(-jnp.exp(decay_log))
     skip = lax.dynamic_index_in_dim(skip_gain.reshape(heads, shards), place, 1, False)
     skip = jnp.repeat(skip, HEAD_DIM)[None, :]
-    gain = own(norm_gain[None, :], place, shards, heads, HEAD_DIM)
+    gain = norm_gain.reshape(heads, shards, HEAD_DIM)
+    gain = lax.dynamic_index_in_dim(gain, place, 1, False).reshape(1, width)
 
     whole = lambda *dims: pl.BlockSpec((1, *dims), lambda v: (v,) + (0,) * len(dims))
     fixed = lambda *dims: pl.BlockSpec(dims, lambda *_: (0,) * len(dims))
@@ -367,28 +375,38 @@
             jax.ShapeDtypeStruct((VIEWS, rows, LANES), f32),
         ],
     )(raw, x, coef, bias, rate)
-    everything = lax.all_gather(final, "ctx")
-
+    decay = jnp.exp(final[:, :, STATE : STATE + 1, :])
+    forward_in = carried_in(final[:, 0, :STATE], decay[:, 0], "ctx", False)
+    reverse_in = carried_in(final[:, 1, :STATE], decay[:, 1], "ctx", True)
+
+    local = ()
+    for v in range(VIEWS):
+        at = lambda *dims, v=v: pl.BlockSpec(
+            (1, *dims), lambda i: (v, i) + (0,) * (len(dims) - 1)
+        )
+        local = (call(
+            functools.partial(inside_kernel, heads), "inside",
+            rows * D * 8192, rows * 8192,
+            grid=(pieces,),
+            in_specs=[at(BLOCK, width), at(BLOCK, 4 * STATE),
+                      pl.BlockSpec((1, 2, 1, 2 * STATE, width), lambda i, v=v: (v, 0, i, 0, 0)),
+                      at(BLOCK, LANES), at(BLOCK, LANES), fixed(1, width)]
+            + [pl.BlockSpec(memory_space=pl.ANY)] * len(local),
+            out_specs=at(BLOCK, width),
+            out_shape=jax.ShapeDtypeStruct((VIEWS, rows, width), f32),
+            input_output_aliases={6: 0} if local else {},
+        )(x, coef, prefix, steps, run, skip, *local),)
+    (local,) = local
     block = lambda *dims: pl.BlockSpec((1, *dims), lambda v, i: (v, i) + (0,) * (len(dims) - 1))
-    local = call(
-        functools.partial(inside_kernel, heads), "inside",
-        VIEWS * rows * STATE * width * 16, VIEWS * rows * 8192,
-        grid=(VIEWS, pieces),
-        in_specs=[block(BLOCK, width), block(BLOCK, 4 * STATE),
-                  pl.BlockSpec((1, 2, 1, 2 * STATE, width), lambda v, i: (v, 0, i, 0, 0)),
-                  block(BLOCK, LANES), block(BLOCK, LANES), fixed(1, width)],
-        out_specs=block(BLOCK, width),
-        out_shape=jax.ShapeDtypeStruct((VIEWS, rows, width), f32),
-    )(x, coef, prefix, steps, run, skip)
+    entering = pl.BlockSpec((1, STATE, width), lambda v, i: (v, 0, 0))
 
     span = min(rows, 512)
     mixed, squares = call(
-        functools.partial(incoming_kernel, heads, ctx_count), "incoming",
+        functools.partial(incoming_kernel, heads), "incoming",
         VIEWS * rows * STATE * width * 8, VIEWS * rows * 8192,
         grid=(VIEWS, rows // span),
         in_specs=[
-            pl.BlockSpec(memory_space=pltpu.SMEM),
-            pl.BlockSpec((ctx_count, 1, 2, STATE + LOG_ROWS, width), lambda v, i: (0, v, 0, 0, 0)),
+            entering, entering,
             block(span, 4 * STATE), block(span, LANES), block(span, width)],
         out_specs=[block(span, width), pl.BlockSpec((1, 8, span), lambda v, i: (v, 0, i))],
         out_shape=[
@@ -396,9 +414,9 @@
             jax.ShapeDtypeStruct((VIEWS, 8, rows), f32),
         ],
         scratch_shapes=[pltpu.VMEM((2, 2 * STATE, width), bf16)],
-    )(lax.axis_index("ctx").reshape(1), everything, coef, pos, local)
-
-    square_total = lax.psum(squares[:, 0, :], "fsdp")
+    )(forward_in, reverse_in, coef, pos, local)
+
+    square_total = jnp.sum(lax.all_gather(squares[:, 0, :], "fsdp"), axis=0)
     scaling = lax.rsqrt(square_total / inner + 1e-05)
     normed = (mixed * scaling[:, :, None] * gain[None]).astype(bf16)
     outgoing = normed.reshape(VIEWS, shards, row_count, width).transpose(1, 0, 2, 3)
@@ -441,7 +459,7 @@
             out_specs=fixed(width, D),
             out_shape=jax.ShapeDtypeStruct((width, D), f32),
         )(normed, grads_all, head_weight)
-        grad_out = lax.psum_scatter(grad_rows, "ctx", scatter_dimension=0, tiled=True)
+        grad_out = scatter_sum(grad_rows, "ctx", ctx_count)
     else:
         grad_hidden = lax.dot_general(
             grads, head_weight, (((2,), (1,)), ((), ())), preferred_element_type=f32
@@ -453,7 +471,7 @@
         grad_out = lax.psum_scatter(
             grad_rows.reshape(inner, D), ("ctx", "fsdp"), scatter_dimension=0, tiled=True
         )
-    grad_head = lax.psum_scatter(head_term, ("ctx", "fsdp"), scatter_dimension=0, tiled=True)
+    grad_head = scatter_sum(head_term, ("ctx", "fsdp"), ctx_count * shards)
     return (grad_out, grad_head, losses[:, 0])
 
 

time: 334 us -> 249 us (0.75)
  waiting for transfers between devices: 176 us -> 79.5 us
  starting transfers between devices: 3.81 us -> 33.9 us
  local copies, waits for them, and re-layouts: 31.8 us -> 21.7 us
  Pallas kernels: 68.9 us -> 60.6 us
    all_gather x2 -> x0, waiting for transfers between devices: 70.7 us -> none  [the longest x1 43.1 us: on_device(): everything = lax.all_gather(final, 'ctx')]
    reduce_scatter x2 -> x0, waiting for transfers between devices: 65.1 us -> none  [the longest x1 36.1 us: on_device(): lax.psum_scatter(head_term, ('ctx', 'fsdp'), scatter_dimension=0, tiled=T...]
    all_to_all x0 -> x3, waiting for transfers between devices: none -> 25.3 us  [the longest x2 24.9 us: scatter_sum(): lax.all_to_all(blocks, axes, split_axis=0, concat_axis=0)]
    ppermute x0 -> x6, starting transfers between devices: none -> 16.7 us  [carried_in(): got = lax.ppermute(sent, axis, hops)]
    all_to_all x0 -> x3, starting transfers between devices: none -> 13.4 us  [the longest x2 9.2 us: scatter_sum(): lax.all_to_all(blocks, axes, split_axis=0, concat_axis=0)]
    psum x1 -> x0, blocking collectives: 11.4 us -> none  [on_device(): square_total = lax.psum(squares[:, 0, :], 'fsdp')]
    ppermute x0 -> x6, waiting for transfers between devices: none -> 9.79 us  [carried_in(): got = lax.ppermute(sent, axis, hops)]
    pallas_call x1, Pallas kernels: 25.9 us -> 16.9 us  [on_device(): call(functools.partial(states_kernel, heads), 'states', VIEWS * rows * ST...]
  transfers between devices with their start and end apart: 7 -> 12, of which waited for: 6 -> 6; matrix products, arithmetic and copies ran while one was open for 5% -> 13% of each run, Pallas kernels for 12% -> 23%
where the time goes in v2:
time: 249 us; the launch traced here: 247 us
  waiting for transfers between devices  79.5 us (32%)
  Pallas kernels  60.6 us (24%)
  starting transfers between devices  33.9 us (14%)
  local copies, waits for them, and re-layouts  21.7 us (9%)
  blocking collectives  17.6 us (7%)
  between operations  14.4 us (6%)
  other arithmetic  10.9 us (4%)
  matrix products  8.73 us (4%)
    all_gather x1, waiting for transfers between devices, on_device(): patches_all = lax.all_gather(patches, 'fsdp', axis=0, tiled=True)  27.1 us
    all_to_all x2, waiting for transfers between devices, scatter_sum(): lax.all_to_all(blocks, axes, split_axis=0, concat_axis=0)  24.9 us
    pallas_call x3, Pallas kernels, on_device(): call(functools.partial(inside_kernel, heads), 'inside', rows * D * 8192,...  23.3 us
    pallas_call x1, Pallas kernels, on_device(): call(functools.partial(states_kernel, heads), 'states', VIEWS * rows * ST...  16.9 us
    ppermute x6, starting transfers between devices, carried_in(): got = lax.ppermute(sent, axis, hops)  16.7 us
    all_to_all x1, waiting for transfers between devices, on_device(): arrived = lax.all_to_all(outgoing, 'fsdp', split_axis=0, concat_axis=0)  15.9 us
    all_gather x1, blocking collectives, on_device(): grads_all = lax.all_gather(grads, 'fsdp')  12.4 us
    ppermute x6, waiting for transfers between devices, carried_in(): got = lax.ppermute(sent, axis, hops)  9.79 us
  transfers between devices with their start and end apart: 12, of which 6 were waited for; matrix products, arithmetic and copies ran while one was open for 13% of the time, Pallas kernels for 23%

profile of v2, /device:TPU:0, one launch (start us, length us, event | category | flops | bytes accessed | tf_op | source)
XLA Modules:
  0.0 247.3 jit_solution(11702003129108078377)
XLA Ops:
  7.2 0.7 all-gather.5.cloned.1.call-update
  7.9 1.1 slice.44
  9.0 0.7 reshape.68
  9.7 0.2 copy.46
  9.9 0.2 copy.56
  10.2 0.2 copy.47
  10.6 1.6 maximum_maximum_fusion
  12.3 4.2 %all-to-all-start = ((bf16[4,256,896]{2,1,0:T(8,128)(2,1)}), bf16[4,256,896]{2,1,0:T(8,128)(2,1)S(1)}, u32[]{:S(2)}, u32[]{:S(2)}) async-start(bf16[4,256,896]{2,1,0:T(8,128)(2,1)} %maximum_maximum_fusion), calls=%async_computation | async-start | bytes 3670016 | tf_op jit(solution)/shard_map/all_to_all | solution.py:338
  16.5 0.7 all-gather.7.cloned.1.call-update
  17.2 0.1 slice_reduce_fusion
  17.4 0.1 copy.43
  17.5 0.1 copy.42
  17.9 0.2 dynamic-slice_reduce_fusion.3
  18.1 0.1 broadcast_in_dim_reshape.4.skip_ref
  18.3 0.1 mul.101
  18.4 0.2 fusion.5
  18.6 0.1 fusion.4
  18.7 0.2 fusion.3
  18.9 0.2 dynamic-slice_reduce_fusion
  19.1 27.1 %all-gather.5.cloned.1.call-done = bf16[1024,1024]{1,0:T(8,128)(2,1)} async-done(((bf16[256,1024]{1,0:T(8,128)(2,1)}), bf16[1024,1024]{1,0:T(8,128)(2,1)}) %all-gather.5.cloned.1.call-update) | async-done | bytes 2097168 | tf_op jit(solution)/shard_map/all_gather | solution.py:323
  46.3 4.0 %convert_element_type.21 = f32[1024,1024]{1,0:T(8,128)} convert(bf16[1024,1024]{1,0:T(8,128)(2,1)} %all-gather.5.cloned.1.call-done) | non-fusion elementwise | flops 1048576 | bytes 6291456 | tf_op jit(solution)/shard_map/convert_element_type | solution.py:342
  50.3 0.3 all-to-all-done
  50.6 8.6 %fusion.7 = (bf16[3,1024,896]{2,1,0:T(8,128)(2,1)S(1)}, f32[3,1024,896]{2,1,0:T(8,128)S(1)}) fusion(bf16[1024,896,1]{1,0,2:T(8,128)(2,1)S(1)} %bitcast.55, f32[1024,1024]{1,0:T(8,128)} %convert_element_type.21, f32[3,1024]{1,0:T(4,128)S(1)} %concatenate.6.scale_ref), kind=kOutput, calls=%fused_computation.34 | convolution fusion | flops 5646188544 | bytes 22556672 | tf_op jit(solution)/shard_map/dot_general | solution.py:57
  59.2 1.3 slice.56.x_ref
  60.4 2.0 slice.57.coef_ref
  62.4 1.3 slice.55.raw_ref
  63.7 16.9 %states.1 = (f32[3,2,136,256]{3,2,1,0:T(8,128)S(1)}, bf16[3,2,8,256,256]{4,3,2,1,0:T(8,128)(2,1)}, f32[3,1024,128]{2,1,0:T(8,128)S(1)}, f32[3,1024,128]{2,1,0:T(8,128)S(1)}, f32[3,1024,128]{2,1,0:T(8,128)S(1)}) custom-call(f32[3,1024,128]{2,1,0:T(8,128)} %slice.55.raw_ref, bf16[3,1024,256]{2,1,0:T(8,128)(2,1)} %slice.56.x_ref, ...), custom_call_target="tpu_custom_call" | custom-call | flops 805306368 | bytes 25165824 | tf_op jit(solution)/shard_map/states/pallas_call | solution.py:362
  80.7 1.3 collective-permute-start.3
  82.0 4.9 %collective-permute-start = (f32[3,128,256]{2,1,0:T(8,128)S(1)}, f32[3,128,256]{2,1,0:T(8,128)S(1)}, u32[]{:S(2)}, u32[]{:S(2)}) collective-permute-start(f32[3,128,256]{2,1,0:T(8,128)S(1)} %get-tuple-element.28), channel_id=1, source_target_pairs={{0,4},{4,8},{8,12},{1,5},{5,9},{9,13},{2,6},{6,10},{10,14},{3,7},{... | collective-permute-start | bytes 1179656 | tf_op jit(solution)/shard_map/ppermute | solution.py:287
  87.0 6.9 %collective-permute-done.3 = f32[3,128,256]{2,1,0:T(8,128)S(1)} collective-permute-done((f32[3,128,256]{2,1,0:T(8,128)S(1)}, f32[3,128,256]{2,1,0:T(8,128)S(1)}, u32[]{:S(2)}, u32[]{:S(2)}) %collective-permute-start.3) | collective-permute-done | bytes 393248 | tf_op jit(solution)/shard_map/ppermute | solution.py:287
  93.9 1.3 collective-permute-start.4
  95.2 7.8 %inside.3.rest_0_ = f32[3,1024,256]{2,1,0:T(8,128)} custom-call(bf16[3,1024,256]{2,1,0:T(8,128)(2,1)S(1)} %copy-done.2, bf16[3,1024,512]{2,1,0:T(8,128)(2,1)} %slice.57.coef_ref, bf16[3,2,8,256,256]{4,3,2,1,0:T(8,128)(2,1)} %get-tuple-element.15.prefix_ref, f32[3,1024,128]{2,1,0:T(8,128)S(1)} %get-tuple-element.16.steps_ref, ...), custom_call_target="tpu_custom_call" | custom-call | flops 8589934592 | bytes 8388608 | tf_op jit(solution)/shard_map/inside/pallas_call | solution.py:387
  103.0 2.9 %collective-permute-done.4 = f32[3,128,256]{2,1,0:T(8,128)S(1)} collective-permute-done((f32[3,128,256]{2,1,0:T(8,128)S(1)}, f32[3,128,256]{2,1,0:T(8,128)S(1)}, u32[]{:S(2)}, u32[]{:S(2)}) %collective-permute-start.4) | collective-permute-done | bytes 393248 | tf_op jit(solution)/shard_map/ppermute | solution.py:287
  105.9 0.1 multiply_add_fusion
  106.0 3.3 %collective-permute-start.1 = (f32[3,128,256]{2,1,0:T(8,128)S(1)}, f32[3,128,256]{2,1,0:T(8,128)S(1)}, u32[]{:S(2)}, u32[]{:S(2)}) collective-permute-start(f32[3,128,256]{2,1,0:T(8,128)S(1)} %get-tuple-element.26), channel_id=1, source_target_pairs={{0,4},{4,8},{8,12},{1,5},{5,9},{9,13},{2,6},{6,10},{10,14},{3,7},{... | collective-permute-start | bytes 1179656 | tf_op jit(solution)/shard_map/ppermute | solution.py:287
  109.4 7.8 %inside.4.rest_0_ = f32[3,1024,256]{2,1,0:T(8,128)} custom-call(bf16[3,1024,256]{2,1,0:T(8,128)(2,1)S(1)} %copy-done.2, bf16[3,1024,512]{2,1,0:T(8,128)(2,1)} %slice.57.coef_ref, bf16[3,2,8,256,256]{4,3,2,1,0:T(8,128)(2,1)} %get-tuple-element.15.prefix_ref, f32[3,1024,128]{2,1,0:T(8,128)S(1)} %get-tuple-element.16.steps_ref, ...), custom_call_target="tpu_custom_call", output_to_operand_aliasing={{}: (6, {})} | custom-call | flops 8589934592 | bytes 8388608 | tf_op jit(solution)/shard_map/inside/pallas_call | solution.py:387
  117.1 1.3 collective-permute-start.5
  118.5 4.6 %collective-permute-start.2 = (f32[3,128,256]{2,1,0:T(8,128)S(1)}, f32[3,128,256]{2,1,0:T(8,128)S(1)}, u32[]{:S(2)}, u32[]{:S(2)}) collective-permute-start(f32[3,128,256]{2,1,0:T(8,128)S(1)} %multiply_add_fusion.2), channel_id=1, source_target_pairs={{0,4},{4,8},{8,12},{1,5},{5,9},{9,13},{2,6},{6,10},{10,14},{3,7},{... | collective-permute-start | bytes 1179656 | tf_op jit(solution)/shard_map/ppermute | solution.py:287
  123.1 7.8 %inside.5.local_ref = f32[3,1024,256]{2,1,0:T(8,128)} custom-call(bf16[3,1024,256]{2,1,0:T(8,128)(2,1)S(1)} %copy-done.2, bf16[3,1024,512]{2,1,0:T(8,128)(2,1)} %slice.57.coef_ref, bf16[3,2,8,256,256]{4,3,2,1,0:T(8,128)(2,1)} %get-tuple-element.15.prefix_ref, f32[3,1024,128]{2,1,0:T(8,128)S(1)} %get-tuple-element.16.steps_ref, ...), custom_call_target="tpu_custom_call", output_to_operand_aliasing={{}: (6, {})} | custom-call | flops 8589934592 | bytes 8388608 | tf_op jit(solution)/shard_map/inside/pallas_call | solution.py:387
  130.8 7.6 %incoming.1 = (f32[3,1024,256]{2,1,0:T(8,128)S(1)}, f32[3,8,1024]{2,1,0:T(8,128)S(1)}) custom-call(f32[3,128,256]{2,1,0:T(8,128)S(1)} %collective-permute-done.2.forward_ref, f32[3,128,256]{2,1,0:T(8,128)S(1)} %collective-permute-done.5.reverse_ref, bf16[3,1024,512]{2,1,0:T(8,128)(2,1)} %slice.57.coef_ref, f32[3,1024,128]{2,1,0:T(8,128)S(1)} %get-tuple-element.14.pos_ref, ...), custom_call_target="tpu_custom_call" | custom-call | flops 805306368 | bytes 25165824 | tf_op jit(solution)/shard_map/incoming/pallas_call | solution.py:404
  138.5 1.7 copy-done.3
  140.1 5.2 %all-gather = f32[12,1,1024]{2,1,0:T(1,128)S(1)} all-gather(f32[3,1,1024]{2,1,0:T(1,128)S(1)} %slice.54), channel_id=2, replica_groups=mesh['groups'=2,'ctx'=4,'fsdp'=4] {'fsdp'}, dimensions={0}, use_global_device_ids=true | all-gather | bytes 61440 | tf_op jit(solution)/shard_map/all_gather | solution.py:419
  145.3 0.1 reduce.5
  145.5 2.4 multiply_convert_fusion.2.normed_ref
  147.9 1.3 copy.68
  149.2 3.7 %all-to-all-start.1 = ((bf16[4,3,256,256]{3,2,1,0:T(8,128)(2,1)}), bf16[4,3,256,256]{3,2,1,0:T(8,128)(2,1)S(1)}, u32[]{:S(2)}, u32[]{:S(2)}) async-start(bf16[4,3,256,256]{3,2,1,0:T(8,128)(2,1)} %bitcast.51), calls=%async_computation.1 | async-start | bytes 3145728 | tf_op jit(solution)/shard_map/all_to_all | solution.py:423
  152.9 0.8 copy.52.label_ref
  153.8 3.2 %copy.51 = bf16[4,4,64,1024]{3,2,0,1:T(8,128)(2,1)} copy(bf16[4,4,64,1024]{3,2,1,0:T(8,128)(2,1)} %bitcast.52) | data formatting | bytes 4194304 | tf_op jit(solution)/shard_map/reshape | solution.py:425
  156.9 15.9 %all-to-all-done.1.normed_ref = bf16[4,3,256,256]{3,2,1,0:T(8,128)(2,1)S(1)} async-done(((bf16[4,3,256,256]{3,2,1,0:T(8,128)(2,1)}), bf16[4,3,256,256]{3,2,1,0:T(8,128)(2,1)S(1)}, u32[]{:S(2)}, u32[]{:S(2)}) %all-to-all-start.1) | async-done | bytes 1572896 | tf_op jit(solution)/shard_map/all_to_all | solution.py:423
  172.8 1.6 copy-done.4
  174.4 1.0 copy-done.5
  175.4 0.9 copy-done.7
  176.3 0.9 copy-done.8
  177.3 4.5 %tail.1 = (bf16[3,256,128]{2,1,0:T(8,128)(2,1)S(1)}, f32[256,1]{1,0:T(8,128)S(1)}, f32[1024,128]{1,0:T(8,128)S(1)}) custom-call(bf16[4,3,256,256]{3,2,1,0:T(8,128)(2,1)S(1)} %all-to-all-done.1.normed_ref, bf16[4,256,1024]{2,1,0:T(8,128)(2,1)S(1)} %bitcast.48, bf16[1024,128]{1,0:T(8,128)(2,1)S(1)} %copy-done.8, bf16[256,1024]{1,0:T(8,128)(2,1)S(1)} %copy-done.5, ...), custom_call_target="tpu_custom_call" | custom-call | flops 2359296000 | bytes 6291456 | tf_op jit(solution)/shard_map/tail/pallas_call | solution.py:428
  181.8 0.8 copy-done.6
  182.7 3.6 %all-to-all-start.3 = ((f32[16,64,128]{2,1,0:T(8,128)}), f32[16,64,128]{2,1,0:T(8,128)S(1)}, u32[]{:S(2)}, u32[]{:S(2)}) async-start(f32[16,64,128]{2,1,0:T(8,128)} %bitcast.50), calls=%async_computation.3 | async-start | bytes 1048576 | tf_op jit(solution)/shard_map/all_to_all | solution.py:294
  186.2 12.4 %all-gather.1 = bf16[12,256,128]{2,1,0:T(8,128)(2,1)S(1)} all-gather(bf16[3,256,128]{2,1,0:T(8,128)(2,1)S(1)} %get-tuple-element.20), channel_id=3, replica_groups=mesh['groups'=2,'ctx'=4,'fsdp'=4] {'fsdp'}, dimensions={0}, use_global_device_ids=true | all-gather | bytes 983040 | tf_op jit(solution)/shard_map/all_gather | solution.py:450
  198.6 0.9 copy-done.9
  199.6 8.2 %grads.1 = f32[256,1024]{1,0:T(8,128)} custom-call(bf16[3,1024,256]{2,1,0:T(8,128)(2,1)S(1)} %multiply_convert_fusion.2.normed_ref, bf16[4,3,256,128]{3,2,1,0:T(8,128)(2,1)S(1)} %bitcast.49, bf16[1024,128]{1,0:T(8,128)(2,1)S(1)} %copy-done.9), custom_call_target="tpu_custom_call" | custom-call | flops 2415919104 | bytes 8388608 | tf_op jit(solution)/shard_map/grads/pallas_call | solution.py:451
  207.8 5.6 %all-to-all-start.2 = ((f32[4,64,1024]{2,1,0:T(8,128)}), f32[4,64,1024]{2,1,0:T(8,128)S(1)}, u32[]{:S(2)}, u32[]{:S(2)}) async-start(f32[4,64,1024]{2,1,0:T(8,128)} %bitcast.17), calls=%async_computation.2 | async-start | bytes 2097152 | tf_op jit(solution)/shard_map/all_to_all | solution.py:294
  213.4 0.7 reduce.7
  214.1 0.6 reduce_sum.49
  214.8 24.9 %all-to-all-done.2 = f32[4,64,1024]{2,1,0:T(8,128)S(1)} async-done(((f32[4,64,1024]{2,1,0:T(8,128)}), f32[4,64,1024]{2,1,0:T(8,128)S(1)}, u32[]{:S(2)}, u32[]{:S(2)}) %all-to-all-start.2) | async-done | bytes 1048608 | tf_op jit(solution)/shard_map/all_to_all | solution.py:294
  239.7 0.8 reduce_sum.48
  (64 shorter events, 1.1 us)
Async XLA Ops:
  7.2 11.5 %copy-start = (f32[9,1024]{1,0:T(8,128)S(1)}, f32[9,1024]{1,0:T(8,128)}, u32[]{:S(2)}) copy-start(f32[9,1024]{1,0:T(8,128)} %param.17) | copy-start | bytes 110596
  7.2 3.3 %slice-start = ((bf16[256,1536]{1,0:T(8,128)(2,1)}), bf16[256,512]{1,0:T(8,128)(2,1)S(1)}, s32[]{:S(2)}) async-start(bf16[256,1536]{1,0:T(8,128)(2,1)} %param.18), calls=%async_computation.6 | async-start | bytes 524288 | tf_op jit(solution)/shard_map/slice | solution.py:332
  7.2 39.1 %all-gather.5.cloned.1.call-start = ((), (), s32[]{:S(2)}) async-start(), calls=%async_computation.4 | async-start | bytes 2621440 | tf_op jit(solution)/shard_map/all_gather | solution.py:323
  10.6 6.6 %copy-start.14 = (s32[2,4]{1,0:T(2,128)S(1)}, s32[2,4]{1,0:T(2,128)}, u32[]{:S(2)}) copy-start(s32[2,4]{1,0:T(2,128)} %param.16) | copy-start | bytes 100
  10.6 6.9 %copy-start.12 = (s32[2,3]{1,0:T(2,128)S(1)}, s32[2,3]{1,0:T(2,128)}, u32[]{:S(2)}) copy-start(s32[2,3]{1,0:T(2,128)} %param.15) | copy-start | bytes 76
  10.6 7.0 %copy-start.15 = (f32[2,16]{1,0:T(2,128)S(1)}, f32[2,16]{1,0:T(2,128)}, u32[]{:S(2)}) copy-start(f32[2,16]{1,0:T(2,128)} %param.21) | copy-start | bytes 388
  10.6 7.1 %copy-start.13 = (f32[2,16]{1,0:T(2,128)S(1)}, f32[2,16]{1,0:T(2,128)}, u32[]{:S(2)}) copy-start(f32[2,16]{1,0:T(2,128)} %param.20) | copy-start | bytes 388
  10.6 7.2 %copy-start.16 = (f32[16]{0:T(128)S(1)}, f32[16]{0:T(128)}, u32[]{:S(2)}) copy-start(f32[16]{0:T(128)} %param.22) | copy-start | bytes 196
  10.6 7.6 %copy-start.10 = (f32[1024]{0:T(1024)S(1)}, f32[1024]{0:T(1024)}, u32[]{:S(2)}) copy-start(f32[1024]{0:T(1024)} %param.23) | copy-start | bytes 12292
  12.3 38.3 %all-to-all-start = ((bf16[4,256,896]{2,1,0:T(8,128)(2,1)}), bf16[4,256,896]{2,1,0:T(8,128)(2,1)S(1)}, u32[]{:S(2)}, u32[]{:S(2)}) async-start(bf16[4,256,896]{2,1,0:T(8,128)(2,1)} %maximum_maximum_fusion), calls=%async_computation | async-start | bytes 3670016 | tf_op jit(solution)/shard_map/all_to_all | solution.py:338
  16.5 137.3 %all-gather.7.cloned.1.call-start = ((), (), s32[]{:S(2)}) async-start(), calls=%async_computation.5 | async-start | bytes 2621440 | tf_op jit(solution)/shard_map/all_gather | solution.py:340
  63.7 31.5 %copy-start.2 = (bf16[3,1024,256]{2,1,0:T(8,128)(2,1)S(1)}, bf16[3,1024,256]{2,1,0:T(8,128)(2,1)}, u32[]{:S(2)}) copy-start(bf16[3,1024,256]{2,1,0:T(8,128)(2,1)} %slice.56.x_ref) | copy-start | bytes 4718596
  80.7 13.2 %collective-permute-start.3 = (f32[3,128,256]{2,1,0:T(8,128)S(1)}, f32[3,128,256]{2,1,0:T(8,128)S(1)}, u32[]{:S(2)}, u32[]{:S(2)}) collective-permute-start(f32[3,128,256]{2,1,0:T(8,128)S(1)} %get-tuple-element.27), channel_id=1, source_target_pairs={{4,0},{8,4},{12,8},{5,1},{9,5},{13,9},{6,2},{10,6},{14,10},{7,3},{... | collective-permute-start | bytes 1179656 | tf_op jit(solution)/shard_map/ppermute | solution.py:287
  82.0 21.0 %collective-permute-start = (f32[3,128,256]{2,1,0:T(8,128)S(1)}, f32[3,128,256]{2,1,0:T(8,128)S(1)}, u32[]{:S(2)}, u32[]{:S(2)}) collective-permute-start(f32[3,128,256]{2,1,0:T(8,128)S(1)} %get-tuple-element.28), channel_id=1, source_target_pairs={{0,4},{4,8},{8,12},{1,5},{5,9},{9,13},{2,6},{6,10},{10,14},{3,7},{... | collective-permute-start | bytes 1179656 | tf_op jit(solution)/shard_map/ppermute | solution.py:287
  93.9 12.0 %collective-permute-start.4 = (f32[3,128,256]{2,1,0:T(8,128)S(1)}, f32[3,128,256]{2,1,0:T(8,128)S(1)}, u32[]{:S(2)}, u32[]{:S(2)}) collective-permute-start(f32[3,128,256]{2,1,0:T(8,128)S(1)} %multiply_add_fusion.1), channel_id=1, source_target_pairs={{4,0},{8,4},{12,8},{5,1},{9,5},{13,9},{6,2},{10,6},{14,10},{7,3},{... | collective-permute-start | bytes 1179656 | tf_op jit(solution)/shard_map/ppermute | solution.py:287
  106.0 12.4 %collective-permute-start.1 = (f32[3,128,256]{2,1,0:T(8,128)S(1)}, f32[3,128,256]{2,1,0:T(8,128)S(1)}, u32[]{:S(2)}, u32[]{:S(2)}) collective-permute-start(f32[3,128,256]{2,1,0:T(8,128)S(1)} %get-tuple-element.26), channel_id=1, source_target_pairs={{0,4},{4,8},{8,12},{1,5},{5,9},{9,13},{2,6},{6,10},{10,14},{3,7},{... | collective-permute-start | bytes 1179656 | tf_op jit(solution)/shard_map/ppermute | solution.py:287
  117.1 13.7 %collective-permute-start.5 = (f32[3,128,256]{2,1,0:T(8,128)S(1)}, f32[3,128,256]{2,1,0:T(8,128)S(1)}, u32[]{:S(2)}, u32[]{:S(2)}) collective-permute-start(f32[3,128,256]{2,1,0:T(8,128)S(1)} %get-tuple-element.25), channel_id=1, source_target_pairs={{4,0},{8,4},{12,8},{5,1},{9,5},{13,9},{6,2},{10,6},{14,10},{7,3},{... | collective-permute-start | bytes 1179656 | tf_op jit(solution)/shard_map/ppermute | solution.py:287
  118.5 12.3 %collective-permute-start.2 = (f32[3,128,256]{2,1,0:T(8,128)S(1)}, f32[3,128,256]{2,1,0:T(8,128)S(1)}, u32[]{:S(2)}, u32[]{:S(2)}) collective-permute-start(f32[3,128,256]{2,1,0:T(8,128)S(1)} %multiply_add_fusion.2), channel_id=1, source_target_pairs={{0,4},{4,8},{8,12},{1,5},{5,9},{9,13},{2,6},{6,10},{10,14},{3,7},{... | collective-permute-start | bytes 1179656 | tf_op jit(solution)/shard_map/ppermute | solution.py:287
  138.5 1.7 copy-start.3
  147.9 5.0 %copy-start.11 = (s32[256]{0:T(256)S(1)}, s32[256]{0:T(256)}, u32[]{:S(2)}) copy-start(s32[256]{0:T(256)} %param.14) | copy-start | bytes 3076
  149.2 23.6 %all-to-all-start.1 = ((bf16[4,3,256,256]{3,2,1,0:T(8,128)(2,1)}), bf16[4,3,256,256]{3,2,1,0:T(8,128)(2,1)S(1)}, u32[]{:S(2)}, u32[]{:S(2)}) async-start(bf16[4,3,256,256]{3,2,1,0:T(8,128)(2,1)} %bitcast.51), calls=%async_computation.1 | async-start | bytes 3145728 | tf_op jit(solution)/shard_map/all_to_all | solution.py:423
  172.8 1.6 copy-start.4
  174.4 1.0 copy-start.5
  175.4 0.9 copy-start.7
  176.3 0.9 copy-start.8
  181.8 0.8 copy-start.6
  182.7 25.1 %all-to-all-start.3 = ((f32[16,64,128]{2,1,0:T(8,128)}), f32[16,64,128]{2,1,0:T(8,128)S(1)}, u32[]{:S(2)}, u32[]{:S(2)}) async-start(f32[16,64,128]{2,1,0:T(8,128)} %bitcast.50), calls=%async_computation.3 | async-start | bytes 1048576 | tf_op jit(solution)/shard_map/all_to_all | solution.py:294
  198.6 0.9 copy-start.9
  199.6 40.9 %copy-start.1 = (f32[9,1024]{1,0:T(8,128)S(1)}, f32[9,1024]{1,0:T(8,128)}, u32[]{:S(2)}) copy-start(f32[9,1024]{1,0:T(8,128)} %param.17) | copy-start | bytes 110596
  207.8 31.9 %all-to-all-start.2 = ((f32[4,64,1024]{2,1,0:T(8,128)}), f32[4,64,1024]{2,1,0:T(8,128)S(1)}, u32[]{:S(2)}, u32[]{:S(2)}) async-start(f32[4,64,1024]{2,1,0:T(8,128)} %bitcast.17), calls=%async_computation.2 | async-start | bytes 2097152 | tf_op jit(solution)/shard_map/all_to_all | solution.py:294
Sparse Core Ops, SparseCore 0:
  9.6 36.6 all-gather.4
  47.8 22.5 all-gather.6

commit v3 on v2

--- a/solution.py
+++ b/solution.py
@@ -66,6 +66,17 @@
         right = jnp.broadcast_to(columns[:, h + 1 : h + 2], (rows, LANES))
         pieces.append(jnp.where(lane < HEAD_DIM, left, right))
     return jnp.concatenate(pieces, axis=1) if len(pieces) > 1 else pieces[0]
+
+
+def project_kernel(place_ref, patches_ref, scale_ref, weight_ref, x_ref, coef_ref, raw_ref):
+    width = x_ref.shape[2]
+    patches = patches_ref[...].astype(f32)
+    for v in range(VIEWS):
+        view = (scale_ref[v : v + 1, :] * patches).astype(bf16)
+        out = dot(view, weight_ref[...])
+        x_ref[v] = out[:, :width].astype(bf16)
+        coef_ref[v] = out[:, width : width + 4 * STATE].astype(bf16)
+        raw_ref[v] = out[:, width + 4 * STATE :]
 
 
 def states_kernel(heads, raw_ref, x_ref, coef_ref, bias_ref, rate_ref,
@@ -320,7 +331,15 @@
     rows = row_count * shards
     pieces = rows // BLOCK
 
-    patches_all = lax.all_gather(patches, "fsdp", axis=0, tiled=True)
+    if shards == 4:
+        across = lax.ppermute(patches, "fsdp", [(f, f ^ 2) for f in range(shards)])
+        beside = lax.ppermute(patches, "fsdp", [(f, f ^ 1) for f in range(shards)])
+        corner = lax.ppermute(across, "fsdp", [(f, f ^ 1) for f in range(shards)])
+        patches_all = jnp.concatenate([patches, beside, across, corner], axis=0)
+        flip = place
+    else:
+        patches_all = lax.all_gather(patches, "fsdp", axis=0, tiled=True)
+        flip = jnp.zeros_like(place)
     columns_in = inner + 4 * STATE
     depth = in_weight.shape[0]
     sent_weight = jnp.concatenate(
@@ -337,14 +356,30 @@
     )
     mine_weight = lax.all_to_all(sent_weight, "fsdp", split_axis=0, concat_axis=0)
     mine_weight = mine_weight.reshape(D, width + 5 * STATE)
-    out_all = lax.all_gather(out_weight, "fsdp", axis=0, tiled=True)
     scales = view_scales(op_ids, mix_codes, aug_gains)
-    views = (scales[:, None, :] * patches_all.astype(f32)[None]).astype(bf16)
-    projected = dot(views.reshape(VIEWS * rows, D), mine_weight)
-    projected = projected.reshape(VIEWS, rows, width + 5 * STATE)
-    x = projected[:, :, :width].astype(bf16)
-    coef = projected[:, :, width : width + 4 * STATE].astype(bf16)
-    raw = projected[:, :, width + 4 * STATE :]
+    tile = min(row_count, 128)
+    per = row_count // tile
+    placed = lambda s, i, flip_ref: ((s ^ flip_ref[0]) * per + i, 0)
+    piece = lambda lanes: pl.BlockSpec((VIEWS, tile, lanes), lambda s, i, _: (0, s * per + i, 0))
+    constant = lambda *dims: pl.BlockSpec(dims, lambda *_: (0,) * len(dims))
+    x, coef, raw = call(
+        project_kernel, "project",
+        VIEWS * rows * D * (width + 5 * STATE) * 2, rows * D * 8,
+        grid_spec=pltpu.PrefetchScalarGridSpec(
+            num_scalar_prefetch=1,
+            grid=(shards, per),
+            in_specs=[pl.BlockSpec((tile, D), placed), constant(VIEWS, D),
+                      constant(D, width + 5 * STATE)],
+            out_specs=[piece(width), piece(4 * STATE), piece(LANES)],
+        ),
+        out_shape=[
+            jax.ShapeDtypeStruct((VIEWS, rows, width), bf16),
+            jax.ShapeDtypeStruct((VIEWS, rows, 4 * STATE), bf16),
+            jax.ShapeDtypeStruct((VIEWS, rows, LANES), f32),
+        ],
+    )(flip.reshape(1).astype(jnp.int32), patches_all, scales, mine_weight)
+    raw, out_later = lax.optimization_barrier((raw, out_weight))
+    out_all = lax.all_gather(out_later, "fsdp", axis=0, tiled=True)
 
     def local_lanes(values):
         picked = lax.dynamic_index_in_dim(values.reshape(2 * heads, shards), place, 1, False)
@@ -448,18 +483,23 @@
 
     if ctx_count * shards == HEADS:
         grads_all = lax.all_gather(grads, "fsdp")
-        grad_rows = call(
-            functools.partial(grad_kernel, shards), "grads",
-            VIEWS * rows * D * (width + CLASSES) * 2, 8 << 20,
-            grid=(VIEWS, shards),
-            in_specs=[
-                pl.BlockSpec((1, row_count, width), lambda v, s: (v, s, 0)),
-                pl.BlockSpec((1, 1, row_count, CLASSES), lambda v, s: (s, v, 0, 0)),
-                fixed(D, CLASSES)],
-            out_specs=fixed(width, D),
-            out_shape=jax.ShapeDtypeStruct((width, D), f32),
-        )(normed, grads_all, head_weight)
-        grad_out = scatter_sum(grad_rows, "ctx", ctx_count)
+        grads_all, head_term = lax.optimization_barrier((grads_all, head_term))
+        half = D // 2
+        sums = []
+        for k in range(2):
+            grad_rows = call(
+                functools.partial(grad_kernel, shards), "grads",
+                VIEWS * rows * D * (width + CLASSES) * 4, 8 << 20,
+                grid=(VIEWS, shards),
+                in_specs=[
+                    pl.BlockSpec((1, row_count, width), lambda v, s: (v, s, 0)),
+                    pl.BlockSpec((1, 1, row_count, CLASSES), lambda v, s: (s, v, 0, 0)),
+                    pl.BlockSpec((half, CLASSES), lambda v, s, k=k: (k, 0))],
+                out_specs=fixed(width, half),
+                out_shape=jax.ShapeDtypeStruct((width, half), f32),
+            )(normed, grads_all, head_weight)
+            sums.append(scatter_sum(grad_rows, "ctx", ctx_count))
+        grad_out = jnp.concatenate(sums, axis=1)
     else:
         grad_hidden = lax.dot_general(
             grads, head_weight, (((2,), (1,)), ((), ())), preferred_element_type=f32

time: 249 us -> 257 us (1.032)
  waiting for transfers between devices: 79.5 us -> 64.1 us
  Pallas kernels: 60.6 us -> 75.8 us
  blocking collectives: 17.6 us -> 30.1 us
  matrix products: 8.73 us -> 0.17 us
    all_gather x2 -> x1, waiting for transfers between devices: 27.1 us -> 0.02 us  [on_device(): out_all = lax.all_gather(out_later, 'fsdp', axis=0, tiled=True)]
    all_to_all x0 -> x1, blocking collectives: none -> 16.9 us  [scatter_sum(): lax.all_to_all(blocks, axes, split_axis=0, concat_axis=0)]
    all_to_all x1, waiting for transfers between devices: 0.33 us -> 14.4 us  [on_device(): lax.all_to_all(sent_weight, 'fsdp', split_axis=0, concat_axis=0)]
    pallas_call x0 -> x1, Pallas kernels: none -> 10.4 us  [on_device(): call(project_kernel, 'project', VIEWS * rows * D * (width + 5 * STATE) *...]
    dot_general x1 -> x0, matrix products: 8.56 us -> none  [dot(): return lax.dot_general(a, b, (dims, ((), ())), preferred_element_type=f32)]
    unnamed x38 -> x46, local copies, waits for them, and re-layouts: 8.27 us -> 14.6 us
    ppermute x0 -> x3, waiting for transfers between devices: none -> 4.98 us  [the longest x1 3.7 us: on_device(): across = lax.ppermute(patches, 'fsdp', [(f, f ^ 2) for f in range(shards)])]
    slice x3 -> x0, local copies, waits for them, and re-layouts: 4.54 us -> none  [the longest x1 2.01 us: on_device(): coef = projected[:, :, width:width + 4 * STATE].astype(bf16)]
  transfers between devices with their start and end apart: 12 -> 14, of which waited for: 6 -> 7; matrix products, arithmetic and copies ran while one was open for 13% -> 8% of each run, Pallas kernels for 23% -> 14%
where the time goes in v3:
time: 257 us; the launch traced here: 255 us
  Pallas kernels  75.8 us (29%)
  waiting for transfers between devices  64.1 us (25%)
  starting transfers between devices  35.4 us (14%)
  blocking collectives  30.1 us (12%)
  local copies, waits for them, and re-layouts  23.5 us (9%)
  between operations  14.5 us (6%)
  other arithmetic  11.5 us (4%)
    pallas_call x3, Pallas kernels, on_device(): call(functools.partial(inside_kernel, heads), 'inside', rows * D * 8192,...  23.3 us
    all_to_all x2, waiting for transfers between devices, scatter_sum(): lax.all_to_all(blocks, axes, split_axis=0, concat_axis=0)  21.5 us
    ppermute x6, starting transfers between devices, carried_in(): got = lax.ppermute(sent, axis, hops)  17.5 us
    all_to_all x1, blocking collectives, scatter_sum(): lax.all_to_all(blocks, axes, split_axis=0, concat_axis=0)  16.9 us
    pallas_call x1, Pallas kernels, on_device(): call(functools.partial(states_kernel, heads), 'states', VIEWS * rows * ST...  16.8 us
    all_to_all x1, waiting for transfers between devices, on_device(): arrived = lax.all_to_all(outgoing, 'fsdp', split_axis=0, concat_axis=0)  16.7 us
    unnamed x46, local copies, waits for them, and re-layouts  14.6 us
    all_to_all x1, waiting for transfers between devices, on_device(): lax.all_to_all(sent_weight, 'fsdp', split_axis=0, concat_axis=0)  14.4 us
  transfers between devices with their start and end apart: 14, of which 7 were waited for; matrix products, arithmetic and copies ran while one was open for 8% of the time, Pallas kernels for 14%

profile of v3, /device:TPU:0, one launch (start us, length us, event | category | flops | bytes accessed | tf_op | source)
XLA Modules:
  0.0 255.1 jit_solution(1451477935347308181)
XLA Ops:
  7.2 3.0 %collective-permute-start.1 = (bf16[256,1024]{1,0:T(8,128)(2,1)}, bf16[256,1024]{1,0:T(8,128)(2,1)S(1)}, u32[]{:S(2)}, u32[]{:S(2)}) collective-permute-start(bf16[256,1024]{1,0:T(8,128)(2,1)} %patches_ref.1), channel_id=1, source_target_pairs={{0,2},{1,3},{2,0},{3,1},{4,6},{5,7},{6,4},{7,5},{8,10},{9,11},{10,... | collective-permute-start | bytes 1572872 | tf_op jit(solution)/shard_map/ppermute | solution.py:335
  10.2 1.1 slice.33
  11.3 0.7 reshape.68
  12.0 0.2 copy.46
  12.2 0.2 copy.56
  12.5 0.2 copy.47
  12.9 1.6 maximum_maximum_fusion
  14.5 3.6 %all-to-all-start = ((bf16[4,256,896]{2,1,0:T(8,128)(2,1)}), bf16[4,256,896]{2,1,0:T(8,128)(2,1)S(1)}, u32[]{:S(2)}, u32[]{:S(2)}) async-start(bf16[4,256,896]{2,1,0:T(8,128)(2,1)} %maximum_maximum_fusion), calls=%async_computation | async-start | bytes 3670016 | tf_op jit(solution)/shard_map/all_to_all | solution.py:357
  18.2 0.1 slice_reduce_fusion
  18.8 0.2 dynamic-slice_reduce_fusion.3
  19.5 3.7 %collective-permute-done.1 = bf16[256,1024]{1,0:T(8,128)(2,1)S(1)} collective-permute-done((bf16[256,1024]{1,0:T(8,128)(2,1)}, bf16[256,1024]{1,0:T(8,128)(2,1)S(1)}, u32[]{:S(2)}, u32[]{:S(2)}) %collective-permute-start.1) | collective-permute-done | bytes 524320 | tf_op jit(solution)/shard_map/ppermute | solution.py:335
  23.2 0.2 fusion.2
  23.4 0.2 fusion
  23.6 0.2 dynamic-slice_reduce_fusion
  23.8 1.3 collective-permute-done.2
  25.1 2.5 pad_maximum_fusion.patches_ref
  27.6 14.4 %all-to-all-done = bf16[4,256,896]{2,1,0:T(8,128)(2,1)S(1)} async-done(((bf16[4,256,896]{2,1,0:T(8,128)(2,1)}), bf16[4,256,896]{2,1,0:T(8,128)(2,1)S(1)}, u32[]{:S(2)}, u32[]{:S(2)}) %all-to-all-start) | async-done | bytes 1835040 | tf_op jit(solution)/shard_map/all_to_all | solution.py:357
  42.0 10.4 %project.1 = (bf16[3,1024,256]{2,1,0:T(8,128)(2,1)S(1)}, bf16[3,1024,512]{2,1,0:T(8,128)(2,1)}, f32[3,1024,128]{2,1,0:T(8,128)S(1)}) custom-call(s32[1]{0:T(128)} %bitcast.place_ref, bf16[1024,1024]{1,0:T(8,128)(2,1)} %pad_maximum_fusion.patches_ref, f32[3,1024]{1,0:T(4,128)S(1)} %concatenate.13.scale_ref, bf16[1024,896]{1,0:T(8,128)(2,1)S(1)} %bitcast.48), custom_call_target="tpu_custom_call" | custom-call | flops 5637144576 | bytes 8388608 | tf_op jit(solution)/shard_map/project/pallas_call | solution.py:365
  52.4 1.1 copy-done.3
  53.5 1.2 copy-done.5
  54.7 16.8 %states.1 = (f32[3,2,136,256]{3,2,1,0:T(8,128)S(1)}, bf16[3,2,8,256,256]{4,3,2,1,0:T(8,128)(2,1)}, f32[3,1024,128]{2,1,0:T(8,128)S(1)}, f32[3,1024,128]{2,1,0:T(8,128)S(1)}, f32[3,1024,128]{2,1,0:T(8,128)S(1)}) custom-call(f32[3,1024,128]{2,1,0:T(8,128)} %copy-done.5, bf16[3,1024,256]{2,1,0:T(8,128)(2,1)} %copy-done.3, ...), custom_call_target="tpu_custom_call" | custom-call | flops 805306368 | bytes 25165824 | tf_op jit(solution)/shard_map/states/pallas_call | solution.py:397
  71.5 1.2 copy-done.8
  72.7 1.2 copy-done.10
  73.8 0.8 slice_bitcast_fusion
  74.6 1.3 collective-permute-start.6
  76.0 4.6 %collective-permute-start.3 = (f32[3,128,256]{2,1,0:T(8,128)S(1)}, f32[3,128,256]{2,1,0:T(8,128)S(1)}, u32[]{:S(2)}, u32[]{:S(2)}) collective-permute-start(f32[3,128,256]{2,1,0:T(8,128)S(1)} %get-tuple-element.42), channel_id=1, source_target_pairs={{0,4},{4,8},{8,12},{1,5},{5,9},{9,13},{2,6},{6,10},{10,14},{3,7},{... | collective-permute-start | bytes 1179656 | tf_op jit(solution)/shard_map/ppermute | solution.py:298
  80.6 6.6 %collective-permute-done.6 = f32[3,128,256]{2,1,0:T(8,128)} collective-permute-done((f32[3,128,256]{2,1,0:T(8,128)}, f32[3,128,256]{2,1,0:T(8,128)}, u32[]{:S(2)}, u32[]{:S(2)}) %collective-permute-start.6) | collective-permute-done | bytes 393248 | tf_op jit(solution)/shard_map/ppermute | solution.py:298
  87.2 1.1 multiply_add_fusion.1
  88.2 1.3 collective-permute-start.7
  89.6 1.5 copy-done.4
  91.0 1.4 copy-done.9
  92.5 1.4 copy-done.11
  93.9 7.8 %inside.3.rest_0_ = f32[3,1024,256]{2,1,0:T(8,128)} custom-call(bf16[3,1024,256]{2,1,0:T(8,128)(2,1)S(1)} %copy-done.4, bf16[3,1024,512]{2,1,0:T(8,128)(2,1)} %get-tuple-element.23.coef_ref, bf16[3,2,8,256,256]{4,3,2,1,0:T(8,128)(2,1)} %get-tuple-element.26.prefix_ref, f32[3,1024,128]{2,1,0:T(8,128)S(1)} %copy-done.9, f32[3,1024,128]{2,1,0:T(8,128)S(1)} %copy-done.11, ...), custom_call_target="tpu_custom_call" | custom-call | flops 8589934592 | bytes 8388608 | tf_op jit(solution)/shard_map/inside/pallas_call | solution.py:422
  101.8 4.5 %collective-permute-start.4 = (f32[3,128,256]{2,1,0:T(8,128)S(1)}, f32[3,128,256]{2,1,0:T(8,128)S(1)}, u32[]{:S(2)}, u32[]{:S(2)}) collective-permute-start(f32[3,128,256]{2,1,0:T(8,128)S(1)} %get-tuple-element.40), channel_id=1, source_target_pairs={{0,4},{4,8},{8,12},{1,5},{5,9},{9,13},{2,6},{6,10},{10,14},{3,7},{... | collective-permute-start | bytes 1179656 | tf_op jit(solution)/shard_map/ppermute | solution.py:298
  106.3 7.8 %inside.4.rest_0_ = f32[3,1024,256]{2,1,0:T(8,128)} custom-call(bf16[3,1024,256]{2,1,0:T(8,128)(2,1)S(1)} %copy-done.4, bf16[3,1024,512]{2,1,0:T(8,128)(2,1)} %get-tuple-element.23.coef_ref, bf16[3,2,8,256,256]{4,3,2,1,0:T(8,128)(2,1)} %get-tuple-element.26.prefix_ref, f32[3,1024,128]{2,1,0:T(8,128)S(1)} %copy-done.9, ...), custom_call_target="tpu_custom_call", output_to_operand_aliasing={{}: (6, {})} | custom-call | flops 8589934592 | bytes 8388608 | tf_op jit(solution)/shard_map/inside/pallas_call | solution.py:422
  114.0 1.3 collective-permute-start.8
  115.4 4.6 %collective-permute-start.5 = (f32[3,128,256]{2,1,0:T(8,128)S(1)}, f32[3,128,256]{2,1,0:T(8,128)S(1)}, u32[]{:S(2)}, u32[]{:S(2)}) collective-permute-start(f32[3,128,256]{2,1,0:T(8,128)S(1)} %multiply_add_fusion.2), channel_id=1, source_target_pairs={{0,4},{4,8},{8,12},{1,5},{5,9},{9,13},{2,6},{6,10},{10,14},{3,7},{... | collective-permute-start | bytes 1179656 | tf_op jit(solution)/shard_map/ppermute | solution.py:298
  120.0 7.8 %inside.5.local_ref = f32[3,1024,256]{2,1,0:T(8,128)} custom-call(bf16[3,1024,256]{2,1,0:T(8,128)(2,1)S(1)} %copy-done.4, bf16[3,1024,512]{2,1,0:T(8,128)(2,1)} %get-tuple-element.23.coef_ref, bf16[3,2,8,256,256]{4,3,2,1,0:T(8,128)(2,1)} %get-tuple-element.26.prefix_ref, f32[3,1024,128]{2,1,0:T(8,128)S(1)} %copy-done.9, ...), custom_call_target="tpu_custom_call", output_to_operand_aliasing={{}: (6, {})} | custom-call | flops 8589934592 | bytes 8388608 | tf_op jit(solution)/shard_map/inside/pallas_call | solution.py:422
  127.8 7.6 %incoming.1 = (f32[3,1024,256]{2,1,0:T(8,128)S(1)}, f32[3,8,1024]{2,1,0:T(8,128)S(1)}) custom-call(f32[3,128,256]{2,1,0:T(8,128)S(1)} %collective-permute-done.5.forward_ref, f32[3,128,256]{2,1,0:T(8,128)S(1)} %collective-permute-done.8.reverse_ref, bf16[3,1024,512]{2,1,0:T(8,128)(2,1)} %get-tuple-element.23.coef_ref, ...), custom_call_target="tpu_custom_call" | custom-call | flops 805306368 | bytes 25165824 | tf_op jit(solution)/shard_map/incoming/pallas_call | solution.py:439
  135.4 1.6 copy-done.1
  137.1 5.2 %all-gather = f32[12,1,1024]{2,1,0:T(1,128)S(1)} all-gather(f32[3,1,1024]{2,1,0:T(1,128)S(1)} %slice.40), channel_id=2, replica_groups=mesh['groups'=2,'ctx'=4,'fsdp'=4] {'fsdp'}, dimensions={0}, use_global_device_ids=true | all-gather | bytes 61440 | tf_op jit(solution)/shard_map/all_gather | solution.py:454
  142.3 0.1 reduce.5
  142.5 2.4 multiply_convert_fusion.normed_ref
  144.9 1.3 copy.68
  146.2 3.6 %all-to-all-start.1 = ((bf16[4,3,256,256]{3,2,1,0:T(8,128)(2,1)}), bf16[4,3,256,256]{3,2,1,0:T(8,128)(2,1)S(1)}, u32[]{:S(2)}, u32[]{:S(2)}) async-start(bf16[4,3,256,256]{3,2,1,0:T(8,128)(2,1)} %bitcast.52), calls=%async_computation.1 | async-start | bytes 3145728 | tf_op jit(solution)/shard_map/all_to_all | solution.py:458
  149.7 0.1 copy.52.label_ref
  149.9 3.2 %copy.51 = bf16[4,4,64,1024]{3,2,0,1:T(8,128)(2,1)} copy(bf16[4,4,64,1024]{3,2,1,0:T(8,128)(2,1)} %bitcast.53) | data formatting | bytes 4194304 | tf_op jit(solution)/shard_map/reshape | solution.py:460
  153.1 16.7 %all-to-all-done.1.normed_ref = bf16[4,3,256,256]{3,2,1,0:T(8,128)(2,1)S(1)} async-done(((bf16[4,3,256,256]{3,2,1,0:T(8,128)(2,1)}), bf16[4,3,256,256]{3,2,1,0:T(8,128)(2,1)S(1)}, u32[]{:S(2)}, u32[]{:S(2)}) %all-to-all-start.1) | async-done | bytes 1572896 | tf_op jit(solution)/shard_map/all_to_all | solution.py:458
  169.8 1.6 copy-done.2
  171.4 1.0 copy-done.7
  172.4 0.9 copy-done.12
  173.4 5.3 %tail.1 = (bf16[3,256,128]{2,1,0:T(8,128)(2,1)S(1)}, f32[256,1]{1,0:T(8,128)S(1)}, f32[1024,128]{1,0:T(8,128)}) custom-call(bf16[4,3,256,256]{3,2,1,0:T(8,128)(2,1)S(1)} %all-to-all-done.1.normed_ref, bf16[4,256,1024]{2,1,0:T(8,128)(2,1)S(1)} %bitcast.47, bf16[1024,128]{1,0:T(8,128)(2,1)S(1)} %copy-done.12, bf16[256,1024]{1,0:T(8,128)(2,1)S(1)} %copy-done.7, ...), custom_call_target="tpu_custom_call" | custom-call | flops 2359296000 | bytes 6291456 | tf_op jit(solution)/shard_map/tail/pallas_call | solution.py:463
  178.7 8.0 %all-gather.1 = bf16[12,256,128]{2,1,0:T(8,128)(2,1)S(1)} all-gather(bf16[3,256,128]{2,1,0:T(8,128)(2,1)S(1)} %get-tuple-element.32), channel_id=3, replica_groups=mesh['groups'=2,'ctx'=4,'fsdp'=4] {'fsdp'}, dimensions={0}, use_global_device_ids=true | all-gather | bytes 983040 | tf_op jit(solution)/shard_map/all_gather | solution.py:485
  186.7 6.6 %grads.3 = f32[256,512]{1,0:T(8,128)} custom-call(bf16[3,1024,256]{2,1,0:T(8,128)(2,1)S(1)} %multiply_convert_fusion.normed_ref, bf16[4,3,256,128]{3,2,1,0:T(8,128)(2,1)S(1)} %bitcast.49, bf16[1024,128]{1,0:T(8,128)(2,1)S(1)} %copy-done.12), custom_call_target="tpu_custom_call" | custom-call | flops 4831838208 | bytes 8388608 | tf_op jit(solution)/shard_map/grads/pallas_call | solution.py:490
  193.2 4.1 %all-to-all-start.3 = ((f32[4,64,512]{2,1,0:T(8,128)}), f32[4,64,512]{2,1,0:T(8,128)}, u32[]{:S(2)}, u32[]{:S(2)}) async-start(f32[4,64,512]{2,1,0:T(8,128)} %bitcast.18), calls=%async_computation.3 | async-start | bytes 1048576 | tf_op jit(solution)/shard_map/all_to_all | solution.py:305
  197.4 5.7 %grads.2 = f32[256,512]{1,0:T(8,128)S(1)} custom-call(bf16[3,1024,256]{2,1,0:T(8,128)(2,1)S(1)} %multiply_convert_fusion.normed_ref, bf16[4,3,256,128]{3,2,1,0:T(8,128)(2,1)S(1)} %bitcast.50, bf16[1024,128]{1,0:T(8,128)(2,1)S(1)} %copy-done.13), custom_call_target="tpu_custom_call" | custom-call | flops 4831838208 | bytes 8388608 | tf_op jit(solution)/shard_map/grads/pallas_call | solution.py:490
  203.1 9.6 %all-to-all-done.3 = f32[4,64,512]{2,1,0:T(8,128)} async-done(((f32[4,64,512]{2,1,0:T(8,128)}), f32[4,64,512]{2,1,0:T(8,128)}, u32[]{:S(2)}, u32[]{:S(2)}) %all-to-all-start.3) | async-done | bytes 524320 | tf_op jit(solution)/shard_map/all_to_all | solution.py:305
  212.7 16.9 %all_to_all.25 = f32[4,64,512]{2,1,0:T(8,128)S(1)} all-to-all(f32[4,64,512]{2,1,0:T(8,128)S(1)} %bitcast.51), channel_id=1, replica_groups=mesh['groups'=2,'ctx'=4,'fsdp'=4] {'ctx'}, dimensions={0} | all-to-all | bytes 1048576 | tf_op jit(solution)/shard_map/all_to_all | solution.py:305
  229.6 3.6 %all-to-all-start.4 = ((f32[16,64,128]{2,1,0:T(8,128)}), f32[16,64,128]{2,1,0:T(8,128)S(1)}, u32[]{:S(2)}, u32[]{:S(2)}) async-start(f32[16,64,128]{2,1,0:T(8,128)} %bitcast.19), calls=%async_computation.4 | async-start | bytes 1048576 | tf_op jit(solution)/shard_map/all_to_all | solution.py:305
  233.1 0.7 reduce.7
  233.8 1.1 reduce_sum.58
  235.0 0.7 pad_maximum_fusion.1
  235.7 11.9 %all-to-all-done.4 = f32[16,64,128]{2,1,0:T(8,128)S(1)} async-done(((f32[16,64,128]{2,1,0:T(8,128)}), f32[16,64,128]{2,1,0:T(8,128)S(1)}, u32[]{:S(2)}, u32[]{:S(2)}) %all-to-all-start.4) | async-done | bytes 524320 | tf_op jit(solution)/shard_map/all_to_all | solution.py:305
  247.6 0.6 reduce_sum.59
  (76 shorter events, 1.6 us)
Async XLA Ops:
  7.2 16.2 %copy-start = (f32[9,1024]{1,0:T(8,128)S(1)}, f32[9,1024]{1,0:T(8,128)}, u32[]{:S(2)}) copy-start(f32[9,1024]{1,0:T(8,128)} %param.17) | copy-start | bytes 110596
  7.2 5.6 %slice-start = ((bf16[256,1536]{1,0:T(8,128)(2,1)}), bf16[256,512]{1,0:T(8,128)(2,1)S(1)}, s32[]{:S(2)}) async-start(bf16[256,1536]{1,0:T(8,128)(2,1)} %param.18), calls=%async_computation.6 | async-start | bytes 524288 | tf_op jit(solution)/shard_map/slice | solution.py:351
  7.2 16.0 %collective-permute-start.1 = (bf16[256,1024]{1,0:T(8,128)(2,1)}, bf16[256,1024]{1,0:T(8,128)(2,1)S(1)}, u32[]{:S(2)}, u32[]{:S(2)}) collective-permute-start(bf16[256,1024]{1,0:T(8,128)(2,1)} %patches_ref.1), channel_id=1, source_target_pairs={{0,2},{1,3},{2,0},{3,1},{4,6},{5,7},{6,4},{7,5},{8,10},{9,11},{10,... | collective-permute-start | bytes 1572872 | tf_op jit(solution)/shard_map/ppermute | solution.py:335
  10.2 13.6 %collective-permute-start = (bf16[256,1024]{1,0:T(8,128)(2,1)}, bf16[256,1024]{1,0:T(8,128)(2,1)}, u32[]{:S(2)}, u32[]{:S(2)}) collective-permute-start(bf16[256,1024]{1,0:T(8,128)(2,1)} %patches_ref.1), channel_id=1, source_target_pairs={{0,1},{1,0},{2,3},{3,2},{4,5},{5,4},{6,7},{7,6},{8,9},{9,8},{10,11... | collective-permute-start | bytes 1572872 | tf_op jit(solution)/shard_map/ppermute | solution.py:336
  12.8 5.3 %copy-start.18 = (s32[2,4]{1,0:T(2,128)S(1)}, s32[2,4]{1,0:T(2,128)}, u32[]{:S(2)}) copy-start(s32[2,4]{1,0:T(2,128)} %param.16) | copy-start | bytes 100
  12.9 5.6 %copy-start.16 = (s32[2,3]{1,0:T(2,128)S(1)}, s32[2,3]{1,0:T(2,128)}, u32[]{:S(2)}) copy-start(s32[2,3]{1,0:T(2,128)} %param.15) | copy-start | bytes 76
  12.9 5.7 %copy-start.19 = (f32[2,16]{1,0:T(2,128)S(1)}, f32[2,16]{1,0:T(2,128)}, u32[]{:S(2)}) copy-start(f32[2,16]{1,0:T(2,128)} %param.21) | copy-start | bytes 388
  12.9 5.8 %copy-start.17 = (f32[2,16]{1,0:T(2,128)S(1)}, f32[2,16]{1,0:T(2,128)}, u32[]{:S(2)}) copy-start(f32[2,16]{1,0:T(2,128)} %param.20) | copy-start | bytes 388
  12.9 5.8 %copy-start.20 = (f32[16]{0:T(128)S(1)}, f32[16]{0:T(128)}, u32[]{:S(2)}) copy-start(f32[16]{0:T(128)} %param.22) | copy-start | bytes 196
  12.9 6.3 %copy-start.14 = (f32[1024]{0:T(1024)S(1)}, f32[1024]{0:T(1024)}, u32[]{:S(2)}) copy-start(f32[1024]{0:T(1024)} %param.23) | copy-start | bytes 12292
  12.9 12.1 %copy-start.6 = (bf16[256,1024]{1,0:T(8,128)(2,1)S(1)}, bf16[256,1024]{1,0:T(8,128)(2,1)}, u32[]{:S(2)}) copy-start(bf16[256,1024]{1,0:T(8,128)(2,1)} %patches_ref.1) | copy-start | bytes 1572868
  14.5 27.5 %all-to-all-start = ((bf16[4,256,896]{2,1,0:T(8,128)(2,1)}), bf16[4,256,896]{2,1,0:T(8,128)(2,1)S(1)}, u32[]{:S(2)}, u32[]{:S(2)}) async-start(bf16[4,256,896]{2,1,0:T(8,128)(2,1)} %maximum_maximum_fusion), calls=%async_computation | async-start | bytes 3670016 | tf_op jit(solution)/shard_map/all_to_all | solution.py:357
  18.1 131.8 %all-gather.4.cloned.1.call-start = ((), (), s32[]{:S(2)}) async-start(), calls=%async_computation.5 | async-start | bytes 2621440 | tf_op jit(solution)/shard_map/all_gather | solution.py:382
  23.2 1.9 collective-permute-start.2
  52.4 1.2 copy-start.3
  53.5 1.2 copy-start.5
  71.5 1.2 copy-start.8
  72.7 1.2 copy-start.10
  74.6 12.5 %collective-permute-start.6 = (f32[3,128,256]{2,1,0:T(8,128)}, f32[3,128,256]{2,1,0:T(8,128)}, u32[]{:S(2)}, u32[]{:S(2)}) collective-permute-start(f32[3,128,256]{2,1,0:T(8,128)} %get-tuple-element.41), channel_id=1, source_target_pairs={{4,0},{8,4},{12,8},{5,1},{9,5},{13,9},{6,2},{10,6},{14,10},{7,3},{... | collective-permute-start | bytes 1179656 | tf_op jit(solution)/shard_map/ppermute | solution.py:298
  76.0 25.7 %collective-permute-start.3 = (f32[3,128,256]{2,1,0:T(8,128)S(1)}, f32[3,128,256]{2,1,0:T(8,128)S(1)}, u32[]{:S(2)}, u32[]{:S(2)}) collective-permute-start(f32[3,128,256]{2,1,0:T(8,128)S(1)} %get-tuple-element.42), channel_id=1, source_target_pairs={{0,4},{4,8},{8,12},{1,5},{5,9},{9,13},{2,6},{6,10},{10,14},{3,7},{... | collective-permute-start | bytes 1179656 | tf_op jit(solution)/shard_map/ppermute | solution.py:298
  88.2 13.4 %collective-permute-start.7 = (f32[3,128,256]{2,1,0:T(8,128)S(1)}, f32[3,128,256]{2,1,0:T(8,128)S(1)}, u32[]{:S(2)}, u32[]{:S(2)}) collective-permute-start(f32[3,128,256]{2,1,0:T(8,128)S(1)} %multiply_add_fusion.1), channel_id=1, source_target_pairs={{4,0},{8,4},{12,8},{5,1},{9,5},{13,9},{6,2},{10,6},{14,10},{7,3},{... | collective-permute-start | bytes 1179656 | tf_op jit(solution)/shard_map/ppermute | solution.py:298
  89.5 1.5 copy-start.4
  91.0 1.4 copy-start.9
  92.5 1.4 copy-start.11
  101.8 13.6 %collective-permute-start.4 = (f32[3,128,256]{2,1,0:T(8,128)S(1)}, f32[3,128,256]{2,1,0:T(8,128)S(1)}, u32[]{:S(2)}, u32[]{:S(2)}) collective-permute-start(f32[3,128,256]{2,1,0:T(8,128)S(1)} %get-tuple-element.40), channel_id=1, source_target_pairs={{0,4},{4,8},{8,12},{1,5},{5,9},{9,13},{2,6},{6,10},{10,14},{3,7},{... | collective-permute-start | bytes 1179656 | tf_op jit(solution)/shard_map/ppermute | solution.py:298
  114.0 13.7 %collective-permute-start.8 = (f32[3,128,256]{2,1,0:T(8,128)S(1)}, f32[3,128,256]{2,1,0:T(8,128)S(1)}, u32[]{:S(2)}, u32[]{:S(2)}) collective-permute-start(f32[3,128,256]{2,1,0:T(8,128)S(1)} %get-tuple-element.39), channel_id=1, source_target_pairs={{4,0},{8,4},{12,8},{5,1},{9,5},{13,9},{6,2},{10,6},{14,10},{7,3},{... | collective-permute-start | bytes 1179656 | tf_op jit(solution)/shard_map/ppermute | solution.py:298
  115.4 12.4 %collective-permute-start.5 = (f32[3,128,256]{2,1,0:T(8,128)S(1)}, f32[3,128,256]{2,1,0:T(8,128)S(1)}, u32[]{:S(2)}, u32[]{:S(2)}) collective-permute-start(f32[3,128,256]{2,1,0:T(8,128)S(1)} %multiply_add_fusion.2), channel_id=1, source_target_pairs={{0,4},{4,8},{8,12},{1,5},{5,9},{9,13},{2,6},{6,10},{10,14},{3,7},{... | collective-permute-start | bytes 1179656 | tf_op jit(solution)/shard_map/ppermute | solution.py:298
  135.4 1.6 copy-start.1
  144.9 4.9 %copy-start.15 = (s32[256]{0:T(256)S(1)}, s32[256]{0:T(256)}, u32[]{:S(2)}) copy-start(s32[256]{0:T(256)} %param.14) | copy-start | bytes 3076
  146.2 23.6 %all-to-all-start.1 = ((bf16[4,3,256,256]{3,2,1,0:T(8,128)(2,1)}), bf16[4,3,256,256]{3,2,1,0:T(8,128)(2,1)S(1)}, u32[]{:S(2)}, u32[]{:S(2)}) async-start(bf16[4,3,256,256]{3,2,1,0:T(8,128)(2,1)} %bitcast.52), calls=%async_computation.1 | async-start | bytes 3145728 | tf_op jit(solution)/shard_map/all_to_all | solution.py:458
  169.8 1.6 copy-start.2
  171.4 1.0 copy-start.7
  172.4 0.9 copy-start.12
  186.7 10.7 %copy-start.13 = (bf16[1024,128]{1,0:T(8,128)(2,1)S(1)}, bf16[1024,128]{1,0:T(8,128)(2,1)}, u32[]{:S(2)}) copy-start(bf16[1024,128]{1,0:T(8,128)(2,1)} %head_ref.5) | copy-start | bytes 786436
  193.2 19.5 %all-to-all-start.3 = ((f32[4,64,512]{2,1,0:T(8,128)}), f32[4,64,512]{2,1,0:T(8,128)}, u32[]{:S(2)}, u32[]{:S(2)}) async-start(f32[4,64,512]{2,1,0:T(8,128)} %bitcast.18), calls=%async_computation.3 | async-start | bytes 1048576 | tf_op jit(solution)/shard_map/all_to_all | solution.py:305
  229.6 18.0 %all-to-all-start.4 = ((f32[16,64,128]{2,1,0:T(8,128)}), f32[16,64,128]{2,1,0:T(8,128)S(1)}, u32[]{:S(2)}, u32[]{:S(2)}) async-start(f32[16,64,128]{2,1,0:T(8,128)} %bitcast.19), calls=%async_computation.4 | async-start | bytes 1048576 | tf_op jit(solution)/shard_map/all_to_all | solution.py:305
Sparse Core Ops, SparseCore 0:
  80.7 23.7 all-gather.3

commit v4 on v3

--- a/solution.py
+++ b/solution.py
@@ -483,23 +483,18 @@
 
     if ctx_count * shards == HEADS:
         grads_all = lax.all_gather(grads, "fsdp")
-        grads_all, head_term = lax.optimization_barrier((grads_all, head_term))
-        half = D // 2
-        sums = []
-        for k in range(2):
-            grad_rows = call(
-                functools.partial(grad_kernel, shards), "grads",
-                VIEWS * rows * D * (width + CLASSES) * 4, 8 << 20,
-                grid=(VIEWS, shards),
-                in_specs=[
-                    pl.BlockSpec((1, row_count, width), lambda v, s: (v, s, 0)),
-                    pl.BlockSpec((1, 1, row_count, CLASSES), lambda v, s: (s, v, 0, 0)),
-                    pl.BlockSpec((half, CLASSES), lambda v, s, k=k: (k, 0))],
-                out_specs=fixed(width, half),
-                out_shape=jax.ShapeDtypeStruct((width, half), f32),
-            )(normed, grads_all, head_weight)
-            sums.append(scatter_sum(grad_rows, "ctx", ctx_count))
-        grad_out = jnp.concatenate(sums, axis=1)
+        grad_rows = call(
+            functools.partial(grad_kernel, shards), "grads",
+            VIEWS * rows * D * (width + CLASSES) * 2, 8 << 20,
+            grid=(VIEWS, shards),
+            in_specs=[
+                pl.BlockSpec((1, row_count, width), lambda v, s: (v, s, 0)),
+                pl.BlockSpec((1, 1, row_count, CLASSES), lambda v, s: (s, v, 0, 0)),
+                fixed(D, CLASSES)],
+            out_specs=fixed(width, D),
+            out_shape=jax.ShapeDtypeStruct((width, D), f32),
+        )(normed, grads_all, head_weight)
+        grad_out = scatter_sum(grad_rows, "ctx", ctx_count)
     else:
         grad_hidden = lax.dot_general(
             grads, head_weight, (((2,), (1,)), ((), ())), preferred_element_type=f32

time: 257 us -> 246 us (0.957)
  blocking collectives: 30.1 us -> 17.7 us
  Pallas kernels: 75.8 us -> 70.9 us
  local copies, waits for them, and re-layouts: 23.5 us -> 26.8 us
  waiting for transfers between devices: 64.1 us -> 67 us
    all_to_all x1 -> x0, blocking collectives: 16.9 us -> none  [scatter_sum(): lax.all_to_all(blocks, axes, split_axis=0, concat_axis=0)]
    all_gather x1, blocking collectives: 8 us -> 12.5 us  [on_device(): grads_all = lax.all_gather(grads, 'fsdp')]
    pallas_call x2 -> x1, Pallas kernels: 12.3 us -> 8.22 us  [on_device(): call(functools.partial(grad_kernel, shards), 'grads', VIEWS * rows * D *...]
    all_to_all x2, waiting for transfers between devices: 21.5 us -> 24.9 us  [scatter_sum(): lax.all_to_all(blocks, axes, split_axis=0, concat_axis=0)]
    unnamed x46 -> x50, local copies, waits for them, and re-layouts: 14.6 us -> 17.2 us
  transfers between devices with their start and end apart: 14 -> 14, of which waited for: 7 -> 6; matrix products, arithmetic and copies ran while one was open for 8% -> 8% of each run, Pallas kernels for 14% -> 16%
where the time goes in v4:
time: 246 us; the launch traced here: 245 us
  Pallas kernels  70.9 us (29%)
  waiting for transfers between devices  67 us (27%)
  starting transfers between devices  37.1 us (15%)
  local copies, waits for them, and re-layouts  26.8 us (11%)
  blocking collectives  17.7 us (7%)
  between operations  14.4 us (6%)
  other arithmetic  10.4 us (4%)
    all_to_all x2, waiting for transfers between devices, scatter_sum(): lax.all_to_all(blocks, axes, split_axis=0, concat_axis=0)  24.9 us
    pallas_call x3, Pallas kernels, on_device(): call(functools.partial(inside_kernel, heads), 'inside', rows * D * 8192,...  23.3 us
    ppermute x6, starting transfers between devices, carried_in(): got = lax.ppermute(sent, axis, hops)  17.5 us
    unnamed x50, local copies, waits for them, and re-layouts  17.2 us
    pallas_call x1, Pallas kernels, on_device(): call(functools.partial(states_kernel, heads), 'states', VIEWS * rows * ST...  16.8 us
    all_to_all x1, waiting for transfers between devices, on_device(): arrived = lax.all_to_all(outgoing, 'fsdp', split_axis=0, concat_axis=0)  16.1 us
    all_to_all x1, waiting for transfers between devices, on_device(): lax.all_to_all(sent_weight, 'fsdp', split_axis=0, concat_axis=0)  14.4 us
    all_gather x1, blocking collectives, on_device(): grads_all = lax.all_gather(grads, 'fsdp')  12.5 us
  transfers between devices with their start and end apart: 14, of which 6 were waited for; matrix products, arithmetic and copies ran while one was open for 8% of the time, Pallas kernels for 16%

profile of v4, /device:TPU:0, one launch (start us, length us, event | category | flops | bytes accessed | tf_op | source)
XLA Modules:
  0.0 244.5 jit_solution(13652046436867871614)
XLA Ops:
  7.2 3.0 %collective-permute-start.1 = (bf16[256,1024]{1,0:T(8,128)(2,1)}, bf16[256,1024]{1,0:T(8,128)(2,1)S(1)}, u32[]{:S(2)}, u32[]{:S(2)}) collective-permute-start(bf16[256,1024]{1,0:T(8,128)(2,1)} %patches_ref.1), channel_id=1, source_target_pairs={{0,2},{1,3},{2,0},{3,1},{4,6},{5,7},{6,4},{7,5},{8,10},{9,11},{10,... | collective-permute-start | bytes 1572872 | tf_op jit(solution)/shard_map/ppermute | solution.py:335
  10.2 1.1 slice.33
  11.3 0.7 reshape.65
  12.0 0.2 copy.46
  12.2 0.2 copy.56
  12.5 0.2 copy.47
  12.9 1.6 maximum_maximum_fusion
  14.5 3.6 %all-to-all-start = ((bf16[4,256,896]{2,1,0:T(8,128)(2,1)}), bf16[4,256,896]{2,1,0:T(8,128)(2,1)S(1)}, u32[]{:S(2)}, u32[]{:S(2)}) async-start(bf16[4,256,896]{2,1,0:T(8,128)(2,1)} %maximum_maximum_fusion), calls=%async_computation | async-start | bytes 3670016 | tf_op jit(solution)/shard_map/all_to_all | solution.py:357
  18.2 0.1 slice_reduce_fusion
  18.8 0.2 dynamic-slice_reduce_fusion.3
  19.4 3.7 %collective-permute-done.1 = bf16[256,1024]{1,0:T(8,128)(2,1)S(1)} collective-permute-done((bf16[256,1024]{1,0:T(8,128)(2,1)}, bf16[256,1024]{1,0:T(8,128)(2,1)S(1)}, u32[]{:S(2)}, u32[]{:S(2)}) %collective-permute-start.1) | collective-permute-done | bytes 524320 | tf_op jit(solution)/shard_map/ppermute | solution.py:335
  23.2 0.2 fusion.2
  23.4 0.2 fusion
  23.6 0.2 dynamic-slice_reduce_fusion
  23.8 1.3 collective-permute-done.2
  25.1 2.5 %pad_maximum_fusion.patches_ref = bf16[1024,1024]{1,0:T(8,128)(2,1)} fusion(bf16[256,1024]{1,0:T(8,128)(2,1)S(1)} %collective-permute-done.2, bf16[256,1024]{1,0:T(8,128)(2,1)S(1)} %collective-permute-done.1, bf16[256,1024]{1,0:T(8,128)(2,1)} %collective-permute-done, bf16[256,1024]{1,0:T(8,128)(2,1)S(1)} %copy-done.7), kind=kLoop, calls=%fused_computation.1 | loop fusion | flops 8388608 | bytes 4194304 | tf_op jit(solution)/shard_map/concatenate | solution.py:338
  27.6 14.4 %all-to-all-done = bf16[4,256,896]{2,1,0:T(8,128)(2,1)S(1)} async-done(((bf16[4,256,896]{2,1,0:T(8,128)(2,1)}), bf16[4,256,896]{2,1,0:T(8,128)(2,1)S(1)}, u32[]{:S(2)}, u32[]{:S(2)}) %all-to-all-start) | async-done | bytes 1835040 | tf_op jit(solution)/shard_map/all_to_all | solution.py:357
  42.0 10.3 %project.1 = (bf16[3,1024,256]{2,1,0:T(8,128)(2,1)S(1)}, bf16[3,1024,512]{2,1,0:T(8,128)(2,1)}, f32[3,1024,128]{2,1,0:T(8,128)S(1)}) custom-call(s32[1]{0:T(128)} %bitcast.place_ref, bf16[1024,1024]{1,0:T(8,128)(2,1)} %pad_maximum_fusion.patches_ref, f32[3,1024]{1,0:T(4,128)S(1)} %concatenate.10.scale_ref, bf16[1024,896]{1,0:T(8,128)(2,1)S(1)} %bitcast.47), custom_call_target="tpu_custom_call" | custom-call | flops 5637144576 | bytes 8388608 | tf_op jit(solution)/shard_map/project/pallas_call | solution.py:365
  52.3 1.1 copy-done.3
  53.5 1.2 copy-done.5
  54.6 16.8 %states.1 = (f32[3,2,136,256]{3,2,1,0:T(8,128)S(1)}, bf16[3,2,8,256,256]{4,3,2,1,0:T(8,128)(2,1)}, f32[3,1024,128]{2,1,0:T(8,128)S(1)}, f32[3,1024,128]{2,1,0:T(8,128)S(1)}, f32[3,1024,128]{2,1,0:T(8,128)S(1)}) custom-call(f32[3,1024,128]{2,1,0:T(8,128)} %copy-done.5, bf16[3,1024,256]{2,1,0:T(8,128)(2,1)} %copy-done.3, ...), custom_call_target="tpu_custom_call" | custom-call | flops 805306368 | bytes 25165824 | tf_op jit(solution)/shard_map/states/pallas_call | solution.py:397
  71.5 1.2 copy-done.10
  72.6 1.2 copy-done.12
  73.8 0.8 slice_bitcast_fusion
  74.6 1.3 collective-permute-start.6
  75.9 4.6 %collective-permute-start.3 = (f32[3,128,256]{2,1,0:T(8,128)S(1)}, f32[3,128,256]{2,1,0:T(8,128)S(1)}, u32[]{:S(2)}, u32[]{:S(2)}) collective-permute-start(f32[3,128,256]{2,1,0:T(8,128)S(1)} %get-tuple-element.38), channel_id=1, source_target_pairs={{0,4},{4,8},{8,12},{1,5},{5,9},{9,13},{2,6},{6,10},{10,14},{3,7},{... | collective-permute-start | bytes 1179656 | tf_op jit(solution)/shard_map/ppermute | solution.py:298
  80.5 6.6 %collective-permute-done.6 = f32[3,128,256]{2,1,0:T(8,128)} collective-permute-done((f32[3,128,256]{2,1,0:T(8,128)}, f32[3,128,256]{2,1,0:T(8,128)}, u32[]{:S(2)}, u32[]{:S(2)}) %collective-permute-start.6) | collective-permute-done | bytes 393248 | tf_op jit(solution)/shard_map/ppermute | solution.py:298
  87.1 1.1 multiply_add_fusion.1
  88.2 1.3 collective-permute-start.7
  89.5 1.5 copy-done.4
  91.0 1.4 copy-done.11
  92.4 1.4 copy-done.13
  93.8 7.8 %inside.3.rest_0_ = f32[3,1024,256]{2,1,0:T(8,128)} custom-call(bf16[3,1024,256]{2,1,0:T(8,128)(2,1)S(1)} %copy-done.4, bf16[3,1024,512]{2,1,0:T(8,128)(2,1)} %get-tuple-element.21.coef_ref, bf16[3,2,8,256,256]{4,3,2,1,0:T(8,128)(2,1)} %get-tuple-element.24.prefix_ref, f32[3,1024,128]{2,1,0:T(8,128)S(1)} %copy-done.11, f32[3,1024,128]{2,1,0:T(8,128)S(1)} %copy-done.13, ...), custom_call_target="tpu_custom_call" | custom-call | flops 8589934592 | bytes 8388608 | tf_op jit(solution)/shard_map/inside/pallas_call | solution.py:422
  101.6 0.1 multiply_add_fusion
  101.7 4.5 %collective-permute-start.4 = (f32[3,128,256]{2,1,0:T(8,128)S(1)}, f32[3,128,256]{2,1,0:T(8,128)S(1)}, u32[]{:S(2)}, u32[]{:S(2)}) collective-permute-start(f32[3,128,256]{2,1,0:T(8,128)S(1)} %get-tuple-element.36), channel_id=1, source_target_pairs={{0,4},{4,8},{8,12},{1,5},{5,9},{9,13},{2,6},{6,10},{10,14},{3,7},{... | collective-permute-start | bytes 1179656 | tf_op jit(solution)/shard_map/ppermute | solution.py:298
  106.2 7.8 %inside.4.rest_0_ = f32[3,1024,256]{2,1,0:T(8,128)} custom-call(bf16[3,1024,256]{2,1,0:T(8,128)(2,1)S(1)} %copy-done.4, bf16[3,1024,512]{2,1,0:T(8,128)(2,1)} %get-tuple-element.21.coef_ref, bf16[3,2,8,256,256]{4,3,2,1,0:T(8,128)(2,1)} %get-tuple-element.24.prefix_ref, f32[3,1024,128]{2,1,0:T(8,128)S(1)} %copy-done.11, ...), custom_call_target="tpu_custom_call", output_to_operand_aliasing={{}: (6, {})} | custom-call | flops 8589934592 | bytes 8388608 | tf_op jit(solution)/shard_map/inside/pallas_call | solution.py:422
  114.0 1.3 collective-permute-start.8
  115.3 4.6 %collective-permute-start.5 = (f32[3,128,256]{2,1,0:T(8,128)S(1)}, f32[3,128,256]{2,1,0:T(8,128)S(1)}, u32[]{:S(2)}, u32[]{:S(2)}) collective-permute-start(f32[3,128,256]{2,1,0:T(8,128)S(1)} %multiply_add_fusion.2), channel_id=1, source_target_pairs={{0,4},{4,8},{8,12},{1,5},{5,9},{9,13},{2,6},{6,10},{10,14},{3,7},{... | collective-permute-start | bytes 1179656 | tf_op jit(solution)/shard_map/ppermute | solution.py:298
  119.9 7.8 %inside.5.local_ref = f32[3,1024,256]{2,1,0:T(8,128)} custom-call(bf16[3,1024,256]{2,1,0:T(8,128)(2,1)S(1)} %copy-done.4, bf16[3,1024,512]{2,1,0:T(8,128)(2,1)} %get-tuple-element.21.coef_ref, bf16[3,2,8,256,256]{4,3,2,1,0:T(8,128)(2,1)} %get-tuple-element.24.prefix_ref, f32[3,1024,128]{2,1,0:T(8,128)S(1)} %copy-done.11, ...), custom_call_target="tpu_custom_call", output_to_operand_aliasing={{}: (6, {})} | custom-call | flops 8589934592 | bytes 8388608 | tf_op jit(solution)/shard_map/inside/pallas_call | solution.py:422
  127.7 7.6 %incoming.1 = (f32[3,1024,256]{2,1,0:T(8,128)S(1)}, f32[3,8,1024]{2,1,0:T(8,128)S(1)}) custom-call(f32[3,128,256]{2,1,0:T(8,128)S(1)} %collective-permute-done.5.forward_ref, f32[3,128,256]{2,1,0:T(8,128)S(1)} %collective-permute-done.8.reverse_ref, bf16[3,1024,512]{2,1,0:T(8,128)(2,1)} %get-tuple-element.21.coef_ref, ...), custom_call_target="tpu_custom_call" | custom-call | flops 805306368 | bytes 25165824 | tf_op jit(solution)/shard_map/incoming/pallas_call | solution.py:439
  135.3 1.7 copy-done.1
  137.0 5.2 %all-gather = f32[12,1,1024]{2,1,0:T(1,128)S(1)} all-gather(f32[3,1,1024]{2,1,0:T(1,128)S(1)} %slice.40), channel_id=2, replica_groups=mesh['groups'=2,'ctx'=4,'fsdp'=4] {'fsdp'}, dimensions={0}, use_global_device_ids=true | all-gather | bytes 61440 | tf_op jit(solution)/shard_map/all_gather | solution.py:454
  142.2 0.1 reduce.5
  142.4 2.4 multiply_convert_fusion.normed_ref
  144.8 1.3 copy.68
  146.1 3.6 %all-to-all-start.1 = ((bf16[4,3,256,256]{3,2,1,0:T(8,128)(2,1)}), bf16[4,3,256,256]{3,2,1,0:T(8,128)(2,1)S(1)}, u32[]{:S(2)}, u32[]{:S(2)}) async-start(bf16[4,3,256,256]{3,2,1,0:T(8,128)(2,1)} %bitcast.50), calls=%async_computation.1 | async-start | bytes 3145728 | tf_op jit(solution)/shard_map/all_to_all | solution.py:458
  149.6 0.8 copy.52.label_ref
  150.5 3.2 %copy.51 = bf16[4,4,64,1024]{3,2,0,1:T(8,128)(2,1)} copy(bf16[4,4,64,1024]{3,2,1,0:T(8,128)(2,1)} %bitcast.51) | data formatting | bytes 4194304 | tf_op jit(solution)/shard_map/reshape | solution.py:460
  153.6 16.1 %all-to-all-done.1.normed_ref = bf16[4,3,256,256]{3,2,1,0:T(8,128)(2,1)S(1)} async-done(((bf16[4,3,256,256]{3,2,1,0:T(8,128)(2,1)}), bf16[4,3,256,256]{3,2,1,0:T(8,128)(2,1)S(1)}, u32[]{:S(2)}, u32[]{:S(2)}) %all-to-all-start.1) | async-done | bytes 1572896 | tf_op jit(solution)/shard_map/all_to_all | solution.py:458
  169.7 1.6 copy-done.2
  171.3 1.0 copy-done.8
  172.3 0.9 copy-done.9
  173.2 0.9 copy-done.14
  174.2 4.5 %tail.1 = (bf16[3,256,128]{2,1,0:T(8,128)(2,1)S(1)}, f32[256,1]{1,0:T(8,128)S(1)}, f32[1024,128]{1,0:T(8,128)S(1)}) custom-call(bf16[4,3,256,256]{3,2,1,0:T(8,128)(2,1)S(1)} %all-to-all-done.1.normed_ref, bf16[4,256,1024]{2,1,0:T(8,128)(2,1)S(1)} %bitcast.46, bf16[1024,128]{1,0:T(8,128)(2,1)S(1)} %copy-done.14, bf16[256,1024]{1,0:T(8,128)(2,1)S(1)} %copy-done.8, ...), custom_call_target="tpu_custom_call" | custom-call | flops 2359296000 | bytes 6291456 | tf_op jit(solution)/shard_map/tail/pallas_call | solution.py:463
  178.7 0.8 copy-done.6
  179.5 3.9 %all-to-all-start.3 = ((f32[16,64,128]{2,1,0:T(8,128)}), f32[16,64,128]{2,1,0:T(8,128)S(1)}, u32[]{:S(2)}, u32[]{:S(2)}) async-start(f32[16,64,128]{2,1,0:T(8,128)} %bitcast.49), calls=%async_computation.3 | async-start | bytes 1048576 | tf_op jit(solution)/shard_map/all_to_all | solution.py:305
  183.5 12.5 %all-gather.1 = bf16[12,256,128]{2,1,0:T(8,128)(2,1)S(1)} all-gather(bf16[3,256,128]{2,1,0:T(8,128)(2,1)S(1)} %get-tuple-element.30), channel_id=3, replica_groups=mesh['groups'=2,'ctx'=4,'fsdp'=4] {'fsdp'}, dimensions={0}, use_global_device_ids=true | all-gather | bytes 983040 | tf_op jit(solution)/shard_map/all_gather | solution.py:485
  196.0 0.9 copy-done.15
  196.9 8.2 %grads.1 = f32[256,1024]{1,0:T(8,128)} custom-call(bf16[3,1024,256]{2,1,0:T(8,128)(2,1)S(1)} %multiply_convert_fusion.normed_ref, bf16[4,3,256,128]{3,2,1,0:T(8,128)(2,1)S(1)} %bitcast.48, bf16[1024,128]{1,0:T(8,128)(2,1)S(1)} %copy-done.15), custom_call_target="tpu_custom_call" | custom-call | flops 2415919104 | bytes 8388608 | tf_op jit(solution)/shard_map/grads/pallas_call | solution.py:486
  205.1 5.5 %all-to-all-start.2 = ((f32[4,64,1024]{2,1,0:T(8,128)}), f32[4,64,1024]{2,1,0:T(8,128)S(1)}, u32[]{:S(2)}, u32[]{:S(2)}) async-start(f32[4,64,1024]{2,1,0:T(8,128)} %bitcast.17), calls=%async_computation.2 | async-start | bytes 2097152 | tf_op jit(solution)/shard_map/all_to_all | solution.py:305
  210.7 0.7 reduce.7
  211.3 0.6 reduce_sum.49
  212.0 24.9 %all-to-all-done.2 = f32[4,64,1024]{2,1,0:T(8,128)S(1)} async-done(((f32[4,64,1024]{2,1,0:T(8,128)}), f32[4,64,1024]{2,1,0:T(8,128)S(1)}, u32[]{:S(2)}, u32[]{:S(2)}) %all-to-all-start.2) | async-done | bytes 1048608 | tf_op jit(solution)/shard_map/all_to_all | solution.py:305
  236.9 0.8 reduce_sum.48
  (76 shorter events, 1.5 us)
Async XLA Ops:
  7.2 16.2 %copy-start = (f32[9,1024]{1,0:T(8,128)S(1)}, f32[9,1024]{1,0:T(8,128)}, u32[]{:S(2)}) copy-start(f32[9,1024]{1,0:T(8,128)} %param.17) | copy-start | bytes 110596
  7.2 5.6 %slice-start = ((bf16[256,1536]{1,0:T(8,128)(2,1)}), bf16[256,512]{1,0:T(8,128)(2,1)S(1)}, s32[]{:S(2)}) async-start(bf16[256,1536]{1,0:T(8,128)(2,1)} %param.18), calls=%async_computation.5 | async-start | bytes 524288 | tf_op jit(solution)/shard_map/slice | solution.py:351
  7.2 16.0 %collective-permute-start.1 = (bf16[256,1024]{1,0:T(8,128)(2,1)}, bf16[256,1024]{1,0:T(8,128)(2,1)S(1)}, u32[]{:S(2)}, u32[]{:S(2)}) collective-permute-start(bf16[256,1024]{1,0:T(8,128)(2,1)} %patches_ref.1), channel_id=1, source_target_pairs={{0,2},{1,3},{2,0},{3,1},{4,6},{5,7},{6,4},{7,5},{8,10},{9,11},{10,... | collective-permute-start | bytes 1572872 | tf_op jit(solution)/shard_map/ppermute | solution.py:335
  10.2 13.6 %collective-permute-start = (bf16[256,1024]{1,0:T(8,128)(2,1)}, bf16[256,1024]{1,0:T(8,128)(2,1)}, u32[]{:S(2)}, u32[]{:S(2)}) collective-permute-start(bf16[256,1024]{1,0:T(8,128)(2,1)} %patches_ref.1), channel_id=1, source_target_pairs={{0,1},{1,0},{2,3},{3,2},{4,5},{5,4},{6,7},{7,6},{8,9},{9,8},{10,11... | collective-permute-start | bytes 1572872 | tf_op jit(solution)/shard_map/ppermute | solution.py:336
  12.8 5.3 %copy-start.20 = (s32[2,4]{1,0:T(2,128)S(1)}, s32[2,4]{1,0:T(2,128)}, u32[]{:S(2)}) copy-start(s32[2,4]{1,0:T(2,128)} %param.16) | copy-start | bytes 100
  12.9 5.6 %copy-start.18 = (s32[2,3]{1,0:T(2,128)S(1)}, s32[2,3]{1,0:T(2,128)}, u32[]{:S(2)}) copy-start(s32[2,3]{1,0:T(2,128)} %param.15) | copy-start | bytes 76
  12.9 5.7 %copy-start.21 = (f32[2,16]{1,0:T(2,128)S(1)}, f32[2,16]{1,0:T(2,128)}, u32[]{:S(2)}) copy-start(f32[2,16]{1,0:T(2,128)} %param.21) | copy-start | bytes 388
  12.9 5.8 %copy-start.19 = (f32[2,16]{1,0:T(2,128)S(1)}, f32[2,16]{1,0:T(2,128)}, u32[]{:S(2)}) copy-start(f32[2,16]{1,0:T(2,128)} %param.20) | copy-start | bytes 388
  12.9 5.8 %copy-start.22 = (f32[16]{0:T(128)S(1)}, f32[16]{0:T(128)}, u32[]{:S(2)}) copy-start(f32[16]{0:T(128)} %param.22) | copy-start | bytes 196
  12.9 6.3 %copy-start.16 = (f32[1024]{0:T(1024)S(1)}, f32[1024]{0:T(1024)}, u32[]{:S(2)}) copy-start(f32[1024]{0:T(1024)} %param.23) | copy-start | bytes 12292
  12.9 12.1 %copy-start.7 = (bf16[256,1024]{1,0:T(8,128)(2,1)S(1)}, bf16[256,1024]{1,0:T(8,128)(2,1)}, u32[]{:S(2)}) copy-start(bf16[256,1024]{1,0:T(8,128)(2,1)} %patches_ref.1) | copy-start | bytes 1572868
  14.5 27.5 %all-to-all-start = ((bf16[4,256,896]{2,1,0:T(8,128)(2,1)}), bf16[4,256,896]{2,1,0:T(8,128)(2,1)S(1)}, u32[]{:S(2)}, u32[]{:S(2)}) async-start(bf16[4,256,896]{2,1,0:T(8,128)(2,1)} %maximum_maximum_fusion), calls=%async_computation | async-start | bytes 3670016 | tf_op jit(solution)/shard_map/all_to_all | solution.py:357
  18.1 132.3 %all-gather.4.cloned.1.call-start = ((), (), s32[]{:S(2)}) async-start(), calls=%async_computation.4 | async-start | bytes 2621440 | tf_op jit(solution)/shard_map/all_gather | solution.py:382
  23.2 1.9 collective-permute-start.2
  52.3 1.1 copy-start.3
  53.5 1.2 copy-start.5
  71.5 1.2 copy-start.10
  72.6 1.2 copy-start.12
  74.6 12.5 %collective-permute-start.6 = (f32[3,128,256]{2,1,0:T(8,128)}, f32[3,128,256]{2,1,0:T(8,128)}, u32[]{:S(2)}, u32[]{:S(2)}) collective-permute-start(f32[3,128,256]{2,1,0:T(8,128)} %get-tuple-element.37), channel_id=1, source_target_pairs={{4,0},{8,4},{12,8},{5,1},{9,5},{13,9},{6,2},{10,6},{14,10},{7,3},{... | collective-permute-start | bytes 1179656 | tf_op jit(solution)/shard_map/ppermute | solution.py:298
  75.9 25.7 %collective-permute-start.3 = (f32[3,128,256]{2,1,0:T(8,128)S(1)}, f32[3,128,256]{2,1,0:T(8,128)S(1)}, u32[]{:S(2)}, u32[]{:S(2)}) collective-permute-start(f32[3,128,256]{2,1,0:T(8,128)S(1)} %get-tuple-element.38), channel_id=1, source_target_pairs={{0,4},{4,8},{8,12},{1,5},{5,9},{9,13},{2,6},{6,10},{10,14},{3,7},{... | collective-permute-start | bytes 1179656 | tf_op jit(solution)/shard_map/ppermute | solution.py:298
  88.2 13.4 %collective-permute-start.7 = (f32[3,128,256]{2,1,0:T(8,128)S(1)}, f32[3,128,256]{2,1,0:T(8,128)S(1)}, u32[]{:S(2)}, u32[]{:S(2)}) collective-permute-start(f32[3,128,256]{2,1,0:T(8,128)S(1)} %multiply_add_fusion.1), channel_id=1, source_target_pairs={{4,0},{8,4},{12,8},{5,1},{9,5},{13,9},{6,2},{10,6},{14,10},{7,3},{... | collective-permute-start | bytes 1179656 | tf_op jit(solution)/shard_map/ppermute | solution.py:298
  89.5 1.5 copy-start.4
  91.0 1.4 copy-start.11
  92.4 1.4 copy-start.13
  101.7 13.5 %collective-permute-start.4 = (f32[3,128,256]{2,1,0:T(8,128)S(1)}, f32[3,128,256]{2,1,0:T(8,128)S(1)}, u32[]{:S(2)}, u32[]{:S(2)}) collective-permute-start(f32[3,128,256]{2,1,0:T(8,128)S(1)} %get-tuple-element.36), channel_id=1, source_target_pairs={{0,4},{4,8},{8,12},{1,5},{5,9},{9,13},{2,6},{6,10},{10,14},{3,7},{... | collective-permute-start | bytes 1179656 | tf_op jit(solution)/shard_map/ppermute | solution.py:298
  114.0 13.7 %collective-permute-start.8 = (f32[3,128,256]{2,1,0:T(8,128)S(1)}, f32[3,128,256]{2,1,0:T(8,128)S(1)}, u32[]{:S(2)}, u32[]{:S(2)}) collective-permute-start(f32[3,128,256]{2,1,0:T(8,128)S(1)} %get-tuple-element.35), channel_id=1, source_target_pairs={{4,0},{8,4},{12,8},{5,1},{9,5},{13,9},{6,2},{10,6},{14,10},{7,3},{... | collective-permute-start | bytes 1179656 | tf_op jit(solution)/shard_map/ppermute | solution.py:298
  115.3 12.3 %collective-permute-start.5 = (f32[3,128,256]{2,1,0:T(8,128)S(1)}, f32[3,128,256]{2,1,0:T(8,128)S(1)}, u32[]{:S(2)}, u32[]{:S(2)}) collective-permute-start(f32[3,128,256]{2,1,0:T(8,128)S(1)} %multiply_add_fusion.2), channel_id=1, source_target_pairs={{0,4},{4,8},{8,12},{1,5},{5,9},{9,13},{2,6},{6,10},{10,14},{3,7},{... | collective-permute-start | bytes 1179656 | tf_op jit(solution)/shard_map/ppermute | solution.py:298
  135.3 1.7 copy-start.1
  144.8 4.9 %copy-start.17 = (s32[256]{0:T(256)S(1)}, s32[256]{0:T(256)}, u32[]{:S(2)}) copy-start(s32[256]{0:T(256)} %param.14) | copy-start | bytes 3076
  146.1 23.6 %all-to-all-start.1 = ((bf16[4,3,256,256]{3,2,1,0:T(8,128)(2,1)}), bf16[4,3,256,256]{3,2,1,0:T(8,128)(2,1)S(1)}, u32[]{:S(2)}, u32[]{:S(2)}) async-start(bf16[4,3,256,256]{3,2,1,0:T(8,128)(2,1)} %bitcast.50), calls=%async_computation.1 | async-start | bytes 3145728 | tf_op jit(solution)/shard_map/all_to_all | solution.py:458
  169.7 1.6 copy-start.2
  171.3 1.0 copy-start.8
  172.3 0.9 copy-start.9
  173.2 0.9 copy-start.14
  178.7 0.8 copy-start.6
  179.5 25.6 %all-to-all-start.3 = ((f32[16,64,128]{2,1,0:T(8,128)}), f32[16,64,128]{2,1,0:T(8,128)S(1)}, u32[]{:S(2)}, u32[]{:S(2)}) async-start(f32[16,64,128]{2,1,0:T(8,128)} %bitcast.49), calls=%async_computation.3 | async-start | bytes 1048576 | tf_op jit(solution)/shard_map/all_to_all | solution.py:305
  196.0 0.9 copy-start.15
  205.1 31.8 %all-to-all-start.2 = ((f32[4,64,1024]{2,1,0:T(8,128)}), f32[4,64,1024]{2,1,0:T(8,128)S(1)}, u32[]{:S(2)}, u32[]{:S(2)}) async-start(f32[4,64,1024]{2,1,0:T(8,128)} %bitcast.17), calls=%async_computation.2 | async-start | bytes 2097152 | tf_op jit(solution)/shard_map/all_to_all | solution.py:305
Sparse Core Ops, SparseCore 0:
  80.7 23.7 all-gather.3

commit v5 on v4

--- a/solution.py
+++ b/solution.py
@@ -73,7 +73,11 @@
     patches = patches_ref[...].astype(f32)
     for v in range(VIEWS):
         view = (scale_ref[v : v + 1, :] * patches).astype(bf16)
-        out = dot(view, weight_ref[...])
+        depth = weight_ref.shape[1]
+        out = sum(
+            dot(view[:, s * depth : (s + 1) * depth], weight_ref[s ^ place_ref[0]])
+            for s in range(weight_ref.shape[0])
+        )
         x_ref[v] = out[:, :width].astype(bf16)
         coef_ref[v] = out[:, width : width + 4 * STATE].astype(bf16)
         raw_ref[v] = out[:, width + 4 * STATE :]
@@ -354,8 +358,20 @@
         ],
         axis=2,
     )
-    mine_weight = lax.all_to_all(sent_weight, "fsdp", split_axis=0, concat_axis=0)
-    mine_weight = mine_weight.reshape(D, width + 5 * STATE)
+    if shards == 4:
+        move = lambda part, r: lax.ppermute(part, "fsdp", [(f, f ^ r) for f in range(shards)])
+        pick = lambda r: lax.dynamic_index_in_dim(sent_weight, place ^ r, 0, False)
+        split = width + 4 * STATE
+        far = move(pick(2), 2)
+        third = pick(3)
+        relayed = move(jnp.concatenate([third[:, :width], third[:, split:]], axis=1), 2)
+        near = move(pick(1), 1)
+        relayed = jnp.concatenate(
+            [relayed[:, :width], far[:, width:split], relayed[:, width:]], axis=1
+        )
+        mine_weight = jnp.stack([pick(0), near, far, move(relayed, 1)])
+    else:
+        mine_weight = lax.all_to_all(sent_weight, "fsdp", split_axis=0, concat_axis=0)
     scales = view_scales(op_ids, mix_codes, aug_gains)
     tile = min(row_count, 128)
     per = row_count // tile
@@ -369,7 +385,7 @@
             num_scalar_prefetch=1,
             grid=(shards, per),
             in_specs=[pl.BlockSpec((tile, D), placed), constant(VIEWS, D),
-                      constant(D, width + 5 * STATE)],
+                      constant(shards, depth, width + 5 * STATE)],
             out_specs=[piece(width), piece(4 * STATE), piece(LANES)],
         ),
         out_shape=[

time: 246 us -> 249 us (1.012)
  waiting for transfers between devices: 67 us -> 69.9 us
    ppermute x0 -> x4, waiting for transfers between devices: none -> 21.5 us  [on_device(): lax.ppermute(part, 'fsdp', [(f, f ^ r) for f in range(shards)])]
    all_to_all x1 -> x0, waiting for transfers between devices: 14.4 us -> none  [on_device(): lax.all_to_all(sent_weight, 'fsdp', split_axis=0, concat_axis=0)]
    ppermute x1, waiting for transfers between devices: 3.71 us -> 0.01 us  [on_device(): across = lax.ppermute(patches, 'fsdp', [(f, f ^ 2) for f in range(shards)])]
    all_to_all x1 -> x0, starting transfers between devices: 3.58 us -> none  [on_device(): lax.all_to_all(sent_weight, 'fsdp', split_axis=0, concat_axis=0)]
  transfers between devices with their start and end apart: 14 -> 17, of which waited for: 6 -> 6; matrix products, arithmetic and copies ran while one was open for 8% -> 7% of each run, Pallas kernels for 16% -> 16%
where the time goes in v5:
time: 249 us; the launch traced here: 247 us
  Pallas kernels  70.8 us (28%)
  waiting for transfers between devices  69.9 us (28%)
  starting transfers between devices  37.8 us (15%)
  local copies, waits for them, and re-layouts  25.9 us (10%)
  blocking collectives  17.7 us (7%)
  between operations  14.5 us (6%)
  other arithmetic  10.5 us (4%)
    all_to_all x2, waiting for transfers between devices, scatter_sum(): lax.all_to_all(blocks, axes, split_axis=0, concat_axis=0)  24.9 us
    pallas_call x3, Pallas kernels, on_device(): call(functools.partial(inside_kernel, heads), 'inside', rows * D * 8192,...  23.3 us
    ppermute x4, waiting for transfers between devices, on_device(): lax.ppermute(part, 'fsdp', [(f, f ^ r) for f in range(shards)])  21.5 us
    ppermute x6, starting transfers between devices, carried_in(): got = lax.ppermute(sent, axis, hops)  17.6 us
    unnamed x50, local copies, waits for them, and re-layouts  17.1 us
    pallas_call x1, Pallas kernels, on_device(): call(functools.partial(states_kernel, heads), 'states', VIEWS * rows * ST...  16.8 us
    all_to_all x1, waiting for transfers between devices, on_device(): arrived = lax.all_to_all(outgoing, 'fsdp', split_axis=0, concat_axis=0)  15.9 us
    all_gather x1, blocking collectives, on_device(): grads_all = lax.all_gather(grads, 'fsdp')  12.5 us
  transfers between devices with their start and end apart: 17, of which 6 were waited for; matrix products, arithmetic and copies ran while one was open for 7% of the time, Pallas kernels for 16%

profile of v5, /device:TPU:0, one launch (start us, length us, event | category | flops | bytes accessed | tf_op | source)
XLA Modules:
  0.0 247.2 jit_solution(11528267483166820811)
XLA Ops:
  7.2 3.0 %collective-permute-start.1 = (bf16[256,1024]{1,0:T(8,128)(2,1)}, bf16[256,1024]{1,0:T(8,128)(2,1)S(1)}, u32[]{:S(2)}, u32[]{:S(2)}) collective-permute-start(bf16[256,1024]{1,0:T(8,128)(2,1)} %patches_ref.1), channel_id=1, source_target_pairs={{0,2},{1,3},{2,0},{3,1},{4,6},{5,7},{6,4},{7,5},{8,10},{9,11},{10,... | collective-permute-start | bytes 1572872 | tf_op jit(solution)/shard_map/ppermute | solution.py:339
  10.2 0.8 reshape.62
  11.0 0.2 copy.45
  11.2 0.2 copy.55
  11.5 0.2 copy.46
  11.9 0.4 maximum_maximum_fusion
  12.5 0.2 collective-permute-start.5
  12.7 1.9 collective-permute-start.4
  15.1 12.3 %collective-permute-done.5 = bf16[256,384]{1,0:T(8,128)(2,1)S(1)} collective-permute-done((bf16[256,384]{1,0:T(8,128)(2,1)S(1)}, bf16[256,384]{1,0:T(8,128)(2,1)S(1)}, u32[]{:S(2)}, u32[]{:S(2)}) %collective-permute-start.5) | collective-permute-done | bytes 196640 | tf_op jit(solution)/shard_map/ppermute | solution.py:362
  27.4 9.0 %collective-permute-done.4 = bf16[256,896]{1,0:T(8,128)(2,1)S(1)} collective-permute-done((bf16[256,896]{1,0:T(8,128)(2,1)S(1)}, bf16[256,896]{1,0:T(8,128)(2,1)S(1)}, u32[]{:S(2)}, u32[]{:S(2)}) %collective-permute-start.4) | collective-permute-done | bytes 458784 | tf_op jit(solution)/shard_map/ppermute | solution.py:362
  36.4 0.8 pad_maximum_fusion.2
  37.3 0.2 fusion.2
  37.7 0.2 dynamic-slice_reduce_fusion.3
  38.2 0.5 collective-permute-start.2
  38.8 0.2 fusion
  38.9 0.2 dynamic-slice_reduce_fusion
  39.2 0.2 collective-permute-done.6
  39.4 1.4 pad_maximum_fusion.1.weight_ref
  40.9 1.5 pad_maximum_fusion.patches_ref
  42.4 10.3 %project.1 = (bf16[3,1024,256]{2,1,0:T(8,128)(2,1)S(1)}, bf16[3,1024,512]{2,1,0:T(8,128)(2,1)}, f32[3,1024,128]{2,1,0:T(8,128)S(1)}) custom-call(s32[1]{0:T(128)} %bitcast.place_ref, bf16[1024,1024]{1,0:T(8,128)(2,1)} %pad_maximum_fusion.patches_ref, f32[3,1024]{1,0:T(4,128)S(1)} %concatenate.16.scale_ref, bf16[4,256,896]{2,1,0:T(8,128)(2,1)S(1)} %pad_maximum_fusion.1.weight_ref), custom_call_target="tpu_custom_call" | custom-call | flops 5637144576 | bytes 8388608 | tf_op jit(solution)/shard_map/project/pallas_call | solution.py:381
  52.7 1.1 copy-done.3
  53.8 1.2 copy-done.5
  55.0 16.8 %states.1 = (f32[3,2,136,256]{3,2,1,0:T(8,128)S(1)}, bf16[3,2,8,256,256]{4,3,2,1,0:T(8,128)(2,1)}, f32[3,1024,128]{2,1,0:T(8,128)S(1)}, f32[3,1024,128]{2,1,0:T(8,128)S(1)}, f32[3,1024,128]{2,1,0:T(8,128)S(1)}) custom-call(f32[3,1024,128]{2,1,0:T(8,128)} %copy-done.5, bf16[3,1024,256]{2,1,0:T(8,128)(2,1)} %copy-done.3, ...), custom_call_target="tpu_custom_call" | custom-call | flops 805306368 | bytes 25165824 | tf_op jit(solution)/shard_map/states/pallas_call | solution.py:413
  71.8 1.2 copy-done.10
  73.0 1.2 copy-done.12
  74.1 0.8 slice_bitcast_fusion
  75.0 1.3 collective-permute-start.10
  76.3 4.6 %collective-permute-start.7 = (f32[3,128,256]{2,1,0:T(8,128)S(1)}, f32[3,128,256]{2,1,0:T(8,128)S(1)}, u32[]{:S(2)}, u32[]{:S(2)}) collective-permute-start(f32[3,128,256]{2,1,0:T(8,128)S(1)} %get-tuple-element.42), channel_id=1, source_target_pairs={{0,4},{4,8},{8,12},{1,5},{5,9},{9,13},{2,6},{6,10},{10,14},{3,7},{... | collective-permute-start | bytes 1179656 | tf_op jit(solution)/shard_map/ppermute | solution.py:302
  80.9 7.5 %collective-permute-done.10 = f32[3,128,256]{2,1,0:T(8,128)} collective-permute-done((f32[3,128,256]{2,1,0:T(8,128)}, f32[3,128,256]{2,1,0:T(8,128)}, u32[]{:S(2)}, u32[]{:S(2)}) %collective-permute-start.10) | collective-permute-done | bytes 393248 | tf_op jit(solution)/shard_map/ppermute | solution.py:302
  88.4 1.1 multiply_add_fusion.1
  89.5 1.3 collective-permute-start.11
  90.8 1.4 copy-done.4
  92.2 1.4 copy-done.11
  93.6 1.4 copy-done.13
  95.0 7.8 %inside.3.rest_0_ = f32[3,1024,256]{2,1,0:T(8,128)} custom-call(bf16[3,1024,256]{2,1,0:T(8,128)(2,1)S(1)} %copy-done.4, bf16[3,1024,512]{2,1,0:T(8,128)(2,1)} %get-tuple-element.21.coef_ref, bf16[3,2,8,256,256]{4,3,2,1,0:T(8,128)(2,1)} %get-tuple-element.24.prefix_ref, f32[3,1024,128]{2,1,0:T(8,128)S(1)} %copy-done.11, f32[3,1024,128]{2,1,0:T(8,128)S(1)} %copy-done.13, ...), custom_call_target="tpu_custom_call" | custom-call | flops 8589934592 | bytes 8388608 | tf_op jit(solution)/shard_map/inside/pallas_call | solution.py:438
  102.9 4.6 %collective-permute-start.8 = (f32[3,128,256]{2,1,0:T(8,128)S(1)}, f32[3,128,256]{2,1,0:T(8,128)S(1)}, u32[]{:S(2)}, u32[]{:S(2)}) collective-permute-start(f32[3,128,256]{2,1,0:T(8,128)S(1)} %get-tuple-element.40), channel_id=1, source_target_pairs={{0,4},{4,8},{8,12},{1,5},{5,9},{9,13},{2,6},{6,10},{10,14},{3,7},{... | collective-permute-start | bytes 1179656 | tf_op jit(solution)/shard_map/ppermute | solution.py:302
  107.5 7.8 %inside.4.rest_0_ = f32[3,1024,256]{2,1,0:T(8,128)} custom-call(bf16[3,1024,256]{2,1,0:T(8,128)(2,1)S(1)} %copy-done.4, bf16[3,1024,512]{2,1,0:T(8,128)(2,1)} %get-tuple-element.21.coef_ref, bf16[3,2,8,256,256]{4,3,2,1,0:T(8,128)(2,1)} %get-tuple-element.24.prefix_ref, f32[3,1024,128]{2,1,0:T(8,128)S(1)} %copy-done.11, ...), custom_call_target="tpu_custom_call", output_to_operand_aliasing={{}: (6, {})} | custom-call | flops 8589934592 | bytes 8388608 | tf_op jit(solution)/shard_map/inside/pallas_call | solution.py:438
  115.2 1.3 collective-permute-start.12
  116.6 4.6 %collective-permute-start.9 = (f32[3,128,256]{2,1,0:T(8,128)S(1)}, f32[3,128,256]{2,1,0:T(8,128)S(1)}, u32[]{:S(2)}, u32[]{:S(2)}) collective-permute-start(f32[3,128,256]{2,1,0:T(8,128)S(1)} %multiply_add_fusion.2), channel_id=1, source_target_pairs={{0,4},{4,8},{8,12},{1,5},{5,9},{9,13},{2,6},{6,10},{10,14},{3,7},{... | collective-permute-start | bytes 1179656 | tf_op jit(solution)/shard_map/ppermute | solution.py:302
  121.2 7.8 %inside.5.local_ref = f32[3,1024,256]{2,1,0:T(8,128)} custom-call(bf16[3,1024,256]{2,1,0:T(8,128)(2,1)S(1)} %copy-done.4, bf16[3,1024,512]{2,1,0:T(8,128)(2,1)} %get-tuple-element.21.coef_ref, bf16[3,2,8,256,256]{4,3,2,1,0:T(8,128)(2,1)} %get-tuple-element.24.prefix_ref, f32[3,1024,128]{2,1,0:T(8,128)S(1)} %copy-done.11, ...), custom_call_target="tpu_custom_call", output_to_operand_aliasing={{}: (6, {})} | custom-call | flops 8589934592 | bytes 8388608 | tf_op jit(solution)/shard_map/inside/pallas_call | solution.py:438
  129.0 7.6 %incoming.1 = (f32[3,1024,256]{2,1,0:T(8,128)S(1)}, f32[3,8,1024]{2,1,0:T(8,128)S(1)}) custom-call(f32[3,128,256]{2,1,0:T(8,128)S(1)} %collective-permute-done.9.forward_ref, f32[3,128,256]{2,1,0:T(8,128)S(1)} %collective-permute-done.12.reverse_ref, bf16[3,1024,512]{2,1,0:T(8,128)(2,1)} %get-tuple-element.21.coef_ref, ...), custom_call_target="tpu_custom_call" | custom-call | flops 805306368 | bytes 25165824 | tf_op jit(solution)/shard_map/incoming/pallas_call | solution.py:455
  136.6 1.7 copy-done.1
  138.3 5.2 %all-gather = f32[12,1,1024]{2,1,0:T(1,128)S(1)} all-gather(f32[3,1,1024]{2,1,0:T(1,128)S(1)} %slice.60), channel_id=2, replica_groups=mesh['groups'=2,'ctx'=4,'fsdp'=4] {'fsdp'}, dimensions={0}, use_global_device_ids=true | all-gather | bytes 61440 | tf_op jit(solution)/shard_map/all_gather | solution.py:470
  143.7 2.4 multiply_convert_fusion.normed_ref
  146.1 1.2 copy.67
  147.3 3.9 %all-to-all-start = ((bf16[4,3,256,256]{3,2,1,0:T(8,128)(2,1)}), bf16[4,3,256,256]{3,2,1,0:T(8,128)(2,1)S(1)}, u32[]{:S(2)}, u32[]{:S(2)}) async-start(bf16[4,3,256,256]{3,2,1,0:T(8,128)(2,1)} %bitcast.57), calls=%async_computation | async-start | bytes 3145728 | tf_op jit(solution)/shard_map/all_to_all | solution.py:474
  151.2 0.8 copy.51.label_ref
  152.0 3.2 %copy.50 = bf16[4,4,64,1024]{3,2,0,1:T(8,128)(2,1)} copy(bf16[4,4,64,1024]{3,2,1,0:T(8,128)(2,1)} %bitcast.58) | data formatting | bytes 4194304 | tf_op jit(solution)/shard_map/reshape | solution.py:476
  155.2 15.9 %all-to-all-done.normed_ref = bf16[4,3,256,256]{3,2,1,0:T(8,128)(2,1)S(1)} async-done(((bf16[4,3,256,256]{3,2,1,0:T(8,128)(2,1)}), bf16[4,3,256,256]{3,2,1,0:T(8,128)(2,1)S(1)}, u32[]{:S(2)}, u32[]{:S(2)}) %all-to-all-start) | async-done | bytes 1572896 | tf_op jit(solution)/shard_map/all_to_all | solution.py:474
  171.1 1.6 copy-done.2
  172.7 1.0 copy-done.8
  173.7 0.9 copy-done.9
  174.6 0.9 copy-done.14
  175.6 4.5 %tail.1 = (bf16[3,256,128]{2,1,0:T(8,128)(2,1)S(1)}, f32[256,1]{1,0:T(8,128)S(1)}, f32[1024,128]{1,0:T(8,128)S(1)}) custom-call(bf16[4,3,256,256]{3,2,1,0:T(8,128)(2,1)S(1)} %all-to-all-done.normed_ref, bf16[4,256,1024]{2,1,0:T(8,128)(2,1)S(1)} %bitcast.54, bf16[1024,128]{1,0:T(8,128)(2,1)S(1)} %copy-done.14, bf16[256,1024]{1,0:T(8,128)(2,1)S(1)} %copy-done.8, ...), custom_call_target="tpu_custom_call" | custom-call | flops 2359296000 | bytes 6291456 | tf_op jit(solution)/shard_map/tail/pallas_call | solution.py:479
  180.1 0.8 copy-done.6
  180.9 5.2 %all-to-all-start.2 = ((f32[16,64,128]{2,1,0:T(8,128)}), f32[16,64,128]{2,1,0:T(8,128)S(1)}, u32[]{:S(2)}, u32[]{:S(2)}) async-start(f32[16,64,128]{2,1,0:T(8,128)} %bitcast.56), calls=%async_computation.2 | async-start | bytes 1048576 | tf_op jit(solution)/shard_map/all_to_all | solution.py:309
  186.1 12.5 %all-gather.1 = bf16[12,256,128]{2,1,0:T(8,128)(2,1)S(1)} all-gather(bf16[3,256,128]{2,1,0:T(8,128)(2,1)S(1)} %get-tuple-element.30), channel_id=3, replica_groups=mesh['groups'=2,'ctx'=4,'fsdp'=4] {'fsdp'}, dimensions={0}, use_global_device_ids=true | all-gather | bytes 983040 | tf_op jit(solution)/shard_map/all_gather | solution.py:501
  198.6 0.9 copy-done.15
  199.6 8.2 %grads.1 = f32[256,1024]{1,0:T(8,128)} custom-call(bf16[3,1024,256]{2,1,0:T(8,128)(2,1)S(1)} %multiply_convert_fusion.normed_ref, bf16[4,3,256,128]{3,2,1,0:T(8,128)(2,1)S(1)} %bitcast.55, bf16[1024,128]{1,0:T(8,128)(2,1)S(1)} %copy-done.15), custom_call_target="tpu_custom_call" | custom-call | flops 2415919104 | bytes 8388608 | tf_op jit(solution)/shard_map/grads/pallas_call | solution.py:502
  207.8 5.5 %all-to-all-start.1 = ((f32[4,64,1024]{2,1,0:T(8,128)}), f32[4,64,1024]{2,1,0:T(8,128)S(1)}, u32[]{:S(2)}, u32[]{:S(2)}) async-start(f32[4,64,1024]{2,1,0:T(8,128)} %bitcast.22), calls=%async_computation.1 | async-start | bytes 2097152 | tf_op jit(solution)/shard_map/all_to_all | solution.py:309
  213.4 0.7 reduce.7
  214.0 0.6 reduce_sum.49
  214.7 24.9 %all-to-all-done.1 = f32[4,64,1024]{2,1,0:T(8,128)S(1)} async-done(((f32[4,64,1024]{2,1,0:T(8,128)}), f32[4,64,1024]{2,1,0:T(8,128)S(1)}, u32[]{:S(2)}, u32[]{:S(2)}) %all-to-all-start.1) | async-done | bytes 1048608 | tf_op jit(solution)/shard_map/all_to_all | solution.py:309
  239.6 0.8 reduce_sum.48
  (92 shorter events, 2.0 us)
Async XLA Ops:
  7.2 31.6 %copy-start = (f32[9,1024]{1,0:T(8,128)S(1)}, f32[9,1024]{1,0:T(8,128)}, u32[]{:S(2)}) copy-start(f32[9,1024]{1,0:T(8,128)} %param.17) | copy-start | bytes 110596
  7.2 4.0 %slice-start.1 = ((bf16[256,1536]{1,0:T(8,128)(2,1)}), bf16[256,1024]{1,0:T(8,128)(2,1)S(1)}, s32[]{:S(2)}) async-start(bf16[256,1536]{1,0:T(8,128)(2,1)} %param.18), calls=%async_computation.5 | async-start | bytes 1048576 | tf_op jit(solution)/shard_map/slice | solution.py:351
  7.2 144.8 %all-gather.4.cloned.1.call-start = ((), (), s32[]{:S(2)}) async-start(), calls=%async_computation.3 | async-start | bytes 2621440 | tf_op jit(solution)/shard_map/all_gather | solution.py:398
  7.2 31.0 %collective-permute-start.1 = (bf16[256,1024]{1,0:T(8,128)(2,1)}, bf16[256,1024]{1,0:T(8,128)(2,1)S(1)}, u32[]{:S(2)}, u32[]{:S(2)}) collective-permute-start(bf16[256,1024]{1,0:T(8,128)(2,1)} %patches_ref.1), channel_id=1, source_target_pairs={{0,2},{1,3},{2,0},{3,1},{4,6},{5,7},{6,4},{7,5},{8,10},{9,11},{10,... | collective-permute-start | bytes 1572872 | tf_op jit(solution)/shard_map/ppermute | solution.py:339
  10.2 30.6 %collective-permute-start = (bf16[256,1024]{1,0:T(8,128)(2,1)}, bf16[256,1024]{1,0:T(8,128)(2,1)S(1)}, u32[]{:S(2)}, u32[]{:S(2)}) collective-permute-start(bf16[256,1024]{1,0:T(8,128)(2,1)} %patches_ref.1), channel_id=1, source_target_pairs={{0,1},{1,0},{2,3},{3,2},{4,5},{5,4},{6,7},{7,6},{8,9},{9,8},{10,11... | collective-permute-start | bytes 1572872 | tf_op jit(solution)/shard_map/ppermute | solution.py:340
  10.2 1.5 slice-start
  12.2 2.4 copy-start.20
  12.2 2.7 %copy-start.18 = (s32[2,3]{1,0:T(2,128)S(1)}, s32[2,3]{1,0:T(2,128)}, u32[]{:S(2)}) copy-start(s32[2,3]{1,0:T(2,128)} %param.15) | copy-start | bytes 76
  12.2 2.9 %copy-start.21 = (f32[2,16]{1,0:T(2,128)S(1)}, f32[2,16]{1,0:T(2,128)}, u32[]{:S(2)}) copy-start(f32[2,16]{1,0:T(2,128)} %param.21) | copy-start | bytes 388
  12.4 25.1 %copy-start.19 = (f32[2,16]{1,0:T(2,128)S(1)}, f32[2,16]{1,0:T(2,128)}, u32[]{:S(2)}) copy-start(f32[2,16]{1,0:T(2,128)} %param.20) | copy-start | bytes 388
  12.4 25.2 %copy-start.22 = (f32[16]{0:T(128)S(1)}, f32[16]{0:T(128)}, u32[]{:S(2)}) copy-start(f32[16]{0:T(128)} %param.22) | copy-start | bytes 196
  12.4 25.6 %copy-start.16 = (f32[1024]{0:T(1024)S(1)}, f32[1024]{0:T(1024)}, u32[]{:S(2)}) copy-start(f32[1024]{0:T(1024)} %param.23) | copy-start | bytes 12292
  12.5 14.9 %collective-permute-start.5 = (bf16[256,384]{1,0:T(8,128)(2,1)S(1)}, bf16[256,384]{1,0:T(8,128)(2,1)S(1)}, u32[]{:S(2)}, u32[]{:S(2)}) collective-permute-start(bf16[256,384]{1,0:T(8,128)(2,1)S(1)} %pad_maximum_fusion.3), channel_id=1, source_target_pairs={{0,2},{1,3},{2,0},{3,1},{4,6},{5,7},{6,4},{7,5},{8,10},{9,11},{10,... | collective-permute-start | bytes 589832 | tf_op jit(solution)/shard_map/ppermute | solution.py:362
  12.7 23.7 %collective-permute-start.4 = (bf16[256,896]{1,0:T(8,128)(2,1)S(1)}, bf16[256,896]{1,0:T(8,128)(2,1)S(1)}, u32[]{:S(2)}, u32[]{:S(2)}) collective-permute-start(bf16[256,896]{1,0:T(8,128)(2,1)S(1)} %get-tuple-element.37), channel_id=1, source_target_pairs={{0,2},{1,3},{2,0},{3,1},{4,6},{5,7},{6,4},{7,5},{8,10},{9,11},{10,... | collective-permute-start | bytes 1376264 | tf_op jit(solution)/shard_map/ppermute | solution.py:362
  14.6 24.6 %collective-permute-start.3 = (bf16[256,896]{1,0:T(8,128)(2,1)S(1)}, bf16[256,896]{1,0:T(8,128)(2,1)}, u32[]{:S(2)}, u32[]{:S(2)}) collective-permute-start(bf16[256,896]{1,0:T(8,128)(2,1)S(1)} %get-tuple-element.38), channel_id=1, source_target_pairs={{0,1},{1,0},{2,3},{3,2},{4,5},{5,4},{6,7},{7,6},{8,9},{9,8},{10,11... | collective-permute-start | bytes 1376264 | tf_op jit(solution)/shard_map/ppermute | solution.py:362
  37.3 3.6 %copy-start.7 = (bf16[256,1024]{1,0:T(8,128)(2,1)S(1)}, bf16[256,1024]{1,0:T(8,128)(2,1)}, u32[]{:S(2)}) copy-start(bf16[256,1024]{1,0:T(8,128)(2,1)} %patches_ref.1) | copy-start | bytes 1572868
  37.3 2.2 collective-permute-start.6
  38.2 2.6 %collective-permute-start.2 = (bf16[256,1024]{1,0:T(8,128)(2,1)S(1)}, bf16[256,1024]{1,0:T(8,128)(2,1)S(1)}, u32[]{:S(2)}, u32[]{:S(2)}) collective-permute-start(bf16[256,1024]{1,0:T(8,128)(2,1)S(1)} %collective-permute-done.1), channel_id=1, source_target_pairs={{0,1},{1,0},{2,3},{3,2},{4,5},{5,4},{6,7},{7,6},{8,9},{9,8},{10,11... | collective-permute-start | bytes 1572872 | tf_op jit(solution)/shard_map/ppermute | solution.py:341
  52.7 1.1 copy-start.3
  53.8 1.2 copy-start.5
  71.8 1.2 copy-start.10
  73.0 1.2 copy-start.12
  75.0 13.4 %collective-permute-start.10 = (f32[3,128,256]{2,1,0:T(8,128)}, f32[3,128,256]{2,1,0:T(8,128)}, u32[]{:S(2)}, u32[]{:S(2)}) collective-permute-start(f32[3,128,256]{2,1,0:T(8,128)} %get-tuple-element.41), channel_id=1, source_target_pairs={{4,0},{8,4},{12,8},{5,1},{9,5},{13,9},{6,2},{10,6},{14,10},{7,3},{... | collective-permute-start | bytes 1179656 | tf_op jit(solution)/shard_map/ppermute | solution.py:302
  76.3 26.5 %collective-permute-start.7 = (f32[3,128,256]{2,1,0:T(8,128)S(1)}, f32[3,128,256]{2,1,0:T(8,128)S(1)}, u32[]{:S(2)}, u32[]{:S(2)}) collective-permute-start(f32[3,128,256]{2,1,0:T(8,128)S(1)} %get-tuple-element.42), channel_id=1, source_target_pairs={{0,4},{4,8},{8,12},{1,5},{5,9},{9,13},{2,6},{6,10},{10,14},{3,7},{... | collective-permute-start | bytes 1179656 | tf_op jit(solution)/shard_map/ppermute | solution.py:302
  89.5 13.3 %collective-permute-start.11 = (f32[3,128,256]{2,1,0:T(8,128)S(1)}, f32[3,128,256]{2,1,0:T(8,128)S(1)}, u32[]{:S(2)}, u32[]{:S(2)}) collective-permute-start(f32[3,128,256]{2,1,0:T(8,128)S(1)} %multiply_add_fusion.1), channel_id=1, source_target_pairs={{4,0},{8,4},{12,8},{5,1},{9,5},{13,9},{6,2},{10,6},{14,10},{7,3},{... | collective-permute-start | bytes 1179656 | tf_op jit(solution)/shard_map/ppermute | solution.py:302
  90.8 1.4 copy-start.4
  92.2 1.4 copy-start.11
  93.6 1.4 copy-start.13
  102.9 13.6 %collective-permute-start.8 = (f32[3,128,256]{2,1,0:T(8,128)S(1)}, f32[3,128,256]{2,1,0:T(8,128)S(1)}, u32[]{:S(2)}, u32[]{:S(2)}) collective-permute-start(f32[3,128,256]{2,1,0:T(8,128)S(1)} %get-tuple-element.40), channel_id=1, source_target_pairs={{0,4},{4,8},{8,12},{1,5},{5,9},{9,13},{2,6},{6,10},{10,14},{3,7},{... | collective-permute-start | bytes 1179656 | tf_op jit(solution)/shard_map/ppermute | solution.py:302
  115.2 13.7 %collective-permute-start.12 = (f32[3,128,256]{2,1,0:T(8,128)S(1)}, f32[3,128,256]{2,1,0:T(8,128)S(1)}, u32[]{:S(2)}, u32[]{:S(2)}) collective-permute-start(f32[3,128,256]{2,1,0:T(8,128)S(1)} %get-tuple-element.39), channel_id=1, source_target_pairs={{4,0},{8,4},{12,8},{5,1},{9,5},{13,9},{6,2},{10,6},{14,10},{7,3},{... | collective-permute-start | bytes 1179656 | tf_op jit(solution)/shard_map/ppermute | solution.py:302
  116.6 12.4 %collective-permute-start.9 = (f32[3,128,256]{2,1,0:T(8,128)S(1)}, f32[3,128,256]{2,1,0:T(8,128)S(1)}, u32[]{:S(2)}, u32[]{:S(2)}) collective-permute-start(f32[3,128,256]{2,1,0:T(8,128)S(1)} %multiply_add_fusion.2), channel_id=1, source_target_pairs={{0,4},{4,8},{8,12},{1,5},{5,9},{9,13},{2,6},{6,10},{10,14},{3,7},{... | collective-permute-start | bytes 1179656 | tf_op jit(solution)/shard_map/ppermute | solution.py:302
  136.6 1.7 copy-start.1
  147.3 3.9 %copy-start.17 = (s32[256]{0:T(256)S(1)}, s32[256]{0:T(256)}, u32[]{:S(2)}) copy-start(s32[256]{0:T(256)} %param.14) | copy-start | bytes 3076
  147.3 23.7 %all-to-all-start = ((bf16[4,3,256,256]{3,2,1,0:T(8,128)(2,1)}), bf16[4,3,256,256]{3,2,1,0:T(8,128)(2,1)S(1)}, u32[]{:S(2)}, u32[]{:S(2)}) async-start(bf16[4,3,256,256]{3,2,1,0:T(8,128)(2,1)} %bitcast.57), calls=%async_computation | async-start | bytes 3145728 | tf_op jit(solution)/shard_map/all_to_all | solution.py:474
  171.1 1.6 copy-start.2
  172.7 1.0 copy-start.8
  173.7 0.9 copy-start.9
  174.6 0.9 copy-start.14
  180.1 0.8 copy-start.6
  180.9 26.9 %all-to-all-start.2 = ((f32[16,64,128]{2,1,0:T(8,128)}), f32[16,64,128]{2,1,0:T(8,128)S(1)}, u32[]{:S(2)}, u32[]{:S(2)}) async-start(f32[16,64,128]{2,1,0:T(8,128)} %bitcast.56), calls=%async_computation.2 | async-start | bytes 1048576 | tf_op jit(solution)/shard_map/all_to_all | solution.py:309
  198.6 0.9 copy-start.15
  207.8 31.8 %all-to-all-start.1 = ((f32[4,64,1024]{2,1,0:T(8,128)}), f32[4,64,1024]{2,1,0:T(8,128)S(1)}, u32[]{:S(2)}, u32[]{:S(2)}) async-start(f32[4,64,1024]{2,1,0:T(8,128)} %bitcast.22), calls=%async_computation.1 | async-start | bytes 2097152 | tf_op jit(solution)/shard_map/all_to_all | solution.py:309
Sparse Core Ops, SparseCore 0:
  81.0 23.7 all-gather.3
